TPU v7x, 32 devices: a whole 2x2x4 slice. The times are simulated.
32 devices in a mesh: gx: 16 (over z, y, core), gy: 2 (over x).
Axes of the slice: x: 2, y: 2, z: 4, core: 2. Of those that a mesh axis runs over, the one named last changes fastest.
Arguments:
- cell_bin: int32 [524288], P(('gx', 'gy')), may hold values from 0 to 8191
- cell_layer: int32 [524288], P(('gx', 'gy')), may hold values from 0 to 7
- cell_offset: int32 [524288], P(('gx', 'gy')), may hold values from 0 to 8, as said below
- cell_power: float32 [524288], P(('gx', 'gy')), may hold values from 1 to 10
- spill_weight: float32 [524288], P(('gx', 'gy')), may hold values from 0.05 to 0.5
- conductivity: float32 [8, 512, 512], P(None, 'gx', 'gy'), may hold values from 0.5 to 2
- layer_coupling: float32 [7], replicated, may hold values from 0.5 to 2
Outputs:
- final_warmth: float32 [8, 512, 512], P(None, 'gx', 'gy')
- warmth_driven_pull: float32 [2, 524288], P(None, ('gx', 'gy'))
Inputs may be any that keep to these rules, and one draw needn't show every extreme that they name: `cell_offset`: an offset never points outside the grid of tiles; among the cells held by one tile at most 2048 have any one offset other than 4, and in every draw each tile has some offset held by exactly 2048 of its cells, and some tile receives exactly 2048 cells from each of its neighbouring tiles.
All inputs are finite; a program needn't handle non-finite values.
Results may differ from a plain program's by a relative error of at most 0.00002.
Values sent between devices are 32-bit elements; how exact they have to be, the bound alone decides.
No kernel may reach another device: no remote copies, remote signals or barrier semaphores. Data moves between devices by JAX's collectives and lax.ppermute only.
A program may use at most 64 MiB of HBM per device.

v0:
```python
import jax
import jax.numpy as jnp
from jax import lax
from jax.sharding import PartitionSpec as P

ITERS = 4
CAP = 2048


SINK_RATE = 0.5
LOW_BOUND = 0.5
HIGH_BOUND = 33.0


def padded(block, sides, width):
    for axis, dim in sides:
        count = lax.axis_size(axis)
        forward = [(i, i + 1) for i in range(count - 1)]
        backward = [(target, source) for source, target in forward]
        low = lax.ppermute(
            lax.slice_in_dim(block, block.shape[dim] - width, None, axis=dim), axis, forward
        )
        high = lax.ppermute(lax.slice_in_dim(block, 0, width, axis=dim), axis, backward)
        block = jnp.concatenate([low, block, high], axis=dim)
    return block


def shifted(value, axis, by):
    size = lax.axis_size(axis)
    pairs = [(i, i + by) for i in range(size) if 0 <= i + by < size]
    return lax.ppermute(value, axis, pairs)


def operator_core(padded_values, padded_conduct, coupling):
    vertical_count = padded_values.shape[1] - 2
    horizontal_count = padded_values.shape[2] - 2
    centre_values = padded_values[:, 1 : 1 + vertical_count, 1 : 1 + horizontal_count]
    centre_conduct = padded_conduct[:, 1 : 1 + vertical_count, 1 : 1 + horizontal_count]
    result = SINK_RATE * centre_values
    for column_start, row_start in ((2, 1), (0, 1), (1, 2), (1, 0)):
        beside_values = padded_values[
            :,
            column_start : column_start + vertical_count,
            row_start : row_start + horizontal_count,
        ]
        beside_conduct = padded_conduct[
            :,
            column_start : column_start + vertical_count,
            row_start : row_start + horizontal_count,
        ]
        result = result + 0.5 * (centre_conduct + beside_conduct) * (centre_values - beside_values)
    face_conduct = coupling[:, None, None] * (0.5 * (centre_conduct[:-1] + centre_conduct[1:]))
    vertical_flow = face_conduct * (centre_values[:-1] - centre_values[1:])
    zero_layer = jnp.zeros_like(vertical_flow[:1])
    return (
        result
        + jnp.concatenate([vertical_flow, zero_layer], 0)
        - jnp.concatenate([zero_layer, vertical_flow], 0)
    )


def polynomial_iterative_method(dissipation_map, diffusion_matrix_product, inner_nodes):
    middle_window = 0.5 * (HIGH_BOUND + LOW_BOUND)
    spread = 0.5 * (HIGH_BOUND - LOW_BOUND)
    sigma_value = middle_window / spread
    ratio_now = 1.0 / sigma_value
    final_warmth = dissipation_map / middle_window
    iterate_advance = dissipation_map / middle_window
    for sweep_index in range(ITERS):
        leftover_error_map = (
            dissipation_map - diffusion_matrix_product(final_warmth)
        ) * inner_nodes
        ratio_next = 1.0 / (2.0 * sigma_value - ratio_now)
        iterate_advance = (
            ratio_next * ratio_now * iterate_advance
            + 2.0 * ratio_next / spread * leftover_error_map
        )
        final_warmth = final_warmth + iterate_advance
        ratio_now = ratio_next
    return final_warmth


def slope_couples(bordered_warmth, border_width, vertical_count, horizontal_count):
    horizontal_share = bordered_warmth[:, :, border_width : border_width + horizontal_count]
    vertical_slope = 0.5 * (
        horizontal_share[:, border_width + 1 : border_width + 1 + vertical_count]
        - horizontal_share[:, border_width - 1 : border_width - 1 + vertical_count]
    )
    vertical_share = bordered_warmth[:, border_width : border_width + vertical_count, :]
    horizontal_slope = 0.5 * (
        vertical_share[:, :, border_width + 1 : border_width + 1 + horizontal_count]
        - vertical_share[:, :, border_width - 1 : border_width - 1 + horizontal_count]
    )
    return (vertical_slope, horizontal_slope)


def including_edge_sides(values):
    return padded(values, (("gx", 1), ("gy", 2)), 1)


def send_grouped(record_index, record_amount):
    across = []
    for column_step, first_slot in ((-1, 0), (1, 5)):
        across.append(
            shifted(
                (
                    record_index[first_slot : first_slot + 3],
                    record_amount[:, first_slot : first_slot + 3],
                ),
                "gx",
                column_step,
            )
        )
    along = []
    for row_step, member_pos, own_slot in ((-1, 0, 3), (1, 2, 4)):
        group_index = jnp.stack(
            [across[0][0][member_pos], record_index[own_slot], across[1][0][member_pos]]
        )
        group_amount = jnp.stack(
            [across[0][1][:, member_pos], record_amount[:, own_slot], across[1][1][:, member_pos]],
            axis=1,
        )
        along.append(shifted((group_index, group_amount), "gy", row_step))
    selections = (
        (along, 0, 0),
        (across, 0, 1),
        (along, 1, 0),
        (along, 0, 1),
        (along, 1, 1),
        (along, 0, 2),
        (across, 1, 1),
        (along, 1, 2),
    )
    final_index = jnp.stack(
        [source[group_pos][0][member_pos] for source, group_pos, member_pos in selections]
    )
    final_amount = jnp.stack(
        [source[group_pos][1][:, member_pos] for source, group_pos, member_pos in selections],
        axis=1,
    )
    return (final_index, final_amount)


def return_grouped(reply):
    along = []
    for row_step, slot_group in ((-1, (0, 3, 5)), (1, (2, 4, 7))):
        stacked = jnp.stack([reply[:, slot_item] for slot_item in slot_group], axis=1)
        along.append(shifted(stacked, "gy", -row_step))
    across = []
    for column_step, member_pos, direct_slot in ((-1, 0, 1), (1, 2, 6)):
        stacked = jnp.stack(
            [along[0][:, member_pos], reply[:, direct_slot], along[1][:, member_pos]], axis=1
        )
        across.append(shifted(stacked, "gx", -column_step))
    selections = (
        (across, 0, 0),
        (across, 0, 1),
        (across, 0, 2),
        (along, 0, 1),
        (along, 1, 1),
        (across, 1, 0),
        (across, 1, 1),
        (across, 1, 2),
    )
    return jnp.stack(
        [source[group_pos][:, member_pos] for source, group_pos, member_pos in selections], axis=1
    )


def shards(
    cell_bin, cell_layer, cell_offset, cell_power, spill_weight, conductivity, layer_coupling
):
    layer_count, vertical_count, horizontal_count = conductivity.shape
    plane_cells = vertical_count * horizontal_count
    grid_cells = layer_count * plane_cells
    capacity = CAP
    spill_layer = jnp.where(cell_layer == layer_count - 1, layer_count - 2, cell_layer + 1)
    main_index = cell_layer * plane_cells + cell_bin
    spill_index = spill_layer * plane_cells + cell_bin
    main_power = cell_power * (1.0 - spill_weight)
    spill_power = cell_power * spill_weight
    moving = cell_offset != 4
    direction_slot = cell_offset - (cell_offset > 4).astype(jnp.int32)
    matches = (cell_offset[None, :] == jnp.arange(9, dtype=jnp.int32)[:, None]).astype(jnp.int32)
    rank_within = jnp.sum((jnp.cumsum(matches, axis=1) - 1) * matches, axis=0)
    slot = jnp.where(moving, direction_slot * capacity + rank_within, 8 * capacity)
    send_index = (
        jnp.zeros((8 * capacity + 1,), jnp.int32).at[slot].set(main_index)[:-1].reshape(8, capacity)
    )
    amounts = jnp.stack([main_power, spill_power])
    send_amount = (
        jnp.zeros((2, 8 * capacity + 1), jnp.float32)
        .at[:, slot]
        .set(amounts)[:, :-1]
        .reshape(2, 8, capacity)
    )
    arrived_index, arrived_amount = send_grouped(send_index, send_amount)
    flat_index = arrived_index.reshape(-1)
    arrived_layer = flat_index // plane_cells
    arrived_spill_layer = jnp.where(
        arrived_layer == layer_count - 1, layer_count - 2, arrived_layer + 1
    )
    arrived_spill = arrived_spill_layer * plane_cells + flat_index % plane_cells
    staying = jnp.where(moving, 0.0, 1.0).astype(jnp.float32)
    every_index = jnp.concatenate([main_index, spill_index, flat_index, arrived_spill])
    every_amount = jnp.concatenate(
        [
            main_power * staying,
            spill_power * staying,
            arrived_amount[0].reshape(-1),
            arrived_amount[1].reshape(-1),
        ]
    )
    dissipation_map = jax.ops.segment_sum(
        every_amount, every_index, num_segments=grid_cells
    ).reshape(layer_count, vertical_count, horizontal_count)
    padded_conduct = including_edge_sides(conductivity)

    def block_matrix_product(values):
        return operator_core(including_edge_sides(values), padded_conduct, layer_coupling)

    final_warmth = polynomial_iterative_method(dissipation_map, block_matrix_product, 1.0)
    vertical_slope, horizontal_slope = slope_couples(
        including_edge_sides(final_warmth), 1, vertical_count, horizontal_count
    )
    column_flat = vertical_slope.reshape(-1)
    row_flat = horizontal_slope.reshape(-1)
    reply = jnp.stack([column_flat[arrived_index], row_flat[arrived_index]])
    returned = return_grouped(reply)
    remote_slot = jnp.where(moving, slot, 0)
    value_column = jnp.where(moving, returned[0].reshape(-1)[remote_slot], column_flat[main_index])
    value_row = jnp.where(moving, returned[1].reshape(-1)[remote_slot], row_flat[main_index])
    warmth_driven_pull = jnp.stack([-cell_power * value_column, -cell_power * value_row])
    return (final_warmth, warmth_driven_pull)


def solution(mesh):
    return jax.shard_map(
        shards,
        mesh=mesh,
        in_specs=(
            P(("gx", "gy")),
            P(("gx", "gy")),
            P(("gx", "gy")),
            P(("gx", "gy")),
            P(("gx", "gy")),
            P(None, "gx", "gy"),
            P(),
        ),
        out_specs=(P(None, "gx", "gy"), P(None, ("gx", "gy"))),
        check_vma=False,
    )
```

profile of v0, /device:TPU:0, one launch (start us, length us, event | category | flops | bytes accessed | tf_op | source)
XLA Modules:
  0.0 1189.9 jit_solution(16360832107623076068)
XLA Ops:
  3.5 1.6 select_multiply_fusion.1
  5.1 4.9 copy.23
  10.8 44.5 %scatter_custom_fusion.1 = f32[2,16385]{0,1:T(8,128)} fusion(s32[16384]{0:T(1024)S(1)} %get-tuple-element.99, f32[16384,2]{1,0:T(8,128)} %copy.23, f32[]{:T(128)} %constant.26.clone.1), kind=kCustom, calls=%fused_computation.9 | custom fusion | bytes 131592 | tf_op jit(solution)/shard_map/scatter | solution.py:194
  55.3 3.8 slice.552
  59.1 3.3 copy-done
  62.4 2.1 fusion.106
  64.5 3.3 copy.30
  67.8 3.0 collective-permute-start.5
  70.8 2.1 copy.28
  72.9 1.4 collective-permute-start.4
  74.3 60.5 %scatter_custom_fusion = s32[16385]{0:T(1024)S(1)} fusion(s32[16384]{0:T(1024)} %copy-done.11, s32[16384]{0:T(1024)} %get-tuple-element.3, s32[]{:T(128)} %constant.31.clone.1), kind=kCustom, calls=%fused_computation.201 | custom fusion | bytes 66052 | tf_op jit(solution)/shard_map/scatter | solution.py:188
  134.8 4.6 collective-permute-start.1
  139.4 3.6 collective-permute-start.10
  144.3 1.7 fusion.105
  150.2 4.6 collective-permute-start.14
  158.6 4.5 collective-permute-start.7
  165.6 4.1 collective-permute-done.6
  170.1 379.3 %scatter_custom_fusion.2 = f32[65536]{0:T(1024)S(1)} fusion(s32[65536]{0:T(1024)S(1)} %pad_add_fusion, f32[65536]{0:T(1024)S(1)} %pad_maximum_fusion.54, f32[]{:T(128)} %constant.26.clone.1), kind=kCustom, calls=%fused_computation.170 | custom fusion | flops 65536 | bytes 262148 | tf_op jit(solution)/shard_map/scatter-add | solution.py:214
  552.1 3.8 collective-permute-done.9
  557.4 4.9 collective-permute-start.15
  562.4 1.9 collective-permute-done.13
  564.3 1.8 collective-permute-done.15
  568.0 3.4 collective-permute-start.17
  572.4 1.5 collective-permute-start.18
  573.9 4.6 collective-permute-start.19
  578.5 1.3 collective-permute-done.18
  579.8 1.5 collective-permute-done.19
  583.1 4.4 collective-permute-start.21
  589.8 4.6 collective-permute-start.23
  594.4 1.3 collective-permute-done.22
  595.7 1.5 collective-permute-done.23
  599.1 5.2 collective-permute-start.25
  606.6 4.6 collective-permute-start.27
  611.2 1.3 collective-permute-done.26
  612.5 1.5 collective-permute-done.27
  615.9 4.8 collective-permute-start.29
  622.9 4.6 collective-permute-start.31
  627.5 1.3 collective-permute-done.30
  628.8 1.5 collective-permute-done.31
  630.7 90.5 %gather_fusion.1 = f32[16384]{0:T(1024)S(1)} fusion(f32[65536]{0:T(1024)S(1)} %bitcast.55, s32[16384]{0:T(1024)S(1)} %broadcast_clamp_fusion), kind=kCustom, calls=%fused_computation.1 | custom fusion | bytes 196608 | tf_op jit(solution)/shard_map/gather | solution.py:228
  721.5 90.5 %gather_fusion = f32[16384]{0:T(1024)S(1)} fusion(f32[65536]{0:T(1024)S(1)} %bitcast.57, s32[16384]{0:T(1024)S(1)} %broadcast_clamp_fusion), kind=kCustom, calls=%fused_computation | custom fusion | bytes 196608 | tf_op jit(solution)/shard_map/gather | solution.py:228
  812.2 4.4 collective-permute-start.32
  818.5 4.3 collective-permute-done.33
  822.9 2.4 collective-permute-start.34
  826.7 90.5 %gather_fusion.3 = f32[16384]{0:T(1024)S(1)} fusion(f32[65536]{0:T(1024)S(1)} %bitcast.58, s32[16384]{0:T(1024)S(1)} %get-tuple-element.2), kind=kCustom, calls=%fused_computation.3 | custom fusion | bytes 196608 | tf_op jit(solution)/shard_map/gather | solution.py:231
  917.3 90.5 %gather_fusion.5 = f32[16384]{0:T(1024)S(1)} fusion(f32[65536]{0:T(1024)S(1)} %bitcast.56, s32[16384]{0:T(1024)S(1)} %get-tuple-element.2), kind=kCustom, calls=%fused_computation.5 | custom fusion | bytes 196608 | tf_op jit(solution)/shard_map/gather | solution.py:232
  1008.0 90.5 %gather_fusion.4 = f32[16384]{0:T(1024)S(1)} fusion(f32[16384]{0:T(1024)S(1)} %bitcast.59, s32[16384]{0:T(1024)S(1)} %get-tuple-element.4), kind=kCustom, calls=%fused_computation.4 | custom fusion | bytes 196608 | tf_op jit(solution)/shard_map/gather | solution.py:232
  1098.5 90.5 %gather_fusion.2 = f32[16384]{0:T(1024)S(1)} fusion(f32[16384]{0:T(1024)S(1)} %bitcast.60, s32[16384]{0:T(1024)S(1)} %get-tuple-element.4), kind=kCustom, calls=%fused_computation.2 | custom fusion | bytes 196608 | tf_op jit(solution)/shard_map/gather | solution.py:231
  (160 shorter events, 40.0 us)
Async XLA Ops:
  0.6 9.5 copy-start.3
  0.6 9.5 copy-start.9
  0.7 9.4 copy-start.10
  10.8 48.3 %copy-start.11 = (s32[16384]{0:T(1024)}, s32[16384]{0:T(1024)S(1)}, u32[]{:S(2)}) copy-start(s32[16384]{0:T(1024)S(1)} %get-tuple-element.99) | copy-start | bytes 196612
  59.1 3.3 copy-start
  62.4 76.9 %copy-start.1 = (f32[8,32,256]{2,1,0:T(8,128)S(1)}, f32[8,32,256]{2,1,0:T(8,128)}, u32[]{:S(2)}) copy-start(f32[8,32,256]{2,1,0:T(8,128)} %param.12) | copy-start | bytes 786436
  67.8 88.4 %collective-permute-start.5 = (f32[2,3,2048]{2,1,0:T(4,128)}, f32[2,3,2048]{2,1,0:T(4,128)}, u32[]{:S(2)}, u32[]{:S(2)}) collective-permute-start(f32[2,3,2048]{2,1,0:T(4,128)} %copy.30), channel_id=1, source_target_pairs={{0,2},{2,4},{4,6},{6,8},{8,10},{10,12},{12,14},{14,16},{16,18},{18... | collective-permute-start | bytes 147464 | tf_op jit(solution)/shard_map/ppermute | solution.py:31
  72.8 91.9 %copy-start.7 = (s32[16384]{0:T(1024)S(1)}, s32[16384]{0:T(1024)}, u32[]{:S(2)}) copy-start(s32[16384]{0:T(1024)} %get-tuple-element.3) | copy-start | bytes 196612
  72.8 92.0 %copy-start.8 = (s32[16384]{0:T(1024)S(1)}, s32[16384]{0:T(1024)}, u32[]{:S(2)}) copy-start(s32[16384]{0:T(1024)} %get-tuple-element.62) | copy-start | bytes 196612
  72.8 97.2 %copy-start.5 = (f32[16384]{0:T(1024)S(1)}, f32[16384]{0:T(1024)}, u32[]{:S(2)}) copy-start(f32[16384]{0:T(1024)} %get-tuple-element.14) | copy-start | bytes 196612
  72.8 97.2 %copy-start.6 = (f32[16384]{0:T(1024)S(1)}, f32[16384]{0:T(1024)}, u32[]{:S(2)}) copy-start(f32[16384]{0:T(1024)} %get-tuple-element.48) | copy-start | bytes 196612
  72.9 85.6 %collective-permute-start.4 = (f32[2,3,2048]{2,1,0:T(4,128)}, f32[2,3,2048]{2,1,0:T(4,128)S(1)}, u32[]{:S(2)}, u32[]{:S(2)}) collective-permute-start(f32[2,3,2048]{2,1,0:T(4,128)} %copy.28), channel_id=1, source_target_pairs={{2,0},{4,2},{6,4},{8,6},{10,8},{12,10},{14,12},{16,14},{18,16},{20... | collective-permute-start | bytes 147464 | tf_op jit(solution)/shard_map/ppermute | solution.py:31
  134.8 15.4 %collective-permute-start.1 = (s32[3,2048]{1,0:T(4,128)S(1)}, s32[3,2048]{1,0:T(4,128)S(1)}, u32[]{:S(2)}, u32[]{:S(2)}) collective-permute-start(s32[3,2048]{1,0:T(4,128)S(1)} %slice.415), channel_id=1, source_target_pairs={{0,2},{2,4},{4,6},{6,8},{8,10},{10,12},{12,14},{14,16},{16,18},{18... | collective-permute-start | bytes 73736 | tf_op jit(solution)/shard_map/ppermute | solution.py:31
  139.4 8.0 collective-permute-start.10
  143.0 5.7 collective-permute-start.8
  147.4 7.4 collective-permute-start
  148.9 413.6 %collective-permute-start.12 = (f32[8,34,1]{2,1,0:T(8,128)S(1)}, f32[8,34,1]{2,1,0:T(8,128)S(1)}, u32[]{:S(2)}, u32[]{:S(2)}) collective-permute-start(f32[8,34,1]{2,1,0:T(8,128)S(1)} %get-tuple-element.30), channel_id=1, source_target_pairs={{1,0},{3,2},{5,4},{7,6},{9,8},{11,10},{13,12},{15,14},{17,16},{19,... | collective-permute-start | bytes 3272 | tf_op jit(solution)/shard_map/ppermute | solution.py:23
  150.2 412.3 %collective-permute-start.14 = (f32[8,34,1]{2,1,0:T(8,128)S(1)}, f32[8,34,1]{2,1,0:T(8,128)S(1)}, u32[]{:S(2)}, u32[]{:S(2)}) collective-permute-start(f32[8,34,1]{2,1,0:T(8,128)S(1)} %get-tuple-element.31), channel_id=1, source_target_pairs={{0,1},{2,3},{4,5},{6,7},{8,9},{10,11},{12,13},{14,15},{16,17},{18,... | collective-permute-start | bytes 3272 | tf_op jit(solution)/shard_map/ppermute | solution.py:20
  154.8 8.4 collective-permute-start.3
  156.2 8.4 collective-permute-start.2
  158.6 7.0 collective-permute-start.7
  163.2 6.5 collective-permute-start.6
  549.5 2.6 collective-permute-start.11
  550.8 5.1 collective-permute-start.9
  556.1 8.2 collective-permute-start.13
  557.4 8.7 collective-permute-start.15
  566.7 4.8 collective-permute-start.16
  568.0 4.3 collective-permute-start.17
  572.4 7.4 collective-permute-start.18
  573.9 7.4 collective-permute-start.19
  581.8 5.7 collective-permute-start.20
  583.1 5.2 collective-permute-start.21
  588.5 7.2 collective-permute-start.22
  589.8 7.4 collective-permute-start.23
  597.8 6.6 collective-permute-start.24
  599.1 6.1 collective-permute-start.25
  605.3 7.2 collective-permute-start.26
  606.6 7.4 collective-permute-start.27
  614.5 106.7 %copy-start.2 = (f32[8,32,256]{2,1,0:T(8,128)}, f32[8,32,256]{2,1,0:T(8,128)S(1)}, u32[]{:S(2)}) copy-start(f32[8,32,256]{2,1,0:T(8,128)S(1)} %fusion.17) | copy-start | bytes 786436
  614.6 6.2 collective-permute-start.28
  615.9 5.6 collective-permute-start.29
  621.6 7.2 collective-permute-start.30
  622.9 7.4 collective-permute-start.31
  812.2 6.3 collective-permute-start.32
  816.7 6.2 collective-permute-start.33
  822.9 184.9 %collective-permute-start.34 = (f32[2,3,2048]{2,1,0:T(4,128)S(1)}, f32[2,3,2048]{2,1,0:T(4,128)S(1)}, u32[]{:S(2)}, u32[]{:S(2)}) collective-permute-start(f32[2,3,2048]{2,1,0:T(4,128)S(1)} %pad_maximum_fusion.61), channel_id=1, source_target_pairs={{0,2},{2,4},{4,6},{6,8},{8,10},{10,12},{12,14},{14,16},{16,18},{18... | collective-permute-start | bytes 147464 | tf_op jit(solution)/shard_map/ppermute | solution.py:31
  825.4 182.4 %collective-permute-start.35 = (f32[2,3,2048]{2,1,0:T(4,128)S(1)}, f32[2,3,2048]{2,1,0:T(4,128)S(1)}, u32[]{:S(2)}, u32[]{:S(2)}) collective-permute-start(f32[2,3,2048]{2,1,0:T(4,128)S(1)} %pad_maximum_fusion.62), channel_id=1, source_target_pairs={{2,0},{4,2},{6,4},{8,6},{10,8},{12,10},{14,12},{16,14},{18,16},{20... | collective-permute-start | bytes 147464 | tf_op jit(solution)/shard_map/ppermute | solution.py:31
  1098.5 90.6 %copy-start.4 = (f32[16384]{0:T(1024)S(1)}, f32[16384]{0:T(1024)}, u32[]{:S(2)}) copy-start(f32[16384]{0:T(1024)} %param.10) | copy-start | bytes 196612
where the time goes:
time: 1210 us; the launch traced here: 1190 us
  local copies, waits for them, and re-layouts  674 us (56%)
  other arithmetic  388 us (32%)
  starting transfers between devices  94.3 us (8%)
  waiting for transfers between devices  31.3 us (3%)
    scatter-add x1, other arithmetic, shards(): jax.ops.segment_sum(every_amount, every_index, num_segments=grid_cells)  379 us
    gather x2, local copies, waits for them, and re-layouts, shards(): reply = jnp.stack([column_flat[arrived_index], row_flat[arrived_index]])  181 us
    gather x1, local copies, waits for them, and re-layouts, shards(): column_flat[main_index]  90.5 us
    gather x1, local copies, waits for them, and re-layouts, shards(): row_flat[main_index]  90.5 us
    gather x1, local copies, waits for them, and re-layouts, shards(): returned[1].reshape(-1)[remote_slot]  90.5 us
    gather x1, local copies, waits for them, and re-layouts, shards(): returned[0].reshape(-1)[remote_slot]  90.5 us
    scatter x1, local copies, waits for them, and re-layouts, shards(): jnp.zeros((8 * capacity + 1,), jnp.int32).at[slot].set(main_index)[:-1]  60.5 us
    ppermute x12, starting transfers between devices, padded(): lax.ppermute(lax.slice_in_dim(block, block.shape[dim] - width, None, axis...  50.5 us
  transfers between devices with their start and end apart: 36, of which 19 were waited for; matrix products, arithmetic and copies ran while one was open for 53% of the time, Pallas kernels for 0%

commit v1 on v0

v1 whole, which is shorter than its diff:
```python
import functools

import jax
import jax.numpy as jnp
from jax import lax
from jax.experimental import pallas as pl
from jax.experimental.pallas import tpu as pltpu
from jax.sharding import PartitionSpec as P

ITERS = 4
CAP = 2048
SINK_RATE = 0.5
LOW_BOUND = 0.5
HIGH_BOUND = 33.0

WIDE = 256
GROUP = CAP // WIDE
HALO = 8
F32, BF16 = jnp.float32, jnp.bfloat16


def partner(place, kind, count):
    if kind == 0:
        return place
    if kind == 1:
        return place ^ 1
    return (place - 1 if place % 2 == 0 else place + 1) % count


def exchange(value, x_kind, y_kind):
    nx, ny = lax.axis_size("gx"), lax.axis_size("gy")
    pairs = [
        (a * ny + b, partner(a, x_kind, nx) * ny + partner(b, y_kind, ny))
        for a in range(nx)
        for b in range(ny)
    ]
    return lax.ppermute(value, ("gx", "gy"), pairs)


def pieces(value):
    high = value.astype(BF16).astype(F32)
    return high, value - high


def row_iota(count, width=128):
    return lax.broadcasted_iota(jnp.int32, (count, width), 0).astype(F32)


def onehot(row, count):
    return jnp.where(row_iota(count, row.shape[1]) == row, 1.0, 0.0).astype(BF16)


def lanes(parts):
    return jnp.concatenate(parts, axis=1) if len(parts) > 1 else parts[0]


def transposed_dot(left, right):
    return lax.dot_general(left, right, (((1,), (1,)), ((), ())), preferred_element_type=F32)


def dot(left, right):
    return lax.dot_general(left, right, (((1,), (0,)), ((), ())), preferred_element_type=F32)


def kind_of(step, place):
    ahead = 1 - 2 * lax.rem(place, 2)
    return jnp.where(step == 0, 0, jnp.where(step == ahead, 1, 2))


def pack_kernel(
    nyc, cols, rows,
    bin_ref, layer_ref, off_ref, power_ref, spill_ref, cond_ref,
    msga_ref, msgb_ref, owny_ref, slot_ref,
    q_ref, lam_ref, field_ref, acc_ref,
):
    a, b = lax.axis_index("gx"), lax.axis_index("gy")
    groups = 3 * nyc - 1
    table = groups * GROUP
    off = off_ref[...]
    col_code = (off >= 3).astype(jnp.int32) + (off >= 6).astype(jnp.int32)
    x_kind = kind_of(col_code - 1, a)
    y_kind = kind_of(off - 3 * col_code - 1, b)
    group = jnp.where(x_kind > 0, (x_kind - 1) * nyc + y_kind, 2 * nyc - 1 + y_kind)
    group = jnp.where(off == 4, -1, group)
    size = off.shape[0]
    r_i = lax.broadcasted_iota(jnp.int32, (size, size), 0)
    c_i = lax.broadcasted_iota(jnp.int32, (size, size), 1)
    upper = jnp.where(r_i < c_i, 1.0, 0.0).astype(BF16)
    lower = jnp.where(r_i > c_i, 1.0, 0.0).astype(BF16)
    ones = jnp.ones((size, size), BF16)
    slot = jnp.full(off.shape, -1.0, F32)
    for g in range(groups):
        mine = group == g
        mask = jnp.where(mine, 1.0, 0.0).astype(BF16)
        totals = dot(mask, ones).astype(BF16)
        rank = dot(mask, upper) + dot(lower, totals)
        slot = jnp.where(mine, rank + float(g * CAP), slot)
    slot_ref[...] = slot
    q = jnp.floor(slot * (1.0 / WIDE))
    q_ref[...] = q
    lam_ref[...] = slot - q * WIDE
    code = layer_ref[...] * (cols * rows) + bin_ref[...]
    field_ref[0] = (code // rows).astype(F32)
    field_ref[1] = (code % rows).astype(F32)
    power = power_ref[...]
    spill = spill_ref[...]
    field_ref[2], field_ref[3] = pieces(power * (1.0 - spill))
    field_ref[4], field_ref[5] = pieces(power * spill)
    acc_ref[...] = jnp.zeros_like(acc_ref)
    step = 8

    def body(j, carry):
        base = pl.multiple_of(j * step, step)
        q8 = q_ref[pl.ds(base, step), :]
        lam8 = lam_ref[pl.ds(base, step), :]
        vals = [field_ref[f, pl.ds(base, step), :] for f in range(6)]
        picks, marks = [], []
        for i in range(step):
            hit = row_iota(table) == q8[i : i + 1]
            picks.append(
                jnp.concatenate([jnp.where(hit, v[i : i + 1], 0.0) for v in vals], axis=0)
            )
            marks.append(onehot(lam8[i : i + 1], WIDE))
        acc_ref[...] += transposed_dot(lanes(picks).astype(BF16), lanes(marks))
        return carry

    lax.fori_loop(0, size // step, body, 0)
    out = [acc_ref[f * table : (f + 1) * table, :] for f in range(6)]
    sent = [out[0] * float(rows) + out[1], out[2] + out[3], out[4] + out[5]]

    def put(ref, at, g):
        for f in range(3):
            ref[(at * 3 + f) * GROUP : (at * 3 + f + 1) * GROUP, :] = sent[f][
                g * GROUP : (g + 1) * GROUP
            ]

    for y in range(nyc):
        put(msga_ref, y, y)
        put(msgb_ref, y, nyc + y)
        if y:
            put(owny_ref, y - 1, 2 * nyc + y - 1)
    first, last = cond_ref[:, :HALO, :], cond_ref[:, cols - HALO :, :]
    even = lax.rem(a, 2) == 0
    top = nyc * 3 * GROUP
    flat = (-1, cond_ref.shape[2])
    msga_ref[top:, :] = jnp.where(even, last, first).reshape(flat)
    msgb_ref[top:, :] = jnp.where(even, first, last).reshape(flat)


def deposit_block(lc, r, main, spill, cols, cells):
    count = cells
    picks, marks = [], []
    for lc_i, r_i, (mh, ml), (sh, sl) in zip(lc, r, main, spill):
        spot = row_iota(count, lc_i.shape[1])
        other = jnp.where(lc_i >= float(count - cols), lc_i - cols, lc_i + cols)
        here, there = spot == lc_i, spot == other
        high = jnp.where(here, mh, jnp.where(there, sh, 0.0))
        low = jnp.where(here, ml, jnp.where(there, sl, 0.0))
        picks.append(jnp.concatenate([high.astype(BF16), low.astype(BF16)], axis=0))
        marks.append(onehot(r_i, WIDE))
    return transposed_dot(lanes(picks), lanes(marks))


def stay_deposit_kernel(
    cols, bin_ref, layer_ref, off_ref, power_ref, spill_ref, grid_ref, lc_ref, r_ref, val_ref
):
    count, rows = grid_ref.shape[0] // 2, grid_ref.shape[1]
    code = layer_ref[...] * (cols * rows) + bin_ref[...]
    lc_ref[...] = (code // rows).astype(F32)
    r_ref[...] = (code % rows).astype(F32)
    power = jnp.where(off_ref[...] == 4, power_ref[...], 0.0)
    spill = spill_ref[...]
    val_ref[0], val_ref[1] = pieces(power * (1.0 - spill))
    val_ref[2], val_ref[3] = pieces(power * spill)
    grid_ref[...] = jnp.zeros_like(grid_ref)
    step = 8

    def body(j, carry):
        base = pl.multiple_of(j * step, step)
        lc8, r8 = lc_ref[pl.ds(base, step), :], r_ref[pl.ds(base, step), :]
        v = [val_ref[f, pl.ds(base, step), :] for f in range(4)]
        rows_of = lambda x: [x[i : i + 1] for i in range(step)]
        parts = [rows_of(x) for x in v]
        grid_ref[...] += deposit_block(
            rows_of(lc8), rows_of(r8), list(zip(parts[0], parts[1])),
            list(zip(parts[2], parts[3])), cols, count,
        )
        return carry

    lax.fori_loop(0, lc_ref.shape[0] // step, body, 0)


def deposit_groups(grid_ref, sources, cols):
    count, rows = grid_ref.shape[0] // 2, grid_ref.shape[1]
    step = 4
    for ref, at in sources:
        for half in range(GROUP // step):
            lc, r, main, spill = [], [], [], []
            for i in range(step):
                row = at + half * step + i
                code = ref[row : row + 1, :]
                lc_i = jnp.floor(code * (1.0 / rows))
                lc.append(lc_i)
                r.append(code - lc_i * rows)
                main.append(pieces(ref[row + GROUP : row + GROUP + 1, :]))
                spill.append(pieces(ref[row + 2 * GROUP : row + 2 * GROUP + 1, :]))
            grid_ref[...] += deposit_block(lc, r, main, spill, cols, count)


def near_deposit_kernel(cols, stay_ref, recva_ref, recvb_ref, grid_ref):
    grid_ref[...] = stay_ref[...]
    deposit_groups(grid_ref, [(recva_ref, 0), (recvb_ref, 0)], cols)


def far_deposit_kernel(cols, nyc, *refs):
    near_ref, recvy = refs[0], refs[1:nyc]
    grid_ref, edgea_ref, edgeb_ref, acc_ref = refs[nyc:]
    acc_ref[...] = near_ref[...]
    sources = [(ref, 3 * GROUP * i) for ref in recvy for i in range(3)]
    deposit_groups(acc_ref, sources, cols)
    count = acc_ref.shape[0] // 2
    grid = (acc_ref[:count, :] + acc_ref[count:, :]).reshape(grid_ref.shape)
    grid_ref[...] = grid
    first, last = grid[:, :HALO, :], grid[:, cols - HALO :, :]
    even = lax.rem(lax.axis_index("gx"), 2) == 0
    edgea_ref[...] = jnp.where(even, last, first)
    edgeb_ref[...] = jnp.where(even, first, last)


def with_columns(own, from_a, from_b):
    a = lax.axis_index("gx")
    even = lax.rem(a, 2) == 0
    right = jnp.where(even, from_a, from_b)
    left = jnp.where(even, from_b, from_a)
    right = jnp.where(a < lax.axis_size("gx") - 1, right, 0.0)
    left = jnp.where(a > 0, left, 0.0)
    return jnp.concatenate([left, own, right], axis=1)


def row_edge(wide, last):
    rows = wide.shape[1]
    tile = jnp.where(last, wide[:, rows - 128 :], wide[:, :128]).T
    return jnp.where(last, tile[128 - HALO :], tile[:HALO])


def put_edges(ref, at, edge):
    extra = edge.shape[1] - WIDE
    ref[at : at + HALO, :] = edge[:, :WIDE]
    ref[at + HALO : at + 2 * HALO, :] = jnp.concatenate(
        [edge[:, WIDE:], jnp.zeros((HALO, WIDE - extra), F32)], axis=1
    )


def get_edges(ref, at, count):
    return jnp.concatenate(
        [ref[at : at + HALO, :], ref[at + HALO : at + 2 * HALO, : count - WIDE]], axis=1
    )


def y_edges(refs, at, wide):
    even = lax.rem(lax.axis_index("gy"), 2) == 0
    for kind, ref in enumerate(refs):
        put_edges(ref, at, row_edge(wide, even if kind == 0 else jnp.logical_not(even)))


def halo_of(ref, cols, layers, top):
    return ref[top:, :].reshape(layers, HALO, ref.shape[1])


def forward_kernel(nyc, recva_ref, recvb_ref, owny_ref, cond_ref, *msgy_refs):
    layers, cols, rows = cond_ref.shape
    size, top = 3 * GROUP, nyc * 3 * GROUP
    for y, ref in enumerate(msgy_refs):
        ref[:size, :] = owny_ref[y * size : (y + 1) * size, :]
        ref[size : 2 * size, :] = recva_ref[(y + 1) * size : (y + 2) * size, :]
        ref[2 * size : 3 * size, :] = recvb_ref[(y + 1) * size : (y + 2) * size, :]
    wide = with_columns(
        cond_ref[...], halo_of(recva_ref, cols, layers, top), halo_of(recvb_ref, cols, layers, top)
    )
    y_edges(msgy_refs, 3 * size, wide.reshape(-1, rows))


def power_edge_kernel(grid_ref, froma_ref, fromb_ref, *edge_refs):
    wide = with_columns(grid_ref[...], froma_ref[...], fromb_ref[...])
    y_edges(edge_refs, 0, wide.reshape(-1, grid_ref.shape[2]))


def with_rows(wide, edges):
    b, ny = lax.axis_index("gy"), lax.axis_size("gy")
    layers, span, rows = wide.shape
    count = layers * span
    even = lax.rem(b, 2) == 0
    one = edges[0]
    two = edges[1] if len(edges) > 1 else jnp.zeros_like(one)
    after = jnp.where(b < ny - 1, jnp.where(even, one, two), 0.0)
    before = jnp.where(b > 0, jnp.where(even, two, one), 0.0)
    tile = jnp.concatenate([after, jnp.zeros((128 - 2 * HALO, count), F32), before], axis=0).T
    return jnp.concatenate([wide, tile.reshape(layers, span, 128)], axis=2)


def solve_kernel(nyc, *refs):
    grid_ref, froma_ref, fromb_ref, cond_ref, recva_ref, recvb_ref, coupling_ref = refs[:7]
    edge_refs, recvy_refs = refs[7 : 6 + nyc], refs[6 + nyc : 5 + 2 * nyc]
    warmth_ref, slope_ref, k_ref, p_ref, v_ref, u_ref, fc_ref, fr_ref, fl_ref, e_ref = refs[
        5 + 2 * nyc :
    ]
    layers, cols, rows = cond_ref.shape
    span, wide_rows = cols + 2 * HALO, rows + 128
    count = layers * span
    top = nyc * 3 * GROUP
    a, b = lax.axis_index("gx"), lax.axis_index("gy")
    nx, ny = lax.axis_size("gx"), lax.axis_size("gy")
    k_ref[...] = with_rows(
        with_columns(
            cond_ref[...],
            halo_of(recva_ref, cols, layers, top),
            halo_of(recvb_ref, cols, layers, top),
        ),
        [get_edges(ref, 9 * GROUP, count) for ref in recvy_refs],
    )
    p_ref[...] = with_rows(
        with_columns(grid_ref[...], froma_ref[...], fromb_ref[...]),
        [get_edges(ref, 0, count) for ref in edge_refs],
    )
    shape = (span, wide_rows)
    c_i = lax.broadcasted_iota(jnp.int32, shape, 0)
    r_i = lax.broadcasted_iota(jnp.int32, shape, 1)
    c_low = jnp.where(a > 0, 0, HALO)
    c_high = jnp.where(a < nx - 1, span, span - HALO)
    r_high = jnp.where(b < ny - 1, rows + HALO, rows)
    r_low = jnp.where(b > 0, wide_rows - HALO, wide_rows)
    inside = jnp.where((c_i >= c_low) & (c_i < c_high) & ((r_i < r_high) | (r_i >= r_low)), 1.0, 0.0)
    next_c = lambda x: pltpu.roll(x, span - 1, 0)
    prev_c = lambda x: pltpu.roll(x, 1, 0)
    next_r = lambda x: pltpu.roll(x, wide_rows - 1, 1)
    prev_r = lambda x: pltpu.roll(x, 1, 1)
    both_c, both_r = inside * next_c(inside), inside * next_r(inside)
    for l in range(layers):
        k = k_ref[l]
        face_c, face_r = 0.5 * (k + next_c(k)), 0.5 * (k + next_r(k))
        kept_c, kept_r = face_c * both_c, face_r * both_r
        fc_ref[l], fr_ref[l] = kept_c, kept_r
        lost_c, lost_r = face_c - kept_c, face_r - kept_r
        e_ref[l] = SINK_RATE + ((lost_c + prev_c(lost_c)) + (lost_r + prev_r(lost_r)))
        if l + 1 < layers:
            fl_ref[l] = coupling_ref[l] * (0.5 * (k + k_ref[l + 1])) * inside
    middle = 0.5 * (HIGH_BOUND + LOW_BOUND)
    spread = 0.5 * (HIGH_BOUND - LOW_BOUND)
    sigma = middle / spread
    now = 1.0 / sigma
    for l in range(layers):
        start = p_ref[l] / middle
        v_ref[0, l] = start
        u_ref[l] = start
    for sweep in range(ITERS):
        later = 1.0 / (2.0 * sigma - now)
        keep, gain = later * now, 2.0 * later / spread
        old, new = sweep % 2, (sweep + 1) % 2
        below = None
        for l in range(layers):
            v = v_ref[old, l]
            flow_c = fc_ref[l] * (v - next_c(v))
            flow_r = fr_ref[l] * (v - next_r(v))
            result = e_ref[l] * v + (flow_c - prev_c(flow_c)) + (flow_r - prev_r(flow_r))
            if below is not None:
                result = result - below
            if l + 1 < layers:
                below = fl_ref[l] * (v - v_ref[old, l + 1])
                result = result + below
            advance = keep * u_ref[l] + gain * (p_ref[l] - result)
            u_ref[l] = advance
            v_ref[new, l] = v + advance
        now = later
    final = ITERS % 2
    cells = layers * cols
    for l in range(layers):
        v = v_ref[final, l]
        warmth_ref[l] = v[HALO : HALO + cols, :rows]
        for f, slope in enumerate((0.5 * (next_c(v) - prev_c(v)), 0.5 * (next_r(v) - prev_r(v)))):
            high, low = pieces(slope[HALO : HALO + cols, :rows])
            at = f * cells + l * cols
            slope_ref[at : at + cols, :rows] = high.astype(BF16)
            slope_ref[at : at + cols, rows:] = low.astype(BF16)


def gather_block(slope, lc, r):
    cells = slope.shape[0] // 2
    mark = onehot(r, slope.shape[1] // 2)
    found = dot(slope, jnp.concatenate([mark, mark], axis=0))
    here = row_iota(cells, lc.shape[1]) == lc
    return [
        jnp.sum(jnp.where(here, found[f * cells : (f + 1) * cells], 0.0), axis=0, keepdims=True)
        for f in range(2)
    ]


def gather_kernel(sources, slope_ref, *refs):
    ins, out_ref = refs[:-1], refs[-1]
    rows = slope_ref.shape[1] // 2
    for g, (which, at) in enumerate(sources):
        for t in range(GROUP):
            code = ins[which][at + t : at + t + 1, :]
            lc = jnp.floor(code * (1.0 / rows))
            for f, value in enumerate(gather_block(slope_ref[...], lc, code - lc * rows)):
                row = (g * 2 + f) * GROUP + t
                out_ref[row : row + 1, :] = value


def stay_gather_kernel(cols, slope_ref, bin_ref, layer_ref, out_ref, lc_ref, r_ref):
    rows = slope_ref.shape[1] // 2
    code = layer_ref[...] * (cols * rows) + bin_ref[...]
    lc_ref[...] = (code // rows).astype(F32)
    r_ref[...] = (code % rows).astype(F32)
    step = 8

    def body(j, carry):
        base = pl.multiple_of(j * step, step)
        lc8, r8 = lc_ref[pl.ds(base, step), :], r_ref[pl.ds(base, step), :]
        for i in range(0, step, 2):
            two = lambda x: jnp.concatenate([x[i : i + 1], x[i + 1 : i + 2]], axis=1)
            at = pl.multiple_of(base * 128 + i * 128, 256)
            for f, value in enumerate(gather_block(slope_ref[...], two(lc8), two(r8))):
                out_ref[f : f + 1, pl.ds(at, 256)] = value
        return carry

    lax.fori_loop(0, lc_ref.shape[0] // step, body, 0)


def reply_kernel(nyc, near_ref, *refs):
    size = 2 * GROUP
    backs, (a_ref, b_ref) = refs[: nyc - 1], refs[nyc - 1 :]
    a_ref[:size, :] = near_ref[:size, :]
    b_ref[:size, :] = near_ref[size:, :]
    for y, ref in enumerate(backs):
        a_ref[(y + 1) * size : (y + 2) * size, :] = ref[size : 2 * size, :]
        b_ref[(y + 1) * size : (y + 2) * size, :] = ref[2 * size : 3 * size, :]


def unpack_kernel(nyc, backa_ref, backb_ref, *refs):
    backy, (stay_ref, slot_ref, power_ref, out_ref, q_ref, lam_ref, table_ref) = (
        refs[: nyc - 1], refs[nyc - 1 :],
    )
    groups = [(backa_ref, y) for y in range(nyc)] + [(backb_ref, y) for y in range(nyc)]
    groups += [(ref, 0) for ref in backy]
    table = len(groups) * GROUP
    for f in range(2):
        whole = jnp.concatenate(
            [ref[(2 * at + f) * GROUP : (2 * at + f + 1) * GROUP, :] for ref, at in groups], axis=0
        )
        high, low = pieces(whole)
        table_ref[f * table : (f + 1) * table, :WIDE] = high
        table_ref[f * table : (f + 1) * table, WIDE:] = low
    slot = slot_ref[...]
    q = jnp.floor(slot * (1.0 / WIDE))
    q_ref[...] = q
    lam_ref[...] = slot - q * WIDE
    source = table_ref[...].astype(BF16)
    step = 8

    def body(j, carry):
        base = pl.multiple_of(j * step, step)
        q8, lam8 = q_ref[pl.ds(base, step), :], lam_ref[pl.ds(base, step), :]
        power8 = power_ref[pl.ds(base, step), :]
        for i in range(0, step, 2):
            two = lambda x: jnp.concatenate([x[i : i + 1], x[i + 1 : i + 2]], axis=1)
            at = pl.multiple_of(base * 128 + i * 128, 256)
            mark = onehot(two(lam8), WIDE)
            found = dot(source, jnp.concatenate([mark, mark], axis=0))
            place = two(q8)
            here = row_iota(table, 256) == place
            for f in range(2):
                value = jnp.sum(
                    jnp.where(here, found[f * table : (f + 1) * table], 0.0), axis=0, keepdims=True
                )
                value = jnp.where(place >= 0.0, value, stay_ref[f : f + 1, pl.ds(at, 256)])
                out_ref[f : f + 1, pl.ds(at, 256)] = -two(power8) * value
        return carry

    lax.fori_loop(0, q_ref.shape[0] // step, body, 0)


def call(kernel, outs, scratch, *args, scalars=()):
    space = pl.BlockSpec(memory_space=pltpu.VMEM)
    specs = [
        pl.BlockSpec(memory_space=pltpu.SMEM) if i in scalars else space for i in range(len(args))
    ]
    shapes = [jax.ShapeDtypeStruct(shape, dtype) for shape, dtype in outs]
    return pl.pallas_call(
        kernel,
        out_shape=shapes,
        in_specs=specs,
        out_specs=[space] * len(shapes),
        scratch_shapes=scratch,
        compiler_params=pltpu.CompilerParams(vmem_limit_bytes=48 * 1024 * 1024),
    )(*args)


def shards(
    cell_bin, cell_layer, cell_offset, cell_power, spill_weight, conductivity, layer_coupling
):
    layers, cols, rows = conductivity.shape
    cells = cell_bin.shape[0]
    nyc = 2 if lax.axis_size("gy") == 2 else 3
    count = layers * cols
    groups = 3 * nyc - 1
    flat = lambda x: x.reshape(cells // 128, 128)
    bins, layer, off = flat(cell_bin), flat(cell_layer), flat(cell_offset)
    power, spill = flat(cell_power), flat(spill_weight)
    square = bins.shape
    own = 3 * GROUP
    message = (nyc * own + layers * HALO, WIDE)
    vmem = lambda *shape: pltpu.VMEM(shape, F32)
    partial = functools.partial

    msg_a, msg_b, own_y, slot = call(
        partial(pack_kernel, nyc, cols, rows),
        [(message, F32), (message, F32), (((nyc - 1) * own, WIDE), F32), (square, F32)],
        [vmem(*square), vmem(*square), vmem(6, *square), vmem(6 * groups * GROUP, WIDE)],
        bins, layer, off, power, spill, conductivity,
    )
    recv_a, recv_b = exchange(msg_a, 1, 0), exchange(msg_b, 2, 0)
    (stay_grid,) = call(
        partial(stay_deposit_kernel, cols),
        [((2 * count, rows), F32)],
        [vmem(*square), vmem(*square), vmem(4, *square)],
        bins, layer, off, power, spill,
    )
    msg_y = call(
        partial(forward_kernel, nyc),
        [((3 * own + 2 * HALO, WIDE), F32)] * (nyc - 1),
        [],
        recv_a, recv_b, own_y, conductivity,
    )
    recv_y = [exchange(m, 0, i + 1) for i, m in enumerate(msg_y)]
    (near_grid,) = call(
        partial(near_deposit_kernel, cols),
        [((2 * count, rows), F32)],
        [],
        stay_grid, recv_a, recv_b,
    )
    edge = (layers, HALO, rows)
    grid, edge_a, edge_b = call(
        partial(far_deposit_kernel, cols, nyc),
        [(conductivity.shape, F32), (edge, F32), (edge, F32)],
        [vmem(2 * count, rows)],
        near_grid, *recv_y,
    )
    from_a, from_b = exchange(edge_a, 1, 0), exchange(edge_b, 2, 0)
    edges = call(
        power_edge_kernel, [((2 * HALO, WIDE), F32)] * (nyc - 1), [], grid, from_a, from_b
    )
    from_y = [exchange(e, 0, i + 1) for i, e in enumerate(edges)]
    big = (layers, cols + 2 * HALO, rows + 128)
    final_warmth, slope = call(
        partial(solve_kernel, nyc),
        [(conductivity.shape, F32), ((2 * count, 2 * rows), BF16)],
        [vmem(*big), vmem(*big), vmem(2, *big)] + [vmem(*big)] * 5,
        grid, from_a, from_b, conductivity, recv_a, recv_b, layer_coupling, *from_y, *recv_y,
        scalars=(6,),
    )
    answer_y = [
        call(
            partial(gather_kernel, [(0, own * i) for i in range(3)]),
            [((6 * GROUP, WIDE), F32)],
            [],
            slope, r,
        )[0]
        for r in recv_y
    ]
    back_y = [exchange(m, 0, i + 1) for i, m in enumerate(answer_y)]
    (near_answer,) = call(
        partial(gather_kernel, [(0, 0), (1, 0)]),
        [((4 * GROUP, WIDE), F32)],
        [],
        slope, recv_a, recv_b,
    )
    answer_a, answer_b = call(
        partial(reply_kernel, nyc),
        [((2 * nyc * GROUP, WIDE), F32)] * 2,
        [],
        near_answer, *back_y,
    )
    back_a, back_b = exchange(answer_a, 1, 0), exchange(answer_b, 2, 0)
    (stay_value,) = call(
        partial(stay_gather_kernel, cols),
        [((2, cells), F32)],
        [vmem(*square), vmem(*square)],
        slope, bins, layer,
    )
    (pull,) = call(
        partial(unpack_kernel, nyc),
        [((2, cells), F32)],
        [vmem(*square), vmem(*square), vmem(2 * groups * GROUP, 2 * WIDE)],
        back_a, back_b, *back_y, stay_value, slot, power,
    )
    return final_warmth, pull


def solution(mesh):
    cell = P(("gx", "gy"))
    tile = P(None, "gx", "gy")
    return jax.shard_map(
        shards,
        mesh=mesh,
        in_specs=(cell, cell, cell, cell, cell, tile, P()),
        out_specs=(tile, P(None, ("gx", "gy"))),
        check_vma=False,
    )
```

time: 1210 us -> 79.4 us (0.07); the launches traced: 1190 us -> 79 us
  local copies, waits for them, and re-layouts: 674 us -> 5.17 us
  other arithmetic: 388 us -> 0 us
  starting transfers between devices: 94.3 us -> 15.6 us
  Pallas kernels: 0 us -> 48.7 us
  waiting for transfers between devices: 31.3 us -> 8.82 us
    gather x6 -> x0, local copies, waits for them, and re-layouts: 543 us -> none  [the longest x2 181 us: shards(): reply = jnp.stack([column_flat[arrived_index], row_flat[arrived_index]])]
    scatter-add x1 -> x0, other arithmetic: 379 us -> none  [shards(): jax.ops.segment_sum(every_amount, every_index, num_segments=grid_cells)]
    scatter x2 -> x0, local copies, waits for them, and re-layouts: 105 us -> none  [the longest x1 60.5 us: shards(): jnp.zeros((8 * capacity + 1,), jnp.int32).at[slot].set(main_index)[:-1]]
    ppermute x36 -> x9, starting transfers between devices: 94.3 us -> 15.6 us  [exchange(): return lax.ppermute(value, ('gx', 'gy'), pairs)]
    pallas_call x0 -> x12, Pallas kernels: none -> 48.7 us  [call(): pl.pallas_call(kernel, out_shape=shapes, in_specs=specs, out_specs=[space...]
    ppermute x36 -> x9, waiting for transfers between devices: 31.3 us -> 8.82 us  [exchange(): return lax.ppermute(value, ('gx', 'gy'), pairs)]
  transfers between devices with their start and end apart: 36 -> 9, of which waited for: 19 -> 4; matrix products, arithmetic and copies ran while one was open for 53% -> 0% of each run, Pallas kernels for 0% -> 31%
where the time goes in v1:
time: 79.4 us; the launch traced here: 79 us
  Pallas kernels  48.7 us (61%)
  starting transfers between devices  15.6 us (20%)
  waiting for transfers between devices  8.82 us (11%)
  local copies, waits for them, and re-layouts  5.17 us (7%)
    pallas_call x12, Pallas kernels, call(): pl.pallas_call(kernel, out_shape=shapes, in_specs=specs, out_specs=[space...  48.7 us
    ppermute x9, starting transfers between devices, exchange(): return lax.ppermute(value, ('gx', 'gy'), pairs)  15.6 us
    ppermute x9, waiting for transfers between devices, exchange(): return lax.ppermute(value, ('gx', 'gy'), pairs)  8.82 us
    unnamed x24, local copies, waits for them, and re-layouts  5.17 us
  transfers between devices with their start and end apart: 9, of which 4 were waited for; matrix products, arithmetic and copies ran while one was open for 0% of the time, Pallas kernels for 31%

profile of v1, /device:TPU:0, one launch (start us, length us, event | category | flops | bytes accessed | tf_op | source)
XLA Modules:
  0.0 79.0 jit_solution(17717714855138092195)
XLA Ops:
  0.6 0.0 copy-start
  0.6 0.9 %copy-done = f32[8,32,256]{2,1,0:T(8,128)S(1)} copy-done((f32[8,32,256]{2,1,0:T(8,128)S(1)}, f32[8,32,256]{2,1,0:T(8,128)}, u32[]{:S(2)}) %copy-start) | copy-done | bytes 262168
  1.6 0.0 copy-start.2
  1.6 0.8 %copy-done.2 = s32[16384]{0:T(1024)S(1)} copy-done((s32[16384]{0:T(1024)S(1)}, s32[16384]{0:T(1024)}, u32[]{:S(2)}) %copy-start.2) | copy-done | bytes 65560
  2.4 0.0 copy-start.4
  2.4 0.8 %copy-done.4 = s32[16384]{0:T(1024)S(1)} copy-done((s32[16384]{0:T(1024)S(1)}, s32[16384]{0:T(1024)}, u32[]{:S(2)}) %copy-start.4) | copy-done | bytes 65560
  3.3 0.0 copy-start.6
  3.3 0.8 %copy-done.6 = f32[16384]{0:T(1024)S(1)} copy-done((f32[16384]{0:T(1024)S(1)}, f32[16384]{0:T(1024)}, u32[]{:S(2)}) %copy-start.6) | copy-done | bytes 65560
  4.1 0.0 copy-start.8
  4.1 0.8 %copy-done.8 = s32[16384]{0:T(1024)S(1)} copy-done((s32[16384]{0:T(1024)S(1)}, s32[16384]{0:T(1024)}, u32[]{:S(2)}) %copy-start.8) | copy-done | bytes 65560
  4.9 0.8 %copy-done.9 = f32[16384]{0:T(1024)S(1)} copy-done((f32[16384]{0:T(1024)S(1)}, f32[16384]{0:T(1024)}, u32[]{:S(2)}) %copy-start.9) | copy-done | bytes 65560
  5.8 6.3 %shard_map.87 = (f32[112,256]{1,0:T(8,128)S(1)}, f32[112,256]{1,0:T(8,128)S(1)}, f32[24,256]{1,0:T(8,128)S(1)}, f32[128,128]{1,0:T(8,128)S(1)}) custom-call(s32[128,128]{1,0:T(8,128)S(1)} %bitcast.5, s32[128,128]{1,0:T(8,128)S(1)} %bitcast.8, s32[128,128]{1,0:T(8,128)S(1)} %bitcast.14, f32[128,128]{1,0:T(8,128)S(1)} %bitcast.11, f32[128,128]{1,0:T(8,128)S(1)} %bitcast.16, ...), custom_call_target="tpu_custom_call" | custom-call | tf_op jit(solution)/shard_map/pallas_call | solution.py:488
  12.1 0.5 collective-permute-start
  12.6 5.7 %collective-permute-start.1 = (f32[112,256]{1,0:T(8,128)S(1)}, f32[112,256]{1,0:T(8,128)S(1)}, u32[]{:S(2)}, u32[]{:S(2)}) collective-permute-start(f32[112,256]{1,0:T(8,128)S(1)} %get-tuple-element.14), channel_id=1, source_target_pairs={{0,30},{1,31},{2,4},{3,5},{4,2},{5,3},{6,8},{7,9},{8,6},{9,7},{10,... | collective-permute-start | bytes 344072 | tf_op jit(solution)/shard_map/ppermute | solution.py:37
  18.2 0.0 collective-permute-done.recva_ref.refs_4_.refs_0_
  18.2 2.5 %collective-permute-done.1.recvb_ref.refs_5_.refs_1_ = f32[112,256]{1,0:T(8,128)S(1)} collective-permute-done((f32[112,256]{1,0:T(8,128)S(1)}, f32[112,256]{1,0:T(8,128)S(1)}, u32[]{:S(2)}, u32[]{:S(2)}) %collective-permute-start.1) | collective-permute-done | bytes 114720 | tf_op jit(solution)/shard_map/ppermute | solution.py:37
  20.7 0.0 copy-done.1
  20.7 0.1 shard_map.89
  20.8 1.6 %collective-permute-start.2 = (f32[88,256]{1,0:T(8,128)S(1)}, f32[88,256]{1,0:T(8,128)S(1)}, u32[]{:S(2)}, u32[]{:S(2)}) collective-permute-start(f32[88,256]{1,0:T(8,128)S(1)} %shard_map.89), channel_id=1, source_target_pairs={{0,1},{1,0},{2,3},{3,2},{4,5},{5,4},{6,7},{7,6},{8,9},{9,8},{10,11... | collective-permute-start | bytes 270344 | tf_op jit(solution)/shard_map/ppermute | solution.py:37
  22.4 0.0 copy-done.10
  22.4 8.7 %shard_map.86.stay_ref = f32[512,256]{1,0:T(8,128)S(1)} custom-call(s32[128,128]{1,0:T(8,128)S(1)} %bitcast.6, s32[128,128]{1,0:T(8,128)S(1)} %bitcast.9, s32[128,128]{1,0:T(8,128)S(1)} %bitcast.15, f32[128,128]{1,0:T(8,128)S(1)} %bitcast.12, f32[128,128]{1,0:T(8,128)S(1)} %bitcast.17), custom_call_target="tpu_custom_call" | custom-call | tf_op jit(solution)/shard_map/pallas_call | solution.py:488
  31.2 1.6 %shard_map.88.refs_0_ = f32[512,256]{1,0:T(8,128)S(1)} custom-call(f32[512,256]{1,0:T(8,128)S(1)} %shard_map.86.stay_ref, f32[112,256]{1,0:T(8,128)S(1)} %collective-permute-done.recva_ref.refs_4_.refs_0_, f32[112,256]{1,0:T(8,128)S(1)} %collective-permute-done.1.recvb_ref.refs_5_.refs_1_), custom_call_target="tpu_custom_call" | custom-call | tf_op jit(solution)/shard_map/pallas_call | solution.py:488
  32.8 0.0 collective-permute-done.2.refs_1_.refs_8_.refs_0_
  32.8 2.4 %shard_map.90 = (f32[8,32,256]{2,1,0:T(8,128)S(1)}, f32[8,8,256]{2,1,0:T(8,128)S(1)}, f32[8,8,256]{2,1,0:T(8,128)S(1)}) custom-call(f32[512,256]{1,0:T(8,128)S(1)} %shard_map.88.refs_0_, f32[88,256]{1,0:T(8,128)S(1)} %collective-permute-done.2.refs_1_.refs_8_.refs_0_), custom_call_target="tpu_custom_call" | custom-call | tf_op jit(solution)/shard_map/pallas_call | solution.py:488
  35.2 0.1 collective-permute-start.3
  35.3 4.2 %collective-permute-start.4 = (f32[8,8,256]{2,1,0:T(8,128)S(1)}, f32[8,8,256]{2,1,0:T(8,128)S(1)}, u32[]{:S(2)}, u32[]{:S(2)}) collective-permute-start(f32[8,8,256]{2,1,0:T(8,128)S(1)} %get-tuple-element.18), channel_id=1, source_target_pairs={{0,30},{1,31},{2,4},{3,5},{4,2},{5,3},{6,8},{7,9},{8,6},{9,7},{10,... | collective-permute-start | bytes 196616 | tf_op jit(solution)/shard_map/ppermute | solution.py:37
  39.5 0.0 collective-permute-done.3.froma_ref.refs_1_
  39.5 2.2 %collective-permute-done.4.fromb_ref.refs_2_ = f32[8,8,256]{2,1,0:T(8,128)S(1)} collective-permute-done((f32[8,8,256]{2,1,0:T(8,128)S(1)}, f32[8,8,256]{2,1,0:T(8,128)S(1)}, u32[]{:S(2)}, u32[]{:S(2)}) %collective-permute-start.4) | collective-permute-done | bytes 65568 | tf_op jit(solution)/shard_map/ppermute | solution.py:37
  41.8 0.1 shard_map.91
  41.9 0.7 collective-permute-start.5
  42.6 3.1 %collective-permute-done.5.refs_7_ = f32[16,256]{1,0:T(8,128)S(1)} collective-permute-done((f32[16,256]{1,0:T(8,128)S(1)}, f32[16,256]{1,0:T(8,128)S(1)}, u32[]{:S(2)}, u32[]{:S(2)}) %collective-permute-start.5) | collective-permute-done | bytes 16416 | tf_op jit(solution)/shard_map/ppermute | solution.py:37
  45.7 0.0 copy-done.11
  45.7 5.6 %shard_map.92 = (f32[8,32,256]{2,1,0:T(8,128)}, bf16[512,512]{1,0:T(8,128)(2,1)S(1)}) custom-call(f32[8,32,256]{2,1,0:T(8,128)S(1)} %get-tuple-element.16.grid_ref.refs_0_, f32[8,8,256]{2,1,0:T(8,128)S(1)} %collective-permute-done.3.froma_ref.refs_1_, f32[8,8,256]{2,1,0:T(8,128)S(1)} %collective-permute-done.4.fromb_ref.refs_2_, ...), custom_call_target="tpu_custom_call" | custom-call | tf_op jit(solution)/shard_map/pallas_call | solution.py:488
  51.3 3.5 %shard_map.94 = f32[48,256]{1,0:T(8,128)S(1)} custom-call(bf16[512,512]{1,0:T(8,128)(2,1)S(1)} %get-tuple-element.20.slope_ref, f32[88,256]{1,0:T(8,128)S(1)} %collective-permute-done.2.refs_1_.refs_8_.refs_0_), custom_call_target="tpu_custom_call" | custom-call | tf_op jit(solution)/shard_map/pallas_call | solution.py:488
  54.8 0.7 collective-permute-start.6
  55.5 2.4 %shard_map.93.near_ref = f32[32,256]{1,0:T(8,128)S(1)} custom-call(bf16[512,512]{1,0:T(8,128)(2,1)S(1)} %get-tuple-element.20.slope_ref, f32[112,256]{1,0:T(8,128)S(1)} %collective-permute-done.recva_ref.refs_4_.refs_0_, f32[112,256]{1,0:T(8,128)S(1)} %collective-permute-done.1.recvb_ref.refs_5_.refs_1_), custom_call_target="tpu_custom_call" | custom-call | tf_op jit(solution)/shard_map/pallas_call | solution.py:488
  57.9 0.0 copy-start.3
  57.9 1.0 %collective-permute-done.6.refs_0_ = f32[48,256]{1,0:T(8,128)S(1)} collective-permute-done((f32[48,256]{1,0:T(8,128)S(1)}, f32[48,256]{1,0:T(8,128)S(1)}, u32[]{:S(2)}, u32[]{:S(2)}) %collective-permute-start.6) | collective-permute-done | bytes 49184 | tf_op jit(solution)/shard_map/ppermute | solution.py:37
  59.0 0.0 collective-permute-start.7
  59.0 0.0 copy-start.7
  59.0 2.1 %collective-permute-start.8 = (f32[32,256]{1,0:T(8,128)S(1)}, f32[32,256]{1,0:T(8,128)S(1)}, u32[]{:S(2)}, u32[]{:S(2)}) collective-permute-start(f32[32,256]{1,0:T(8,128)S(1)} %get-tuple-element.22), channel_id=1, source_target_pairs={{0,30},{1,31},{2,4},{3,5},{4,2},{5,3},{6,8},{7,9},{8,6},{9,7},{10,... | collective-permute-start | bytes 98312 | tf_op jit(solution)/shard_map/ppermute | solution.py:37
  61.1 0.0 copy-done.5
  61.1 0.0 copy-done.3
  61.1 11.8 %shard_map.96.refs_1_ = f32[2,16384]{1,0:T(2,128)S(1)} custom-call(bf16[512,512]{1,0:T(8,128)(2,1)S(1)} %get-tuple-element.20.slope_ref, s32[128,128]{1,0:T(8,128)S(1)} %bitcast.7, s32[128,128]{1,0:T(8,128)S(1)} %bitcast.10), custom_call_target="tpu_custom_call" | custom-call | tf_op jit(solution)/shard_map/pallas_call | solution.py:488
  72.9 0.0 collective-permute-done.7.backa_ref
  72.9 0.0 collective-permute-done.8.backb_ref
  73.0 0.0 copy-done.7
  73.0 6.1 %shard_map.97 = f32[2,16384]{1,0:T(2,128)} custom-call(f32[32,256]{1,0:T(8,128)S(1)} %collective-permute-done.7.backa_ref, f32[32,256]{1,0:T(8,128)S(1)} %collective-permute-done.8.backb_ref, f32[48,256]{1,0:T(8,128)S(1)} %collective-permute-done.6.refs_0_, f32[2,16384]{1,0:T(2,128)S(1)} %shard_map.96.refs_1_, f32[128,128]{1,0:T(8,128)S(1)} %get-tuple-element.23.refs_2_, ...), custom_call_target="tpu_custom_call" | custom-call | tf_op jit(solution)/shard_map/pallas_call | solution.py:488
  (6 shorter events, 0.0 us)
Async XLA Ops:
  0.6 1.0 %copy-start = (f32[8,32,256]{2,1,0:T(8,128)S(1)}, f32[8,32,256]{2,1,0:T(8,128)}, u32[]{:S(2)}) copy-start(f32[8,32,256]{2,1,0:T(8,128)} %refs_3_.1) | copy-start | bytes 786436
  1.6 0.8 %copy-start.2 = (s32[16384]{0:T(1024)S(1)}, s32[16384]{0:T(1024)}, u32[]{:S(2)}) copy-start(s32[16384]{0:T(1024)} %param.7) | copy-start | bytes 196612
  2.4 0.8 %copy-start.4 = (s32[16384]{0:T(1024)S(1)}, s32[16384]{0:T(1024)}, u32[]{:S(2)}) copy-start(s32[16384]{0:T(1024)} %param.8) | copy-start | bytes 196612
  3.3 0.8 %copy-start.6 = (f32[16384]{0:T(1024)S(1)}, f32[16384]{0:T(1024)}, u32[]{:S(2)}) copy-start(f32[16384]{0:T(1024)} %param.10) | copy-start | bytes 196612
  4.1 0.8 %copy-start.8 = (s32[16384]{0:T(1024)S(1)}, s32[16384]{0:T(1024)}, u32[]{:S(2)}) copy-start(s32[16384]{0:T(1024)} %param.9) | copy-start | bytes 196612
  4.9 0.8 %copy-start.9 = (f32[16384]{0:T(1024)S(1)}, f32[16384]{0:T(1024)}, u32[]{:S(2)}) copy-start(f32[16384]{0:T(1024)} %param.11) | copy-start | bytes 196612
  5.8 14.9 %copy-start.1 = (f32[8,32,256]{2,1,0:T(8,128)S(1)}, f32[8,32,256]{2,1,0:T(8,128)}, u32[]{:S(2)}) copy-start(f32[8,32,256]{2,1,0:T(8,128)} %refs_3_.1) | copy-start | bytes 786436
  12.1 6.2 %collective-permute-start = (f32[112,256]{1,0:T(8,128)S(1)}, f32[112,256]{1,0:T(8,128)S(1)}, u32[]{:S(2)}, u32[]{:S(2)}) collective-permute-start(f32[112,256]{1,0:T(8,128)S(1)} %get-tuple-element.13), channel_id=1, source_target_pairs={{0,2},{1,3},{2,0},{3,1},{4,6},{5,7},{6,4},{7,5},{8,10},{9,11},{10,... | collective-permute-start | bytes 344072 | tf_op jit(solution)/shard_map/ppermute | solution.py:37
  12.6 8.1 %collective-permute-start.1 = (f32[112,256]{1,0:T(8,128)S(1)}, f32[112,256]{1,0:T(8,128)S(1)}, u32[]{:S(2)}, u32[]{:S(2)}) collective-permute-start(f32[112,256]{1,0:T(8,128)S(1)} %get-tuple-element.14), channel_id=1, source_target_pairs={{0,30},{1,31},{2,4},{3,5},{4,2},{5,3},{6,8},{7,9},{8,6},{9,7},{10,... | collective-permute-start | bytes 344072 | tf_op jit(solution)/shard_map/ppermute | solution.py:37
  20.7 1.7 %copy-start.10 = (f32[16384]{0:T(1024)S(1)}, f32[16384]{0:T(1024)}, u32[]{:S(2)}) copy-start(f32[16384]{0:T(1024)} %param.11) | copy-start | bytes 196612
  20.8 11.9 %collective-permute-start.2 = (f32[88,256]{1,0:T(8,128)S(1)}, f32[88,256]{1,0:T(8,128)S(1)}, u32[]{:S(2)}, u32[]{:S(2)}) collective-permute-start(f32[88,256]{1,0:T(8,128)S(1)} %shard_map.89), channel_id=1, source_target_pairs={{0,1},{1,0},{2,3},{3,2},{4,5},{5,4},{6,7},{7,6},{8,9},{9,8},{10,11... | collective-permute-start | bytes 270344 | tf_op jit(solution)/shard_map/ppermute | solution.py:37
  35.2 4.3 %collective-permute-start.3 = (f32[8,8,256]{2,1,0:T(8,128)S(1)}, f32[8,8,256]{2,1,0:T(8,128)S(1)}, u32[]{:S(2)}, u32[]{:S(2)}) collective-permute-start(f32[8,8,256]{2,1,0:T(8,128)S(1)} %get-tuple-element.17), channel_id=1, source_target_pairs={{0,2},{1,3},{2,0},{3,1},{4,6},{5,7},{6,4},{7,5},{8,10},{9,11},{10,... | collective-permute-start | bytes 196616 | tf_op jit(solution)/shard_map/ppermute | solution.py:37
  35.3 6.5 %collective-permute-start.4 = (f32[8,8,256]{2,1,0:T(8,128)S(1)}, f32[8,8,256]{2,1,0:T(8,128)S(1)}, u32[]{:S(2)}, u32[]{:S(2)}) collective-permute-start(f32[8,8,256]{2,1,0:T(8,128)S(1)} %get-tuple-element.18), channel_id=1, source_target_pairs={{0,30},{1,31},{2,4},{3,5},{4,2},{5,3},{6,8},{7,9},{8,6},{9,7},{10,... | collective-permute-start | bytes 196616 | tf_op jit(solution)/shard_map/ppermute | solution.py:37
  41.8 3.9 %copy-start.11 = (f32[7]{0:T(128)S(1)}, f32[7]{0:T(128)}, u32[]{:S(2)}) copy-start(f32[7]{0:T(128)} %refs_6_.1) | copy-start | bytes 88
  41.9 3.8 %collective-permute-start.5 = (f32[16,256]{1,0:T(8,128)S(1)}, f32[16,256]{1,0:T(8,128)S(1)}, u32[]{:S(2)}, u32[]{:S(2)}) collective-permute-start(f32[16,256]{1,0:T(8,128)S(1)} %shard_map.91), channel_id=1, source_target_pairs={{0,1},{1,0},{2,3},{3,2},{4,5},{5,4},{6,7},{7,6},{8,9},{9,8},{10,11... | collective-permute-start | bytes 49160 | tf_op jit(solution)/shard_map/ppermute | solution.py:37
  54.8 4.2 %collective-permute-start.6 = (f32[48,256]{1,0:T(8,128)S(1)}, f32[48,256]{1,0:T(8,128)S(1)}, u32[]{:S(2)}, u32[]{:S(2)}) collective-permute-start(f32[48,256]{1,0:T(8,128)S(1)} %shard_map.94), channel_id=1, source_target_pairs={{0,1},{1,0},{2,3},{3,2},{4,5},{5,4},{6,7},{7,6},{8,9},{9,8},{10,11... | collective-permute-start | bytes 147464 | tf_op jit(solution)/shard_map/ppermute | solution.py:37
  55.5 5.6 %copy-start.5 = (s32[16384]{0:T(1024)S(1)}, s32[16384]{0:T(1024)}, u32[]{:S(2)}) copy-start(s32[16384]{0:T(1024)} %param.8) | copy-start | bytes 196612
  57.9 3.2 %copy-start.3 = (s32[16384]{0:T(1024)S(1)}, s32[16384]{0:T(1024)}, u32[]{:S(2)}) copy-start(s32[16384]{0:T(1024)} %param.7) | copy-start | bytes 196612
  59.0 14.0 %collective-permute-start.7 = (f32[32,256]{1,0:T(8,128)S(1)}, f32[32,256]{1,0:T(8,128)S(1)}, u32[]{:S(2)}, u32[]{:S(2)}) collective-permute-start(f32[32,256]{1,0:T(8,128)S(1)} %get-tuple-element.21), channel_id=1, source_target_pairs={{0,2},{1,3},{2,0},{3,1},{4,6},{5,7},{6,4},{7,5},{8,10},{9,11},{10,... | collective-permute-start | bytes 98312 | tf_op jit(solution)/shard_map/ppermute | solution.py:37
  59.0 14.0 %copy-start.7 = (f32[16384]{0:T(1024)S(1)}, f32[16384]{0:T(1024)}, u32[]{:S(2)}) copy-start(f32[16384]{0:T(1024)} %param.10) | copy-start | bytes 196612
  59.0 14.0 %collective-permute-start.8 = (f32[32,256]{1,0:T(8,128)S(1)}, f32[32,256]{1,0:T(8,128)S(1)}, u32[]{:S(2)}, u32[]{:S(2)}) collective-permute-start(f32[32,256]{1,0:T(8,128)S(1)} %get-tuple-element.22), channel_id=1, source_target_pairs={{0,30},{1,31},{2,4},{3,5},{4,2},{5,3},{6,8},{7,9},{8,6},{9,7},{10,... | collective-permute-start | bytes 98312 | tf_op jit(solution)/shard_map/ppermute | solution.py:37

commit v2 on v1

--- a/solution.py
+++ b/solution.py
@@ -47,7 +47,11 @@
 
 
 def onehot(row, count):
-    return jnp.where(row_iota(count, row.shape[1]) == row, 1.0, 0.0).astype(BF16)
+    return jnp.where(
+        row_iota(count, row.shape[1]).astype(BF16) == row.astype(BF16),
+        jnp.ones((), BF16),
+        jnp.zeros((), BF16),
+    )
 
 
 def lanes(parts):
@@ -69,13 +73,28 @@
 
 def pack_kernel(
     nyc, cols, rows,
-    bin_ref, layer_ref, off_ref, power_ref, spill_ref, cond_ref,
-    msga_ref, msgb_ref, owny_ref, slot_ref,
-    q_ref, lam_ref, field_ref, acc_ref,
+    bin_hbm, layer_hbm, off_hbm, power_hbm, spill_hbm, cond_hbm,
+    msga_ref, msgb_ref, owny_ref, slot_ref, field_ref, power_ref,
+    bin_ref, layer_ref, off_ref, spill_ref, edge_ref, sems, acc_ref,
 ):
     a, b = lax.axis_index("gx"), lax.axis_index("gy")
+    copies = [
+        pltpu.make_async_copy(src, dst, sems.at[i])
+        for i, (src, dst) in enumerate(
+            [
+                (off_hbm, off_ref), (bin_hbm, bin_ref), (layer_hbm, layer_ref),
+                (power_hbm, power_ref), (spill_hbm, spill_ref),
+                (cond_hbm.at[:, :HALO, :], edge_ref.at[0]),
+                (cond_hbm.at[:, cols - HALO :, :], edge_ref.at[1]),
+            ]
+        )
+    ]
+    for copy in copies:
+        copy.start()
+    acc_ref[...] = jnp.zeros_like(acc_ref)
     groups = 3 * nyc - 1
     table = groups * GROUP
+    copies[0].wait()
     off = off_ref[...]
     col_code = (off >= 3).astype(jnp.int32) + (off >= 6).astype(jnp.int32)
     x_kind = kind_of(col_code - 1, a)
@@ -96,9 +115,8 @@
         rank = dot(mask, upper) + dot(lower, totals)
         slot = jnp.where(mine, rank + float(g * CAP), slot)
     slot_ref[...] = slot
-    q = jnp.floor(slot * (1.0 / WIDE))
-    q_ref[...] = q
-    lam_ref[...] = slot - q * WIDE
+    for copy in copies[1:]:
+        copy.wait()
     code = layer_ref[...] * (cols * rows) + bin_ref[...]
     field_ref[0] = (code // rows).astype(F32)
     field_ref[1] = (code % rows).astype(F32)
@@ -106,22 +124,22 @@
     spill = spill_ref[...]
     field_ref[2], field_ref[3] = pieces(power * (1.0 - spill))
     field_ref[4], field_ref[5] = pieces(power * spill)
-    acc_ref[...] = jnp.zeros_like(acc_ref)
-    step = 8
+    step = 32
 
     def body(j, carry):
         base = pl.multiple_of(j * step, step)
-        q8 = q_ref[pl.ds(base, step), :]
-        lam8 = lam_ref[pl.ds(base, step), :]
+        slots = slot_ref[pl.ds(base, step), :]
+        qs = jnp.floor(slots * (1.0 / WIDE))
+        lams = slots - qs * WIDE
         vals = [field_ref[f, pl.ds(base, step), :] for f in range(6)]
         picks, marks = [], []
         for i in range(step):
-            hit = row_iota(table) == q8[i : i + 1]
+            hit = row_iota(table) == qs[i : i + 1]
             picks.append(
-                jnp.concatenate([jnp.where(hit, v[i : i + 1], 0.0) for v in vals], axis=0)
+                jnp.concatenate([jnp.where(hit, v[i : i + 1], 0.0) for v in vals], axis=0).astype(BF16)
             )
-            marks.append(onehot(lam8[i : i + 1], WIDE))
-        acc_ref[...] += transposed_dot(lanes(picks).astype(BF16), lanes(marks))
+            marks.append(onehot(lams[i : i + 1], WIDE))
+        acc_ref[...] += transposed_dot(lanes(picks), lanes(marks))
         return carry
 
     lax.fori_loop(0, size // step, body, 0)
@@ -139,72 +157,64 @@
         put(msgb_ref, y, nyc + y)
         if y:
             put(owny_ref, y - 1, 2 * nyc + y - 1)
-    first, last = cond_ref[:, :HALO, :], cond_ref[:, cols - HALO :, :]
+    first, last = edge_ref[0], edge_ref[1]
     even = lax.rem(a, 2) == 0
     top = nyc * 3 * GROUP
-    flat = (-1, cond_ref.shape[2])
+    flat = (-1, rows)
     msga_ref[top:, :] = jnp.where(even, last, first).reshape(flat)
     msgb_ref[top:, :] = jnp.where(even, first, last).reshape(flat)
 
 
 def deposit_block(lc, r, main, spill, cols, cells):
-    count = cells
     picks, marks = [], []
+    zero = jnp.zeros((), BF16)
+    narrow = lambda x: x.astype(BF16)
     for lc_i, r_i, (mh, ml), (sh, sl) in zip(lc, r, main, spill):
-        spot = row_iota(count, lc_i.shape[1])
-        other = jnp.where(lc_i >= float(count - cols), lc_i - cols, lc_i + cols)
-        here, there = spot == lc_i, spot == other
-        high = jnp.where(here, mh, jnp.where(there, sh, 0.0))
-        low = jnp.where(here, ml, jnp.where(there, sl, 0.0))
-        picks.append(jnp.concatenate([high.astype(BF16), low.astype(BF16)], axis=0))
+        spot = narrow(row_iota(cells, lc_i.shape[1]))
+        other = jnp.where(lc_i >= float(cells - cols), lc_i - cols, lc_i + cols)
+        here, there = spot == narrow(lc_i), spot == narrow(other)
+        high = jnp.where(here, narrow(mh), jnp.where(there, narrow(sh), zero))
+        low = jnp.where(here, narrow(ml), jnp.where(there, narrow(sl), zero))
+        picks.append(jnp.concatenate([high, low], axis=0))
         marks.append(onehot(r_i, WIDE))
     return transposed_dot(lanes(picks), lanes(marks))
 
 
-def stay_deposit_kernel(
-    cols, bin_ref, layer_ref, off_ref, power_ref, spill_ref, grid_ref, lc_ref, r_ref, val_ref
-):
-    count, rows = grid_ref.shape[0] // 2, grid_ref.shape[1]
-    code = layer_ref[...] * (cols * rows) + bin_ref[...]
-    lc_ref[...] = (code // rows).astype(F32)
-    r_ref[...] = (code % rows).astype(F32)
-    power = jnp.where(off_ref[...] == 4, power_ref[...], 0.0)
-    spill = spill_ref[...]
-    val_ref[0], val_ref[1] = pieces(power * (1.0 - spill))
-    val_ref[2], val_ref[3] = pieces(power * spill)
+def stay_deposit_kernel(cols, field_ref, slot_ref, grid_ref, val_ref):
+    count = grid_ref.shape[0] // 2
+    size = slot_ref.shape[0]
+    stays = slot_ref[...] < 0.0
+    for f in range(4):
+        val_ref[f] = jnp.where(stays, field_ref[2 + f], 0.0)
     grid_ref[...] = jnp.zeros_like(grid_ref)
-    step = 8
+    step = 64
 
     def body(j, carry):
         base = pl.multiple_of(j * step, step)
-        lc8, r8 = lc_ref[pl.ds(base, step), :], r_ref[pl.ds(base, step), :]
-        v = [val_ref[f, pl.ds(base, step), :] for f in range(4)]
+        lcs, rs = field_ref[0, pl.ds(base, step), :], field_ref[1, pl.ds(base, step), :]
         rows_of = lambda x: [x[i : i + 1] for i in range(step)]
-        parts = [rows_of(x) for x in v]
+        parts = [rows_of(val_ref[f, pl.ds(base, step), :]) for f in range(4)]
         grid_ref[...] += deposit_block(
-            rows_of(lc8), rows_of(r8), list(zip(parts[0], parts[1])),
+            rows_of(lcs), rows_of(rs), list(zip(parts[0], parts[1])),
             list(zip(parts[2], parts[3])), cols, count,
         )
         return carry
 
-    lax.fori_loop(0, lc_ref.shape[0] // step, body, 0)
+    lax.fori_loop(0, size // step, body, 0)
 
 
 def deposit_groups(grid_ref, sources, cols):
     count, rows = grid_ref.shape[0] // 2, grid_ref.shape[1]
-    step = 4
+    lc, r, main, spill = [], [], [], []
     for ref, at in sources:
-        for half in range(GROUP // step):
-            lc, r, main, spill = [], [], [], []
-            for i in range(step):
-                row = at + half * step + i
-                code = ref[row : row + 1, :]
-                lc_i = jnp.floor(code * (1.0 / rows))
-                lc.append(lc_i)
-                r.append(code - lc_i * rows)
-                main.append(pieces(ref[row + GROUP : row + GROUP + 1, :]))
-                spill.append(pieces(ref[row + 2 * GROUP : row + 2 * GROUP + 1, :]))
-            grid_ref[...] += deposit_block(lc, r, main, spill, cols, count)
+        for row in range(at, at + GROUP):
+            code = ref[row : row + 1, :]
+            lc_i = jnp.floor(code * (1.0 / rows))
+            lc.append(lc_i)
+            r.append(code - lc_i * rows)
+            main.append(pieces(ref[row + GROUP : row + GROUP + 1, :]))
+            spill.append(pieces(ref[row + 2 * GROUP : row + 2 * GROUP + 1, :]))
+    grid_ref[...] += deposit_block(lc, r, main, spill, cols, count)
 
 
 def near_deposit_kernel(cols, stay_ref, recva_ref, recvb_ref, grid_ref):
@@ -267,7 +277,7 @@
     return ref[top:, :].reshape(layers, HALO, ref.shape[1])
 
 
-def forward_kernel(nyc, recva_ref, recvb_ref, owny_ref, cond_ref, *msgy_refs):
+def forward_kernel(nyc, recva_ref, recvb_ref, owny_ref, cond_ref, after_ref, *msgy_refs):
     layers, cols, rows = cond_ref.shape
     size, top = 3 * GROUP, nyc * 3 * GROUP
     for y, ref in enumerate(msgy_refs):
@@ -298,12 +308,17 @@
     return jnp.concatenate([wide, tile.reshape(layers, span, 128)], axis=2)
 
 
-def solve_kernel(nyc, *refs):
-    grid_ref, froma_ref, fromb_ref, cond_ref, recva_ref, recvb_ref, coupling_ref = refs[:7]
-    edge_refs, recvy_refs = refs[7 : 6 + nyc], refs[6 + nyc : 5 + 2 * nyc]
-    warmth_ref, slope_ref, k_ref, p_ref, v_ref, u_ref, fc_ref, fr_ref, fl_ref, e_ref = refs[
-        5 + 2 * nyc :
-    ]
+def shifts(span, wide_rows):
+    return (
+        lambda x: pltpu.roll(x, span - 1, 0),
+        lambda x: pltpu.roll(x, 1, 0),
+        lambda x: pltpu.roll(x, wide_rows - 1, 1),
+        lambda x: pltpu.roll(x, 1, 1),
+    )
+
+
+def face_kernel(nyc, cond_ref, recva_ref, recvb_ref, coupling_ref, *refs):
+    recvy_refs, (fc_ref, fr_ref, fl_ref, e_ref, k_ref) = refs[: nyc - 1], refs[nyc - 1 :]
     layers, cols, rows = cond_ref.shape
     span, wide_rows = cols + 2 * HALO, rows + 128
     count = layers * span
@@ -318,10 +333,6 @@
         ),
         [get_edges(ref, 9 * GROUP, count) for ref in recvy_refs],
     )
-    p_ref[...] = with_rows(
-        with_columns(grid_ref[...], froma_ref[...], fromb_ref[...]),
-        [get_edges(ref, 0, count) for ref in edge_refs],
-    )
     shape = (span, wide_rows)
     c_i = lax.broadcasted_iota(jnp.int32, shape, 0)
     r_i = lax.broadcasted_iota(jnp.int32, shape, 1)
@@ -330,10 +341,7 @@
     r_high = jnp.where(b < ny - 1, rows + HALO, rows)
     r_low = jnp.where(b > 0, wide_rows - HALO, wide_rows)
     inside = jnp.where((c_i >= c_low) & (c_i < c_high) & ((r_i < r_high) | (r_i >= r_low)), 1.0, 0.0)
-    next_c = lambda x: pltpu.roll(x, span - 1, 0)
-    prev_c = lambda x: pltpu.roll(x, 1, 0)
-    next_r = lambda x: pltpu.roll(x, wide_rows - 1, 1)
-    prev_r = lambda x: pltpu.roll(x, 1, 1)
+    next_c, prev_c, next_r, prev_r = shifts(span, wide_rows)
     both_c, both_r = inside * next_c(inside), inside * next_r(inside)
     for l in range(layers):
         k = k_ref[l]
@@ -344,6 +352,17 @@
         e_ref[l] = SINK_RATE + ((lost_c + prev_c(lost_c)) + (lost_r + prev_r(lost_r)))
         if l + 1 < layers:
             fl_ref[l] = coupling_ref[l] * (0.5 * (k + k_ref[l + 1])) * inside
+
+
+def solve_kernel(nyc, grid_ref, froma_ref, fromb_ref, fc_ref, fr_ref, fl_ref, e_ref, *refs):
+    edge_refs, (warmth_ref, slope_ref, p_ref, v_ref, u_ref) = refs[: nyc - 1], refs[nyc - 1 :]
+    layers, cols, rows = grid_ref.shape
+    span, wide_rows = cols + 2 * HALO, rows + 128
+    p_ref[...] = with_rows(
+        with_columns(grid_ref[...], froma_ref[...], fromb_ref[...]),
+        [get_edges(ref, 0, layers * span) for ref in edge_refs],
+    )
+    next_c, prev_c, next_r, prev_r = shifts(span, wide_rows)
     middle = 0.5 * (HIGH_BOUND + LOW_BOUND)
     spread = 0.5 * (HIGH_BOUND - LOW_BOUND)
     sigma = middle / spread
@@ -406,24 +425,20 @@
                 out_ref[row : row + 1, :] = value
 
 
-def stay_gather_kernel(cols, slope_ref, bin_ref, layer_ref, out_ref, lc_ref, r_ref):
-    rows = slope_ref.shape[1] // 2
-    code = layer_ref[...] * (cols * rows) + bin_ref[...]
-    lc_ref[...] = (code // rows).astype(F32)
-    r_ref[...] = (code % rows).astype(F32)
-    step = 8
+def stay_gather_kernel(slope_ref, field_ref, out_ref):
+    step = 32
 
     def body(j, carry):
         base = pl.multiple_of(j * step, step)
-        lc8, r8 = lc_ref[pl.ds(base, step), :], r_ref[pl.ds(base, step), :]
-        for i in range(0, step, 2):
-            two = lambda x: jnp.concatenate([x[i : i + 1], x[i + 1 : i + 2]], axis=1)
-            at = pl.multiple_of(base * 128 + i * 128, 256)
-            for f, value in enumerate(gather_block(slope_ref[...], two(lc8), two(r8))):
-                out_ref[f : f + 1, pl.ds(at, 256)] = value
+        lcs, rs = field_ref[0, pl.ds(base, step), :], field_ref[1, pl.ds(base, step), :]
+        for i in range(0, step, 4):
+            many = lambda x: lanes([x[i + k : i + k + 1] for k in range(4)])
+            at = pl.multiple_of(base * 128 + i * 128, 512)
+            for f, value in enumerate(gather_block(slope_ref[...], many(lcs), many(rs))):
+                out_ref[f : f + 1, pl.ds(at, 512)] = value
         return carry
 
-    lax.fori_loop(0, lc_ref.shape[0] // step, body, 0)
+    lax.fori_loop(0, field_ref.shape[1] // step, body, 0)
 
 
 def reply_kernel(nyc, near_ref, *refs):
@@ -437,9 +452,7 @@
 
 
 def unpack_kernel(nyc, backa_ref, backb_ref, *refs):
-    backy, (stay_ref, slot_ref, power_ref, out_ref, q_ref, lam_ref, table_ref) = (
-        refs[: nyc - 1], refs[nyc - 1 :],
-    )
+    backy, (stay_ref, slot_ref, power_ref, out_ref, table_ref) = refs[: nyc - 1], refs[nyc - 1 :]
     groups = [(backa_ref, y) for y in range(nyc)] + [(backb_ref, y) for y in range(nyc)]
     groups += [(ref, 0) for ref in backy]
     table = len(groups) * GROUP
@@ -450,40 +463,36 @@
         high, low = pieces(whole)
         table_ref[f * table : (f + 1) * table, :WIDE] = high
         table_ref[f * table : (f + 1) * table, WIDE:] = low
-    slot = slot_ref[...]
-    q = jnp.floor(slot * (1.0 / WIDE))
-    q_ref[...] = q
-    lam_ref[...] = slot - q * WIDE
     source = table_ref[...].astype(BF16)
-    step = 8
+    step = 32
 
     def body(j, carry):
         base = pl.multiple_of(j * step, step)
-        q8, lam8 = q_ref[pl.ds(base, step), :], lam_ref[pl.ds(base, step), :]
-        power8 = power_ref[pl.ds(base, step), :]
-        for i in range(0, step, 2):
-            two = lambda x: jnp.concatenate([x[i : i + 1], x[i + 1 : i + 2]], axis=1)
-            at = pl.multiple_of(base * 128 + i * 128, 256)
-            mark = onehot(two(lam8), WIDE)
+        slots = slot_ref[pl.ds(base, step), :]
+        qs = jnp.floor(slots * (1.0 / WIDE))
+        lams = slots - qs * WIDE
+        powers = power_ref[pl.ds(base, step), :]
+        for i in range(0, step, 8):
+            many = lambda x: lanes([x[i + k : i + k + 1] for k in range(8)])
+            at = pl.multiple_of(base * 128 + i * 128, 1024)
+            mark = onehot(many(lams), WIDE)
             found = dot(source, jnp.concatenate([mark, mark], axis=0))
-            place = two(q8)
-            here = row_iota(table, 256) == place
+            place = many(qs)
+            here = row_iota(table, 1024) == place
             for f in range(2):
                 value = jnp.sum(
                     jnp.where(here, found[f * table : (f + 1) * table], 0.0), axis=0, keepdims=True
                 )
-                value = jnp.where(place >= 0.0, value, stay_ref[f : f + 1, pl.ds(at, 256)])
-                out_ref[f : f + 1, pl.ds(at, 256)] = -two(power8) * value
+                value = jnp.where(place >= 0.0, value, stay_ref[f : f + 1, pl.ds(at, 1024)])
+                out_ref[f : f + 1, pl.ds(at, 1024)] = -many(powers) * value
         return carry
 
-    lax.fori_loop(0, q_ref.shape[0] // step, body, 0)
-
-
-def call(kernel, outs, scratch, *args, scalars=()):
+    lax.fori_loop(0, slot_ref.shape[0] // step, body, 0)
+
+
+def call(kernel, outs, scratch, *args, spaces={}):
     space = pl.BlockSpec(memory_space=pltpu.VMEM)
-    specs = [
-        pl.BlockSpec(memory_space=pltpu.SMEM) if i in scalars else space for i in range(len(args))
-    ]
+    specs = [pl.BlockSpec(memory_space=spaces.get(i, pltpu.VMEM)) for i in range(len(args))]
     shapes = [jax.ShapeDtypeStruct(shape, dtype) for shape, dtype in outs]
     return pl.pallas_call(
         kernel,
@@ -512,24 +521,34 @@
     vmem = lambda *shape: pltpu.VMEM(shape, F32)
     partial = functools.partial
 
-    msg_a, msg_b, own_y, slot = call(
+    tile = conductivity.shape
+    msg_a, msg_b, own_y, slot, fields, power = call(
         partial(pack_kernel, nyc, cols, rows),
-        [(message, F32), (message, F32), (((nyc - 1) * own, WIDE), F32), (square, F32)],
-        [vmem(*square), vmem(*square), vmem(6, *square), vmem(6 * groups * GROUP, WIDE)],
+        [
+            (message, F32), (message, F32), (((nyc - 1) * own, WIDE), F32),
+            (square, F32), ((6, *square), F32), (square, F32),
+        ],
+        [pltpu.VMEM(square, jnp.int32)] * 3
+        + [
+            vmem(*square), vmem(2, layers, HALO, rows), pltpu.SemaphoreType.DMA((7,)),
+            vmem(6 * groups * GROUP, WIDE),
+        ],
         bins, layer, off, power, spill, conductivity,
+        spaces={i: pltpu.HBM for i in range(6)},
     )
     recv_a, recv_b = exchange(msg_a, 1, 0), exchange(msg_b, 2, 0)
     (stay_grid,) = call(
         partial(stay_deposit_kernel, cols),
         [((2 * count, rows), F32)],
-        [vmem(*square), vmem(*square), vmem(4, *square)],
-        bins, layer, off, power, spill,
+        [vmem(4, *square)],
+        fields, slot,
     )
     msg_y = call(
         partial(forward_kernel, nyc),
         [((3 * own + 2 * HALO, WIDE), F32)] * (nyc - 1),
         [],
-        recv_a, recv_b, own_y, conductivity,
+        recv_a, recv_b, own_y, conductivity, stay_grid,
+        spaces={4: pl.ANY},
     )
     recv_y = [exchange(m, 0, i + 1) for i, m in enumerate(msg_y)]
     (near_grid,) = call(
@@ -551,12 +570,18 @@
     )
     from_y = [exchange(e, 0, i + 1) for i, e in enumerate(edges)]
     big = (layers, cols + 2 * HALO, rows + 128)
+    faces = call(
+        partial(face_kernel, nyc),
+        [(big, F32)] * 4,
+        [vmem(*big)],
+        conductivity, recv_a, recv_b, layer_coupling, *recv_y,
+        spaces={3: pltpu.SMEM},
+    )
     final_warmth, slope = call(
         partial(solve_kernel, nyc),
-        [(conductivity.shape, F32), ((2 * count, 2 * rows), BF16)],
-        [vmem(*big), vmem(*big), vmem(2, *big)] + [vmem(*big)] * 5,
-        grid, from_a, from_b, conductivity, recv_a, recv_b, layer_coupling, *from_y, *recv_y,
-        scalars=(6,),
+        [(tile, F32), ((2 * count, 2 * rows), BF16)],
+        [vmem(*big), vmem(2, *big), vmem(*big)],
+        grid, from_a, from_b, *faces, *from_y,
     )
     answer_y = [
         call(
@@ -581,16 +606,11 @@
         near_answer, *back_y,
     )
     back_a, back_b = exchange(answer_a, 1, 0), exchange(answer_b, 2, 0)
-    (stay_value,) = call(
-        partial(stay_gather_kernel, cols),
-        [((2, cells), F32)],
-        [vmem(*square), vmem(*square)],
-        slope, bins, layer,
-    )
+    (stay_value,) = call(stay_gather_kernel, [((2, cells), F32)], [], slope, fields)
     (pull,) = call(
         partial(unpack_kernel, nyc),
         [((2, cells), F32)],
-        [vmem(*square), vmem(*square), vmem(2 * groups * GROUP, 2 * WIDE)],
+        [vmem(2 * groups * GROUP, 2 * WIDE)],
         back_a, back_b, *back_y, stay_value, slot, power,
     )
     return final_warmth, pull

time: 79.4 us -> 64.6 us (0.81)
  Pallas kernels: 48.7 us -> 37.9 us
  starting transfers between devices: 15.6 us -> 12.4 us
    pallas_call x12 -> x13, Pallas kernels: 48.7 us -> 37.9 us  [call(): pl.pallas_call(kernel, out_shape=shapes, in_specs=specs, out_specs=[space...]
    ppermute x9, starting transfers between devices: 15.6 us -> 12.4 us  [exchange(): return lax.ppermute(value, ('gx', 'gy'), pairs)]
    unnamed x24 -> x16, local copies, waits for them, and re-layouts: 5.17 us -> 5.15 us
  transfers between devices with their start and end apart: 9 -> 9, of which waited for: 4 -> 5; matrix products, arithmetic and copies ran while one was open for 0% -> 0% of each run, Pallas kernels for 31% -> 30%
where the time goes in v2:
time: 64.6 us; the launch traced here: 64.2 us
  Pallas kernels  37.9 us (59%)
  starting transfers between devices  12.4 us (19%)
  waiting for transfers between devices  8.03 us (12%)
  local copies, waits for them, and re-layouts  5.15 us (8%)
  between operations  0.79 us (1%)
    pallas_call x13, Pallas kernels, call(): pl.pallas_call(kernel, out_shape=shapes, in_specs=specs, out_specs=[space...  37.9 us
    ppermute x9, starting transfers between devices, exchange(): return lax.ppermute(value, ('gx', 'gy'), pairs)  12.4 us
    ppermute x9, waiting for transfers between devices, exchange(): return lax.ppermute(value, ('gx', 'gy'), pairs)  8.03 us
    unnamed x16, local copies, waits for them, and re-layouts  5.15 us
  transfers between devices with their start and end apart: 9, of which 5 were waited for; matrix products, arithmetic and copies ran while one was open for 0% of the time, Pallas kernels for 30%

profile of v2, /device:TPU:0, one launch (start us, length us, event | category | flops | bytes accessed | tf_op | source)
XLA Modules:
  0.0 64.2 jit_solution(11309070855306811549)
XLA Ops:
  0.6 0.0 copy-start
  0.6 0.9 %copy-done = f32[8,32,256]{2,1,0:T(8,128)S(1)} copy-done((f32[8,32,256]{2,1,0:T(8,128)S(1)}, f32[8,32,256]{2,1,0:T(8,128)}, u32[]{:S(2)}) %copy-start) | copy-done | bytes 262168
  1.6 0.0 copy-start.2
  1.6 0.8 %copy-done.2 = s32[16384]{0:T(1024)S(1)} copy-done((s32[16384]{0:T(1024)S(1)}, s32[16384]{0:T(1024)}, u32[]{:S(2)}) %copy-start.2) | copy-done | bytes 65560
  2.4 0.0 copy-start.3
  2.4 0.8 %copy-done.3 = s32[16384]{0:T(1024)S(1)} copy-done((s32[16384]{0:T(1024)S(1)}, s32[16384]{0:T(1024)}, u32[]{:S(2)}) %copy-start.3) | copy-done | bytes 65560
  3.3 0.0 copy-start.4
  3.3 0.8 %copy-done.4 = s32[16384]{0:T(1024)S(1)} copy-done((s32[16384]{0:T(1024)S(1)}, s32[16384]{0:T(1024)}, u32[]{:S(2)}) %copy-start.4) | copy-done | bytes 65560
  4.1 0.0 copy-start.5
  4.1 0.8 %copy-done.5 = f32[16384]{0:T(1024)S(1)} copy-done((f32[16384]{0:T(1024)S(1)}, f32[16384]{0:T(1024)}, u32[]{:S(2)}) %copy-start.5) | copy-done | bytes 65560
  4.9 0.0 copy-start.6
  4.9 0.8 %copy-done.6 = f32[16384]{0:T(1024)S(1)} copy-done((f32[16384]{0:T(1024)S(1)}, f32[16384]{0:T(1024)}, u32[]{:S(2)}) %copy-start.6) | copy-done | bytes 65560
  5.8 4.3 %shard_map.86 = (f32[112,256]{1,0:T(8,128)S(1)}, f32[112,256]{1,0:T(8,128)S(1)}, f32[24,256]{1,0:T(8,128)S(1)}, f32[128,128]{1,0:T(8,128)S(1)}, f32[6,128,128]{2,1,0:T(8,128)S(1)}, /*index=5*/f32[128,128]{1,0:T(8,128)S(1)}) custom-call(s32[128,128]{1,0:T(8,128)S(1)} %bitcast.5, s32[128,128]{1,0:T(8,128)S(1)} %bitcast.6, s32[128,128]{1,0:T(8,128)S(1)} %bitcast.7, ...), custom_call_target="tpu_custom_call" | custom-call | tf_op jit(solution)/shard_map/pallas_call | solution.py:497
  10.1 0.5 collective-permute-start
  10.6 5.7 %collective-permute-start.1 = (f32[112,256]{1,0:T(8,128)S(1)}, f32[112,256]{1,0:T(8,128)S(1)}, u32[]{:S(2)}, u32[]{:S(2)}) collective-permute-start(f32[112,256]{1,0:T(8,128)S(1)} %get-tuple-element.22), channel_id=1, source_target_pairs={{0,30},{1,31},{2,4},{3,5},{4,2},{5,3},{6,8},{7,9},{8,6},{9,7},{10,... | collective-permute-start | bytes 344072 | tf_op jit(solution)/shard_map/ppermute | solution.py:37
  16.3 0.0 copy-start.1
  16.3 5.0 %shard_map.87.stay_ref.after_ref = f32[512,256]{1,0:T(8,128)S(1)} custom-call(f32[6,128,128]{2,1,0:T(8,128)S(1)} %get-tuple-element.19.field_ref, f32[128,128]{1,0:T(8,128)S(1)} %get-tuple-element.20.slot_ref.refs_2_), custom_call_target="tpu_custom_call" | custom-call | tf_op jit(solution)/shard_map/pallas_call | solution.py:497
  21.2 0.0 collective-permute-done.recva_ref.refs_0_
  21.2 0.0 collective-permute-done.1.recvb_ref.refs_1_
  21.3 0.0 copy-done.1
  21.3 0.1 shard_map.89
  21.4 1.6 %collective-permute-start.2 = (f32[88,256]{1,0:T(8,128)S(1)}, f32[88,256]{1,0:T(8,128)S(1)}, u32[]{:S(2)}, u32[]{:S(2)}) collective-permute-start(f32[88,256]{1,0:T(8,128)S(1)} %shard_map.89), channel_id=1, source_target_pairs={{0,1},{1,0},{2,3},{3,2},{4,5},{5,4},{6,7},{7,6},{8,9},{9,8},{10,11... | collective-permute-start | bytes 270344 | tf_op jit(solution)/shard_map/ppermute | solution.py:37
  23.0 1.3 %shard_map.88.refs_0_ = f32[512,256]{1,0:T(8,128)S(1)} custom-call(f32[512,256]{1,0:T(8,128)S(1)} %shard_map.87.stay_ref.after_ref, f32[112,256]{1,0:T(8,128)S(1)} %collective-permute-done.recva_ref.refs_0_, f32[112,256]{1,0:T(8,128)S(1)} %collective-permute-done.1.recvb_ref.refs_1_), custom_call_target="tpu_custom_call" | custom-call | tf_op jit(solution)/shard_map/pallas_call | solution.py:497
  24.3 1.7 %collective-permute-done.2.refs_1_.refs_0_ = f32[88,256]{1,0:T(8,128)S(1)} collective-permute-done((f32[88,256]{1,0:T(8,128)S(1)}, f32[88,256]{1,0:T(8,128)S(1)}, u32[]{:S(2)}, u32[]{:S(2)}) %collective-permute-start.2) | collective-permute-done | bytes 90144 | tf_op jit(solution)/shard_map/ppermute | solution.py:37
  26.0 1.8 %shard_map.90 = (f32[8,32,256]{2,1,0:T(8,128)S(1)}, f32[8,8,256]{2,1,0:T(8,128)S(1)}, f32[8,8,256]{2,1,0:T(8,128)S(1)}) custom-call(f32[512,256]{1,0:T(8,128)S(1)} %shard_map.88.refs_0_, f32[88,256]{1,0:T(8,128)S(1)} %collective-permute-done.2.refs_1_.refs_0_), custom_call_target="tpu_custom_call" | custom-call | tf_op jit(solution)/shard_map/pallas_call | solution.py:497
  27.8 0.1 collective-permute-start.3
  27.9 1.0 %collective-permute-start.4 = (f32[8,8,256]{2,1,0:T(8,128)S(1)}, f32[8,8,256]{2,1,0:T(8,128)S(1)}, u32[]{:S(2)}, u32[]{:S(2)}) collective-permute-start(f32[8,8,256]{2,1,0:T(8,128)S(1)} %get-tuple-element.26), channel_id=1, source_target_pairs={{0,30},{1,31},{2,4},{3,5},{4,2},{5,3},{6,8},{7,9},{8,6},{9,7},{10,... | collective-permute-start | bytes 196616 | tf_op jit(solution)/shard_map/ppermute | solution.py:37
  28.9 0.2 collective-permute-done.3.froma_ref
  29.2 5.2 %collective-permute-done.4.fromb_ref = f32[8,8,256]{2,1,0:T(8,128)S(1)} collective-permute-done((f32[8,8,256]{2,1,0:T(8,128)S(1)}, f32[8,8,256]{2,1,0:T(8,128)S(1)}, u32[]{:S(2)}, u32[]{:S(2)}) %collective-permute-start.4) | collective-permute-done | bytes 65568 | tf_op jit(solution)/shard_map/ppermute | solution.py:37
  34.4 0.0 copy-start.7
  34.4 0.1 shard_map.92
  34.5 1.6 %collective-permute-start.5 = (f32[16,256]{1,0:T(8,128)S(1)}, f32[16,256]{1,0:T(8,128)S(1)}, u32[]{:S(2)}, u32[]{:S(2)}) collective-permute-start(f32[16,256]{1,0:T(8,128)S(1)} %shard_map.92), channel_id=1, source_target_pairs={{0,1},{1,0},{2,3},{3,2},{4,5},{5,4},{6,7},{7,6},{8,9},{9,8},{10,11... | collective-permute-start | bytes 49160 | tf_op jit(solution)/shard_map/ppermute | solution.py:37
  36.1 0.0 copy-done.7
  36.1 1.4 %shard_map.91 = (f32[8,48,384]{2,1,0:T(8,128)S(1)}, f32[8,48,384]{2,1,0:T(8,128)S(1)}, f32[8,48,384]{2,1,0:T(8,128)S(1)}, f32[8,48,384]{2,1,0:T(8,128)S(1)}) custom-call(f32[8,32,256]{2,1,0:T(8,128)S(1)} %copy-done.1, f32[112,256]{1,0:T(8,128)S(1)} %collective-permute-done.recva_ref.refs_0_, f32[112,256]{1,0:T(8,128)S(1)} %collective-permute-done.1.recvb_ref.refs_1_, ...), custom_call_target="tpu_custom_call" | custom-call | tf_op jit(solution)/shard_map/pallas_call | solution.py:497
  37.6 0.7 %collective-permute-done.5.refs_0_ = f32[16,256]{1,0:T(8,128)S(1)} collective-permute-done((f32[16,256]{1,0:T(8,128)S(1)}, f32[16,256]{1,0:T(8,128)S(1)}, u32[]{:S(2)}, u32[]{:S(2)}) %collective-permute-start.5) | collective-permute-done | bytes 16416 | tf_op jit(solution)/shard_map/ppermute | solution.py:37
  38.3 4.3 %shard_map.93 = (f32[8,32,256]{2,1,0:T(8,128)}, bf16[512,512]{1,0:T(8,128)(2,1)S(1)}) custom-call(f32[8,32,256]{2,1,0:T(8,128)S(1)} %get-tuple-element.24.grid_ref, f32[8,8,256]{2,1,0:T(8,128)S(1)} %collective-permute-done.3.froma_ref, f32[8,8,256]{2,1,0:T(8,128)S(1)} %collective-permute-done.4.fromb_ref, f32[8,48,384]{2,1,0:T(8,128)S(1)} %get-tuple-element.27.fc_ref, ...), custom_call_target="tpu_custom_call" | custom-call | tf_op jit(solution)/shard_map/pallas_call | solution.py:497
  42.6 3.5 %shard_map.95 = f32[48,256]{1,0:T(8,128)S(1)} custom-call(bf16[512,512]{1,0:T(8,128)(2,1)S(1)} %get-tuple-element.32.slope_ref, f32[88,256]{1,0:T(8,128)S(1)} %collective-permute-done.2.refs_1_.refs_0_), custom_call_target="tpu_custom_call" | custom-call | tf_op jit(solution)/shard_map/pallas_call | solution.py:497
  46.1 1.6 %collective-permute-start.6 = (f32[48,256]{1,0:T(8,128)S(1)}, f32[48,256]{1,0:T(8,128)S(1)}, u32[]{:S(2)}, u32[]{:S(2)}) collective-permute-start(f32[48,256]{1,0:T(8,128)S(1)} %shard_map.95), channel_id=1, source_target_pairs={{0,1},{1,0},{2,3},{3,2},{4,5},{5,4},{6,7},{7,6},{8,9},{9,8},{10,11... | collective-permute-start | bytes 147464 | tf_op jit(solution)/shard_map/ppermute | solution.py:37
  47.7 2.4 %shard_map.94.near_ref = f32[32,256]{1,0:T(8,128)S(1)} custom-call(bf16[512,512]{1,0:T(8,128)(2,1)S(1)} %get-tuple-element.32.slope_ref, f32[112,256]{1,0:T(8,128)S(1)} %collective-permute-done.recva_ref.refs_0_, f32[112,256]{1,0:T(8,128)S(1)} %collective-permute-done.1.recvb_ref.refs_1_), custom_call_target="tpu_custom_call" | custom-call | tf_op jit(solution)/shard_map/pallas_call | solution.py:497
  50.1 0.2 collective-permute-done.6.refs_0_
  50.3 0.2 collective-permute-start.7
  50.4 0.1 collective-permute-start.8
  50.5 9.5 %shard_map.97.refs_1_ = f32[2,16384]{1,0:T(2,128)S(1)} custom-call(bf16[512,512]{1,0:T(8,128)(2,1)S(1)} %get-tuple-element.32.slope_ref, f32[6,128,128]{2,1,0:T(8,128)S(1)} %get-tuple-element.19.field_ref), custom_call_target="tpu_custom_call" | custom-call | tf_op jit(solution)/shard_map/pallas_call | solution.py:497
  60.0 0.0 collective-permute-done.7.backa_ref
  60.0 0.0 collective-permute-done.8.backb_ref
  60.0 4.2 %shard_map.98 = f32[2,16384]{1,0:T(2,128)} custom-call(f32[32,256]{1,0:T(8,128)S(1)} %collective-permute-done.7.backa_ref, f32[32,256]{1,0:T(8,128)S(1)} %collective-permute-done.8.backb_ref, f32[48,256]{1,0:T(8,128)S(1)} %collective-permute-done.6.refs_0_, f32[2,16384]{1,0:T(2,128)S(1)} %shard_map.97.refs_1_, ...), custom_call_target="tpu_custom_call" | custom-call | tf_op jit(solution)/shard_map/pallas_call | solution.py:497
  (1 shorter events, 0.0 us)
Async XLA Ops:
  0.6 1.0 %copy-start = (f32[8,32,256]{2,1,0:T(8,128)S(1)}, f32[8,32,256]{2,1,0:T(8,128)}, u32[]{:S(2)}) copy-start(f32[8,32,256]{2,1,0:T(8,128)} %cond_ref.3) | copy-start | bytes 786436
  1.6 0.8 %copy-start.2 = (s32[16384]{0:T(1024)S(1)}, s32[16384]{0:T(1024)}, u32[]{:S(2)}) copy-start(s32[16384]{0:T(1024)} %param.7) | copy-start | bytes 196612
  2.4 0.8 %copy-start.3 = (s32[16384]{0:T(1024)S(1)}, s32[16384]{0:T(1024)}, u32[]{:S(2)}) copy-start(s32[16384]{0:T(1024)} %param.8) | copy-start | bytes 196612
  3.3 0.8 %copy-start.4 = (s32[16384]{0:T(1024)S(1)}, s32[16384]{0:T(1024)}, u32[]{:S(2)}) copy-start(s32[16384]{0:T(1024)} %param.9) | copy-start | bytes 196612
  4.1 0.8 %copy-start.5 = (f32[16384]{0:T(1024)S(1)}, f32[16384]{0:T(1024)}, u32[]{:S(2)}) copy-start(f32[16384]{0:T(1024)} %param.10) | copy-start | bytes 196612
  4.9 0.8 %copy-start.6 = (f32[16384]{0:T(1024)S(1)}, f32[16384]{0:T(1024)}, u32[]{:S(2)}) copy-start(f32[16384]{0:T(1024)} %param.11) | copy-start | bytes 196612
  10.1 11.2 %collective-permute-start = (f32[112,256]{1,0:T(8,128)S(1)}, f32[112,256]{1,0:T(8,128)S(1)}, u32[]{:S(2)}, u32[]{:S(2)}) collective-permute-start(f32[112,256]{1,0:T(8,128)S(1)} %get-tuple-element.21), channel_id=1, source_target_pairs={{0,2},{1,3},{2,0},{3,1},{4,6},{5,7},{6,4},{7,5},{8,10},{9,11},{10,... | collective-permute-start | bytes 344072 | tf_op jit(solution)/shard_map/ppermute | solution.py:37
  10.6 10.7 %collective-permute-start.1 = (f32[112,256]{1,0:T(8,128)S(1)}, f32[112,256]{1,0:T(8,128)S(1)}, u32[]{:S(2)}, u32[]{:S(2)}) collective-permute-start(f32[112,256]{1,0:T(8,128)S(1)} %get-tuple-element.22), channel_id=1, source_target_pairs={{0,30},{1,31},{2,4},{3,5},{4,2},{5,3},{6,8},{7,9},{8,6},{9,7},{10,... | collective-permute-start | bytes 344072 | tf_op jit(solution)/shard_map/ppermute | solution.py:37
  16.3 5.0 %copy-start.1 = (f32[8,32,256]{2,1,0:T(8,128)S(1)}, f32[8,32,256]{2,1,0:T(8,128)}, u32[]{:S(2)}) copy-start(f32[8,32,256]{2,1,0:T(8,128)} %cond_ref.3) | copy-start | bytes 786436
  21.4 4.6 %collective-permute-start.2 = (f32[88,256]{1,0:T(8,128)S(1)}, f32[88,256]{1,0:T(8,128)S(1)}, u32[]{:S(2)}, u32[]{:S(2)}) collective-permute-start(f32[88,256]{1,0:T(8,128)S(1)} %shard_map.89), channel_id=1, source_target_pairs={{0,1},{1,0},{2,3},{3,2},{4,5},{5,4},{6,7},{7,6},{8,9},{9,8},{10,11... | collective-permute-start | bytes 270344 | tf_op jit(solution)/shard_map/ppermute | solution.py:37
  27.8 1.3 %collective-permute-start.3 = (f32[8,8,256]{2,1,0:T(8,128)S(1)}, f32[8,8,256]{2,1,0:T(8,128)S(1)}, u32[]{:S(2)}, u32[]{:S(2)}) collective-permute-start(f32[8,8,256]{2,1,0:T(8,128)S(1)} %get-tuple-element.25), channel_id=1, source_target_pairs={{0,2},{1,3},{2,0},{3,1},{4,6},{5,7},{6,4},{7,5},{8,10},{9,11},{10,... | collective-permute-start | bytes 196616 | tf_op jit(solution)/shard_map/ppermute | solution.py:37
  27.9 6.5 %collective-permute-start.4 = (f32[8,8,256]{2,1,0:T(8,128)S(1)}, f32[8,8,256]{2,1,0:T(8,128)S(1)}, u32[]{:S(2)}, u32[]{:S(2)}) collective-permute-start(f32[8,8,256]{2,1,0:T(8,128)S(1)} %get-tuple-element.26), channel_id=1, source_target_pairs={{0,30},{1,31},{2,4},{3,5},{4,2},{5,3},{6,8},{7,9},{8,6},{9,7},{10,... | collective-permute-start | bytes 196616 | tf_op jit(solution)/shard_map/ppermute | solution.py:37
  34.4 1.7 %copy-start.7 = (f32[7]{0:T(128)S(1)}, f32[7]{0:T(128)}, u32[]{:S(2)}) copy-start(f32[7]{0:T(128)} %coupling_ref.1) | copy-start | bytes 88
  34.5 3.8 %collective-permute-start.5 = (f32[16,256]{1,0:T(8,128)S(1)}, f32[16,256]{1,0:T(8,128)S(1)}, u32[]{:S(2)}, u32[]{:S(2)}) collective-permute-start(f32[16,256]{1,0:T(8,128)S(1)} %shard_map.92), channel_id=1, source_target_pairs={{0,1},{1,0},{2,3},{3,2},{4,5},{5,4},{6,7},{7,6},{8,9},{9,8},{10,11... | collective-permute-start | bytes 49160 | tf_op jit(solution)/shard_map/ppermute | solution.py:37
  46.1 4.2 %collective-permute-start.6 = (f32[48,256]{1,0:T(8,128)S(1)}, f32[48,256]{1,0:T(8,128)S(1)}, u32[]{:S(2)}, u32[]{:S(2)}) collective-permute-start(f32[48,256]{1,0:T(8,128)S(1)} %shard_map.95), channel_id=1, source_target_pairs={{0,1},{1,0},{2,3},{3,2},{4,5},{5,4},{6,7},{7,6},{8,9},{9,8},{10,11... | collective-permute-start | bytes 147464 | tf_op jit(solution)/shard_map/ppermute | solution.py:37
  50.3 9.7 %collective-permute-start.7 = (f32[32,256]{1,0:T(8,128)S(1)}, f32[32,256]{1,0:T(8,128)S(1)}, u32[]{:S(2)}, u32[]{:S(2)}) collective-permute-start(f32[32,256]{1,0:T(8,128)S(1)} %get-tuple-element.33), channel_id=1, source_target_pairs={{0,2},{1,3},{2,0},{3,1},{4,6},{5,7},{6,4},{7,5},{8,10},{9,11},{10,... | collective-permute-start | bytes 98312 | tf_op jit(solution)/shard_map/ppermute | solution.py:37
  50.4 9.6 %collective-permute-start.8 = (f32[32,256]{1,0:T(8,128)S(1)}, f32[32,256]{1,0:T(8,128)S(1)}, u32[]{:S(2)}, u32[]{:S(2)}) collective-permute-start(f32[32,256]{1,0:T(8,128)S(1)} %get-tuple-element.34), channel_id=1, source_target_pairs={{0,30},{1,31},{2,4},{3,5},{4,2},{5,3},{6,8},{7,9},{8,6},{9,7},{10,... | collective-permute-start | bytes 98312 | tf_op jit(solution)/shard_map/ppermute | solution.py:37

commit v3 on v2

--- a/solution.py
+++ b/solution.py
@@ -180,27 +180,23 @@
     return transposed_dot(lanes(picks), lanes(marks))
 
 
-def stay_deposit_kernel(cols, field_ref, slot_ref, grid_ref, val_ref):
-    count = grid_ref.shape[0] // 2
-    size = slot_ref.shape[0]
-    stays = slot_ref[...] < 0.0
-    for f in range(4):
-        val_ref[f] = jnp.where(stays, field_ref[2 + f], 0.0)
-    grid_ref[...] = jnp.zeros_like(grid_ref)
-    step = 64
-
-    def body(j, carry):
-        base = pl.multiple_of(j * step, step)
-        lcs, rs = field_ref[0, pl.ds(base, step), :], field_ref[1, pl.ds(base, step), :]
-        rows_of = lambda x: [x[i : i + 1] for i in range(step)]
-        parts = [rows_of(val_ref[f, pl.ds(base, step), :]) for f in range(4)]
+def deposit_stays(grid_ref, field_ref, slot_ref, first, last, cols):
+    count, step = grid_ref.shape[0] // 2, 32
+    stays = slot_ref[first:last, :] < 0.0
+    vals = [jnp.where(stays, field_ref[2 + f, first:last, :], 0.0) for f in range(4)]
+    lcs, rs = field_ref[0, first:last, :], field_ref[1, first:last, :]
+    for base in range(0, last - first, step):
+        rows_of = lambda x: [x[base + i : base + i + 1] for i in range(step)]
+        parts = [rows_of(v) for v in vals]
         grid_ref[...] += deposit_block(
             rows_of(lcs), rows_of(rs), list(zip(parts[0], parts[1])),
             list(zip(parts[2], parts[3])), cols, count,
         )
-        return carry
-
-    lax.fori_loop(0, size // step, body, 0)
+
+
+def stay_deposit_kernel(cols, split, field_ref, slot_ref, grid_ref):
+    grid_ref[...] = jnp.zeros_like(grid_ref)
+    deposit_stays(grid_ref, field_ref, slot_ref, 0, split, cols)
 
 
 def deposit_groups(grid_ref, sources, cols):
@@ -217,8 +213,9 @@
     grid_ref[...] += deposit_block(lc, r, main, spill, cols, count)
 
 
-def near_deposit_kernel(cols, stay_ref, recva_ref, recvb_ref, grid_ref):
+def near_deposit_kernel(cols, split, stay_ref, recva_ref, recvb_ref, field_ref, slot_ref, grid_ref):
     grid_ref[...] = stay_ref[...]
+    deposit_stays(grid_ref, field_ref, slot_ref, split, slot_ref.shape[0], cols)
     deposit_groups(grid_ref, [(recva_ref, 0), (recvb_ref, 0)], cols)
 
 
@@ -397,25 +394,32 @@
         warmth_ref[l] = v[HALO : HALO + cols, :rows]
         for f, slope in enumerate((0.5 * (next_c(v) - prev_c(v)), 0.5 * (next_r(v) - prev_r(v)))):
             high, low = pieces(slope[HALO : HALO + cols, :rows])
-            at = f * cells + l * cols
-            slope_ref[at : at + cols, :rows] = high.astype(BF16)
-            slope_ref[at : at + cols, rows:] = low.astype(BF16)
+            for part, piece in enumerate((high, low)):
+                at = (part * 2 + f) * cells + l * cols
+                slope_ref[at : at + cols, :] = piece.astype(BF16)
 
 
 def gather_block(slope, lc, r):
-    cells = slope.shape[0] // 2
-    mark = onehot(r, slope.shape[1] // 2)
-    found = dot(slope, jnp.concatenate([mark, mark], axis=0))
+    cells = slope.shape[0] // 4
+    found = dot(slope, onehot(r, slope.shape[1]))
     here = row_iota(cells, lc.shape[1]) == lc
     return [
-        jnp.sum(jnp.where(here, found[f * cells : (f + 1) * cells], 0.0), axis=0, keepdims=True)
+        jnp.sum(
+            jnp.where(
+                here,
+                found[f * cells : (f + 1) * cells] + found[(2 + f) * cells : (3 + f) * cells],
+                0.0,
+            ),
+            axis=0,
+            keepdims=True,
+        )
         for f in range(2)
     ]
 
 
 def gather_kernel(sources, slope_ref, *refs):
     ins, out_ref = refs[:-1], refs[-1]
-    rows = slope_ref.shape[1] // 2
+    rows = slope_ref.shape[1]
     for g, (which, at) in enumerate(sources):
         for t in range(GROUP):
             code = ins[which][at + t : at + t + 1, :]
@@ -460,9 +464,9 @@
         whole = jnp.concatenate(
             [ref[(2 * at + f) * GROUP : (2 * at + f + 1) * GROUP, :] for ref, at in groups], axis=0
         )
-        high, low = pieces(whole)
-        table_ref[f * table : (f + 1) * table, :WIDE] = high
-        table_ref[f * table : (f + 1) * table, WIDE:] = low
+        for part, piece in enumerate(pieces(whole)):
+            at = (part * 2 + f) * table
+            table_ref[at : at + table, :] = piece
     source = table_ref[...].astype(BF16)
     step = 32
 
@@ -476,13 +480,12 @@
             many = lambda x: lanes([x[i + k : i + k + 1] for k in range(8)])
             at = pl.multiple_of(base * 128 + i * 128, 1024)
             mark = onehot(many(lams), WIDE)
-            found = dot(source, jnp.concatenate([mark, mark], axis=0))
+            found = dot(source, mark)
             place = many(qs)
             here = row_iota(table, 1024) == place
             for f in range(2):
-                value = jnp.sum(
-                    jnp.where(here, found[f * table : (f + 1) * table], 0.0), axis=0, keepdims=True
-                )
+                both = found[f * table : (f + 1) * table] + found[(2 + f) * table : (3 + f) * table]
+                value = jnp.sum(jnp.where(here, both, 0.0), axis=0, keepdims=True)
                 value = jnp.where(place >= 0.0, value, stay_ref[f : f + 1, pl.ds(at, 1024)])
                 out_ref[f : f + 1, pl.ds(at, 1024)] = -many(powers) * value
         return carry
@@ -516,6 +519,7 @@
     bins, layer, off = flat(cell_bin), flat(cell_layer), flat(cell_offset)
     power, spill = flat(cell_power), flat(spill_weight)
     square = bins.shape
+    split = square[0] * 3 // 4
     own = 3 * GROUP
     message = (nyc * own + layers * HALO, WIDE)
     vmem = lambda *shape: pltpu.VMEM(shape, F32)
@@ -533,14 +537,17 @@
             vmem(*square), vmem(2, layers, HALO, rows), pltpu.SemaphoreType.DMA((7,)),
             vmem(6 * groups * GROUP, WIDE),
         ],
-        bins, layer, off, power, spill, conductivity,
+        *[
+            pltpu.with_memory_space_constraint(x, pltpu.HBM)
+            for x in (bins, layer, off, power, spill, conductivity)
+        ],
         spaces={i: pltpu.HBM for i in range(6)},
     )
     recv_a, recv_b = exchange(msg_a, 1, 0), exchange(msg_b, 2, 0)
     (stay_grid,) = call(
-        partial(stay_deposit_kernel, cols),
+        partial(stay_deposit_kernel, cols, split),
         [((2 * count, rows), F32)],
-        [vmem(4, *square)],
+        [],
         fields, slot,
     )
     msg_y = call(
@@ -552,10 +559,10 @@
     )
     recv_y = [exchange(m, 0, i + 1) for i, m in enumerate(msg_y)]
     (near_grid,) = call(
-        partial(near_deposit_kernel, cols),
+        partial(near_deposit_kernel, cols, split),
         [((2 * count, rows), F32)],
         [],
-        stay_grid, recv_a, recv_b,
+        stay_grid, recv_a, recv_b, fields, slot,
     )
     edge = (layers, HALO, rows)
     grid, edge_a, edge_b = call(
@@ -579,7 +586,7 @@
     )
     final_warmth, slope = call(
         partial(solve_kernel, nyc),
-        [(tile, F32), ((2 * count, 2 * rows), BF16)],
+        [(tile, F32), ((4 * count, rows), BF16)],
         [vmem(*big), vmem(2, *big), vmem(*big)],
         grid, from_a, from_b, *faces, *from_y,
     )
@@ -610,7 +617,7 @@
     (pull,) = call(
         partial(unpack_kernel, nyc),
         [((2, cells), F32)],
-        [vmem(2 * groups * GROUP, 2 * WIDE)],
+        [vmem(4 * groups * GROUP, WIDE)],
         back_a, back_b, *back_y, stay_value, slot, power,
     )
     return final_warmth, pull

time: 64.6 us -> 57.6 us (0.89)
  local copies, waits for them, and re-layouts: 5.15 us -> 0.01 us
  waiting for transfers between devices: 8.03 us -> 5.23 us
  starting transfers between devices: 12.4 us -> 14.7 us
  Pallas kernels: 37.9 us -> 36.7 us
    unnamed x16 -> x4, local copies, waits for them, and re-layouts: 5.15 us -> 0.01 us
    ppermute x9, waiting for transfers between devices: 8.03 us -> 5.23 us  [exchange(): return lax.ppermute(value, ('gx', 'gy'), pairs)]
    ppermute x9, starting transfers between devices: 12.4 us -> 14.7 us  [exchange(): return lax.ppermute(value, ('gx', 'gy'), pairs)]
    pallas_call x13, Pallas kernels: 37.9 us -> 36.7 us  [call(): pl.pallas_call(kernel, out_shape=shapes, in_specs=specs, out_specs=[space...]
  transfers between devices with their start and end apart: 9 -> 9, of which waited for: 5 -> 4; matrix products, arithmetic and copies ran while one was open for 0% -> 0% of each run, Pallas kernels for 30% -> 33%
where the time goes in v3:
time: 57.6 us; the launch traced here: 57.4 us
  Pallas kernels  36.7 us (64%)
  starting transfers between devices  14.7 us (26%)
  waiting for transfers between devices  5.23 us (9%)
  between operations  0.77 us (1%)
    pallas_call x13, Pallas kernels, call(): pl.pallas_call(kernel, out_shape=shapes, in_specs=specs, out_specs=[space...  36.7 us
    ppermute x9, starting transfers between devices, exchange(): return lax.ppermute(value, ('gx', 'gy'), pairs)  14.7 us
    ppermute x9, waiting for transfers between devices, exchange(): return lax.ppermute(value, ('gx', 'gy'), pairs)  5.23 us
  transfers between devices with their start and end apart: 9, of which 4 were waited for; matrix products, arithmetic and copies ran while one was open for 0% of the time, Pallas kernels for 33%

profile of v3, /device:TPU:0, one launch (start us, length us, event | category | flops | bytes accessed | tf_op | source)
XLA Modules:
  0.0 57.4 jit_solution(14286799657737870699)
XLA Ops:
  0.6 4.7 %shard_map.86 = (f32[112,256]{1,0:T(8,128)S(1)}, f32[112,256]{1,0:T(8,128)S(1)}, f32[24,256]{1,0:T(8,128)S(1)}, f32[128,128]{1,0:T(8,128)S(1)}, f32[6,128,128]{2,1,0:T(8,128)S(1)}, /*index=5*/f32[128,128]{1,0:T(8,128)S(1)}) custom-call(s32[128,128]{1,0:T(8,128)} %bitcast.5, s32[128,128]{1,0:T(8,128)} %bitcast.6, s32[128,128]{1,0:T(8,128)} %bitcast.7, ...), custom_call_target="tpu_custom_call" | custom-call | tf_op jit(solution)/shard_map/pallas_call | solution.py:500
  5.3 0.5 collective-permute-start
  5.9 5.7 %collective-permute-start.1 = (f32[112,256]{1,0:T(8,128)S(1)}, f32[112,256]{1,0:T(8,128)S(1)}, u32[]{:S(2)}, u32[]{:S(2)}) collective-permute-start(f32[112,256]{1,0:T(8,128)S(1)} %get-tuple-element.22), channel_id=1, source_target_pairs={{0,30},{1,31},{2,4},{3,5},{4,2},{5,3},{6,8},{7,9},{8,6},{9,7},{10,... | collective-permute-start | bytes 344072 | tf_op jit(solution)/shard_map/ppermute | solution.py:37
  11.5 0.0 copy-start
  11.5 3.4 %shard_map.87.stay_ref.after_ref = f32[512,256]{1,0:T(8,128)S(1)} custom-call(f32[6,128,128]{2,1,0:T(8,128)S(1)} %get-tuple-element.19.field_ref, f32[128,128]{1,0:T(8,128)S(1)} %get-tuple-element.20.slot_ref.refs_2_), custom_call_target="tpu_custom_call" | custom-call | tf_op jit(solution)/shard_map/pallas_call | solution.py:500
  15.0 0.0 collective-permute-done.recva_ref.refs_0_
  15.0 0.0 collective-permute-done.1.recvb_ref.refs_1_
  15.0 0.0 copy-done
  15.0 0.1 shard_map.89
  15.1 1.6 %collective-permute-start.2 = (f32[88,256]{1,0:T(8,128)S(1)}, f32[88,256]{1,0:T(8,128)S(1)}, u32[]{:S(2)}, u32[]{:S(2)}) collective-permute-start(f32[88,256]{1,0:T(8,128)S(1)} %shard_map.89), channel_id=1, source_target_pairs={{0,1},{1,0},{2,3},{3,2},{4,5},{5,4},{6,7},{7,6},{8,9},{9,8},{10,11... | collective-permute-start | bytes 270344 | tf_op jit(solution)/shard_map/ppermute | solution.py:37
  16.8 2.4 %shard_map.88.refs_0_ = f32[512,256]{1,0:T(8,128)S(1)} custom-call(f32[512,256]{1,0:T(8,128)S(1)} %shard_map.87.stay_ref.after_ref, f32[112,256]{1,0:T(8,128)S(1)} %collective-permute-done.recva_ref.refs_0_, f32[112,256]{1,0:T(8,128)S(1)} %collective-permute-done.1.recvb_ref.refs_1_, f32[6,128,128]{2,1,0:T(8,128)S(1)} %get-tuple-element.19.field_ref, ...), custom_call_target="tpu_custom_call" | custom-call | tf_op jit(solution)/shard_map/pallas_call | solution.py:500
  19.2 0.6 collective-permute-done.2.refs_1_.refs_0_
  19.7 1.8 %shard_map.90 = (f32[8,32,256]{2,1,0:T(8,128)S(1)}, f32[8,8,256]{2,1,0:T(8,128)S(1)}, f32[8,8,256]{2,1,0:T(8,128)S(1)}) custom-call(f32[512,256]{1,0:T(8,128)S(1)} %shard_map.88.refs_0_, f32[88,256]{1,0:T(8,128)S(1)} %collective-permute-done.2.refs_1_.refs_0_), custom_call_target="tpu_custom_call" | custom-call | tf_op jit(solution)/shard_map/pallas_call | solution.py:500
  21.6 0.1 collective-permute-start.3
  21.7 2.6 %collective-permute-start.4 = (f32[8,8,256]{2,1,0:T(8,128)S(1)}, f32[8,8,256]{2,1,0:T(8,128)S(1)}, u32[]{:S(2)}, u32[]{:S(2)}) collective-permute-start(f32[8,8,256]{2,1,0:T(8,128)S(1)} %get-tuple-element.26), channel_id=1, source_target_pairs={{0,30},{1,31},{2,4},{3,5},{4,2},{5,3},{6,8},{7,9},{8,6},{9,7},{10,... | collective-permute-start | bytes 196616 | tf_op jit(solution)/shard_map/ppermute | solution.py:37
  24.3 0.0 collective-permute-done.3.froma_ref
  24.3 3.8 %collective-permute-done.4.fromb_ref = f32[8,8,256]{2,1,0:T(8,128)S(1)} collective-permute-done((f32[8,8,256]{2,1,0:T(8,128)S(1)}, f32[8,8,256]{2,1,0:T(8,128)S(1)}, u32[]{:S(2)}, u32[]{:S(2)}) %collective-permute-start.4) | collective-permute-done | bytes 65568 | tf_op jit(solution)/shard_map/ppermute | solution.py:37
  28.1 0.0 copy-start.1
  28.1 0.1 shard_map.92
  28.2 1.6 %collective-permute-start.5 = (f32[16,256]{1,0:T(8,128)S(1)}, f32[16,256]{1,0:T(8,128)S(1)}, u32[]{:S(2)}, u32[]{:S(2)}) collective-permute-start(f32[16,256]{1,0:T(8,128)S(1)} %shard_map.92), channel_id=1, source_target_pairs={{0,1},{1,0},{2,3},{3,2},{4,5},{5,4},{6,7},{7,6},{8,9},{9,8},{10,11... | collective-permute-start | bytes 49160 | tf_op jit(solution)/shard_map/ppermute | solution.py:37
  29.9 0.0 copy-done.1
  29.9 1.4 %shard_map.91 = (f32[8,48,384]{2,1,0:T(8,128)S(1)}, f32[8,48,384]{2,1,0:T(8,128)S(1)}, f32[8,48,384]{2,1,0:T(8,128)S(1)}, f32[8,48,384]{2,1,0:T(8,128)S(1)}) custom-call(f32[8,32,256]{2,1,0:T(8,128)S(1)} %copy-done, f32[112,256]{1,0:T(8,128)S(1)} %collective-permute-done.recva_ref.refs_0_, f32[112,256]{1,0:T(8,128)S(1)} %collective-permute-done.1.recvb_ref.refs_1_, ...), custom_call_target="tpu_custom_call" | custom-call | tf_op jit(solution)/shard_map/pallas_call | solution.py:500
  31.3 0.7 %collective-permute-done.5.refs_0_ = f32[16,256]{1,0:T(8,128)S(1)} collective-permute-done((f32[16,256]{1,0:T(8,128)S(1)}, f32[16,256]{1,0:T(8,128)S(1)}, u32[]{:S(2)}, u32[]{:S(2)}) %collective-permute-start.5) | collective-permute-done | bytes 16416 | tf_op jit(solution)/shard_map/ppermute | solution.py:37
  32.1 4.3 %shard_map.93 = (f32[8,32,256]{2,1,0:T(8,128)}, bf16[1024,256]{1,0:T(8,128)(2,1)S(1)}) custom-call(f32[8,32,256]{2,1,0:T(8,128)S(1)} %get-tuple-element.24.grid_ref, f32[8,8,256]{2,1,0:T(8,128)S(1)} %collective-permute-done.3.froma_ref, f32[8,8,256]{2,1,0:T(8,128)S(1)} %collective-permute-done.4.fromb_ref, f32[8,48,384]{2,1,0:T(8,128)S(1)} %get-tuple-element.27.fc_ref, ...), custom_call_target="tpu_custom_call" | custom-call | tf_op jit(solution)/shard_map/pallas_call | solution.py:500
  36.3 3.7 %shard_map.95 = f32[48,256]{1,0:T(8,128)S(1)} custom-call(bf16[1024,256]{1,0:T(8,128)(2,1)S(1)} %get-tuple-element.32.slope_ref, f32[88,256]{1,0:T(8,128)S(1)} %collective-permute-done.2.refs_1_.refs_0_), custom_call_target="tpu_custom_call" | custom-call | tf_op jit(solution)/shard_map/pallas_call | solution.py:500
  40.0 1.6 %collective-permute-start.6 = (f32[48,256]{1,0:T(8,128)S(1)}, f32[48,256]{1,0:T(8,128)S(1)}, u32[]{:S(2)}, u32[]{:S(2)}) collective-permute-start(f32[48,256]{1,0:T(8,128)S(1)} %shard_map.95), channel_id=1, source_target_pairs={{0,1},{1,0},{2,3},{3,2},{4,5},{5,4},{6,7},{7,6},{8,9},{9,8},{10,11... | collective-permute-start | bytes 147464 | tf_op jit(solution)/shard_map/ppermute | solution.py:37
  41.6 2.4 %shard_map.94.near_ref = f32[32,256]{1,0:T(8,128)S(1)} custom-call(bf16[1024,256]{1,0:T(8,128)(2,1)S(1)} %get-tuple-element.32.slope_ref, f32[112,256]{1,0:T(8,128)S(1)} %collective-permute-done.recva_ref.refs_0_, f32[112,256]{1,0:T(8,128)S(1)} %collective-permute-done.1.recvb_ref.refs_1_), custom_call_target="tpu_custom_call" | custom-call | tf_op jit(solution)/shard_map/pallas_call | solution.py:500
  44.0 0.1 collective-permute-done.6.refs_0_
  44.2 0.0 collective-permute-start.7
  44.2 0.9 %collective-permute-start.8 = (f32[32,256]{1,0:T(8,128)S(1)}, f32[32,256]{1,0:T(8,128)S(1)}, u32[]{:S(2)}, u32[]{:S(2)}) collective-permute-start(f32[32,256]{1,0:T(8,128)S(1)} %get-tuple-element.34), channel_id=1, source_target_pairs={{0,30},{1,31},{2,4},{3,5},{4,2},{5,3},{6,8},{7,9},{8,6},{9,7},{10,... | collective-permute-start | bytes 98312 | tf_op jit(solution)/shard_map/ppermute | solution.py:37
  45.0 9.4 %shard_map.97.refs_1_ = f32[2,16384]{1,0:T(2,128)S(1)} custom-call(bf16[1024,256]{1,0:T(8,128)(2,1)S(1)} %get-tuple-element.32.slope_ref, f32[6,128,128]{2,1,0:T(8,128)S(1)} %get-tuple-element.19.field_ref), custom_call_target="tpu_custom_call" | custom-call | tf_op jit(solution)/shard_map/pallas_call | solution.py:500
  54.5 0.0 collective-permute-done.7.backa_ref
  54.5 0.0 collective-permute-done.8.backb_ref
  54.5 2.9 %shard_map.98 = f32[2,16384]{1,0:T(2,128)} custom-call(f32[32,256]{1,0:T(8,128)S(1)} %collective-permute-done.7.backa_ref, f32[32,256]{1,0:T(8,128)S(1)} %collective-permute-done.8.backb_ref, f32[48,256]{1,0:T(8,128)S(1)} %collective-permute-done.6.refs_0_, f32[2,16384]{1,0:T(2,128)S(1)} %shard_map.97.refs_1_, ...), custom_call_target="tpu_custom_call" | custom-call | tf_op jit(solution)/shard_map/pallas_call | solution.py:500
  (1 shorter events, 0.0 us)
Async XLA Ops:
  5.3 9.6 %collective-permute-start = (f32[112,256]{1,0:T(8,128)S(1)}, f32[112,256]{1,0:T(8,128)S(1)}, u32[]{:S(2)}, u32[]{:S(2)}) collective-permute-start(f32[112,256]{1,0:T(8,128)S(1)} %get-tuple-element.21), channel_id=1, source_target_pairs={{0,2},{1,3},{2,0},{3,1},{4,6},{5,7},{6,4},{7,5},{8,10},{9,11},{10,... | collective-permute-start | bytes 344072 | tf_op jit(solution)/shard_map/ppermute | solution.py:37
  5.9 9.1 %collective-permute-start.1 = (f32[112,256]{1,0:T(8,128)S(1)}, f32[112,256]{1,0:T(8,128)S(1)}, u32[]{:S(2)}, u32[]{:S(2)}) collective-permute-start(f32[112,256]{1,0:T(8,128)S(1)} %get-tuple-element.22), channel_id=1, source_target_pairs={{0,30},{1,31},{2,4},{3,5},{4,2},{5,3},{6,8},{7,9},{8,6},{9,7},{10,... | collective-permute-start | bytes 344072 | tf_op jit(solution)/shard_map/ppermute | solution.py:37
  11.5 3.5 %copy-start = (f32[8,32,256]{2,1,0:T(8,128)S(1)}, f32[8,32,256]{2,1,0:T(8,128)}, u32[]{:S(2)}) copy-start(f32[8,32,256]{2,1,0:T(8,128)} %cond_ref.3) | copy-start | bytes 786436
  15.1 4.6 %collective-permute-start.2 = (f32[88,256]{1,0:T(8,128)S(1)}, f32[88,256]{1,0:T(8,128)S(1)}, u32[]{:S(2)}, u32[]{:S(2)}) collective-permute-start(f32[88,256]{1,0:T(8,128)S(1)} %shard_map.89), channel_id=1, source_target_pairs={{0,1},{1,0},{2,3},{3,2},{4,5},{5,4},{6,7},{7,6},{8,9},{9,8},{10,11... | collective-permute-start | bytes 270344 | tf_op jit(solution)/shard_map/ppermute | solution.py:37
  21.6 2.7 %collective-permute-start.3 = (f32[8,8,256]{2,1,0:T(8,128)S(1)}, f32[8,8,256]{2,1,0:T(8,128)S(1)}, u32[]{:S(2)}, u32[]{:S(2)}) collective-permute-start(f32[8,8,256]{2,1,0:T(8,128)S(1)} %get-tuple-element.25), channel_id=1, source_target_pairs={{0,2},{1,3},{2,0},{3,1},{4,6},{5,7},{6,4},{7,5},{8,10},{9,11},{10,... | collective-permute-start | bytes 196616 | tf_op jit(solution)/shard_map/ppermute | solution.py:37
  21.7 6.5 %collective-permute-start.4 = (f32[8,8,256]{2,1,0:T(8,128)S(1)}, f32[8,8,256]{2,1,0:T(8,128)S(1)}, u32[]{:S(2)}, u32[]{:S(2)}) collective-permute-start(f32[8,8,256]{2,1,0:T(8,128)S(1)} %get-tuple-element.26), channel_id=1, source_target_pairs={{0,30},{1,31},{2,4},{3,5},{4,2},{5,3},{6,8},{7,9},{8,6},{9,7},{10,... | collective-permute-start | bytes 196616 | tf_op jit(solution)/shard_map/ppermute | solution.py:37
  28.1 1.8 %copy-start.1 = (f32[7]{0:T(128)S(1)}, f32[7]{0:T(128)}, u32[]{:S(2)}) copy-start(f32[7]{0:T(128)} %coupling_ref.1) | copy-start | bytes 88
  28.2 3.8 %collective-permute-start.5 = (f32[16,256]{1,0:T(8,128)S(1)}, f32[16,256]{1,0:T(8,128)S(1)}, u32[]{:S(2)}, u32[]{:S(2)}) collective-permute-start(f32[16,256]{1,0:T(8,128)S(1)} %shard_map.92), channel_id=1, source_target_pairs={{0,1},{1,0},{2,3},{3,2},{4,5},{5,4},{6,7},{7,6},{8,9},{9,8},{10,11... | collective-permute-start | bytes 49160 | tf_op jit(solution)/shard_map/ppermute | solution.py:37
  40.0 4.2 %collective-permute-start.6 = (f32[48,256]{1,0:T(8,128)S(1)}, f32[48,256]{1,0:T(8,128)S(1)}, u32[]{:S(2)}, u32[]{:S(2)}) collective-permute-start(f32[48,256]{1,0:T(8,128)S(1)} %shard_map.95), channel_id=1, source_target_pairs={{0,1},{1,0},{2,3},{3,2},{4,5},{5,4},{6,7},{7,6},{8,9},{9,8},{10,11... | collective-permute-start | bytes 147464 | tf_op jit(solution)/shard_map/ppermute | solution.py:37
  44.2 10.3 %collective-permute-start.7 = (f32[32,256]{1,0:T(8,128)S(1)}, f32[32,256]{1,0:T(8,128)S(1)}, u32[]{:S(2)}, u32[]{:S(2)}) collective-permute-start(f32[32,256]{1,0:T(8,128)S(1)} %get-tuple-element.33), channel_id=1, source_target_pairs={{0,2},{1,3},{2,0},{3,1},{4,6},{5,7},{6,4},{7,5},{8,10},{9,11},{10,... | collective-permute-start | bytes 98312 | tf_op jit(solution)/shard_map/ppermute | solution.py:37
  44.2 10.3 %collective-permute-start.8 = (f32[32,256]{1,0:T(8,128)S(1)}, f32[32,256]{1,0:T(8,128)S(1)}, u32[]{:S(2)}, u32[]{:S(2)}) collective-permute-start(f32[32,256]{1,0:T(8,128)S(1)} %get-tuple-element.34), channel_id=1, source_target_pairs={{0,30},{1,31},{2,4},{3,5},{4,2},{5,3},{6,8},{7,9},{8,6},{9,7},{10,... | collective-permute-start | bytes 98312 | tf_op jit(solution)/shard_map/ppermute | solution.py:37

commit v4 on v3

--- a/solution.py
+++ b/solution.py
@@ -24,16 +24,21 @@
         return place
     if kind == 1:
         return place ^ 1
-    return (place - 1 if place % 2 == 0 else place + 1) % count
+    other = place - 1 if place % 2 == 0 else place + 1
+    return other if 0 <= other < count else None
 
 
 def exchange(value, x_kind, y_kind):
     nx, ny = lax.axis_size("gx"), lax.axis_size("gy")
-    pairs = [
-        (a * ny + b, partner(a, x_kind, nx) * ny + partner(b, y_kind, ny))
-        for a in range(nx)
-        for b in range(ny)
-    ]
+    pairs = []
+    for a in range(nx):
+        for b in range(ny):
+            x, y = partner(a, x_kind, nx), partner(b, y_kind, ny)
+            if x is None:
+                x, y = a, b ^ 1
+            elif y is None:
+                x, y = a ^ 1, b
+            pairs.append((a * ny + b, x * ny + y))
     return lax.ppermute(value, ("gx", "gy"), pairs)
 
 

time: 57.6 us -> 53.3 us (0.925)
  starting transfers between devices: 14.7 us -> 10.8 us
    ppermute x9, starting transfers between devices: 14.7 us -> 10.8 us  [exchange(): return lax.ppermute(value, ('gx', 'gy'), pairs)]
  transfers between devices with their start and end apart: 9 -> 9, of which waited for: 4 -> 4; matrix products, arithmetic and copies ran while one was open for 0% -> 0% of each run, Pallas kernels for 33% -> 36%
where the time goes in v4:
time: 53.3 us; the launch traced here: 53 us
  Pallas kernels  36.7 us (69%)
  starting transfers between devices  10.8 us (20%)
  waiting for transfers between devices  4.76 us (9%)
  between operations  0.77 us (1%)
    pallas_call x13, Pallas kernels, call(): pl.pallas_call(kernel, out_shape=shapes, in_specs=specs, out_specs=[space...  36.7 us
    ppermute x9, starting transfers between devices, exchange(): return lax.ppermute(value, ('gx', 'gy'), pairs)  10.8 us
    ppermute x9, waiting for transfers between devices, exchange(): return lax.ppermute(value, ('gx', 'gy'), pairs)  4.76 us
  transfers between devices with their start and end apart: 9, of which 4 were waited for; matrix products, arithmetic and copies ran while one was open for 0% of the time, Pallas kernels for 36%

profile of v4, /device:TPU:0, one launch (start us, length us, event | category | flops | bytes accessed | tf_op | source)
XLA Modules:
  0.0 53.0 jit_solution(10339133548124856497)
XLA Ops:
  0.6 4.7 %shard_map.86 = (f32[112,256]{1,0:T(8,128)S(1)}, f32[112,256]{1,0:T(8,128)S(1)}, f32[24,256]{1,0:T(8,128)S(1)}, f32[128,128]{1,0:T(8,128)S(1)}, f32[6,128,128]{2,1,0:T(8,128)S(1)}, /*index=5*/f32[128,128]{1,0:T(8,128)S(1)}) custom-call(s32[128,128]{1,0:T(8,128)} %bitcast.5, s32[128,128]{1,0:T(8,128)} %bitcast.6, s32[128,128]{1,0:T(8,128)} %bitcast.7, ...), custom_call_target="tpu_custom_call" | custom-call | tf_op jit(solution)/shard_map/pallas_call | solution.py:505
  5.3 0.5 collective-permute-start
  5.9 2.6 %collective-permute-start.1 = (f32[112,256]{1,0:T(8,128)S(1)}, f32[112,256]{1,0:T(8,128)S(1)}, u32[]{:S(2)}, u32[]{:S(2)}) collective-permute-start(f32[112,256]{1,0:T(8,128)S(1)} %get-tuple-element.22), channel_id=1, source_target_pairs={{0,1},{1,0},{2,4},{3,5},{4,2},{5,3},{6,8},{7,9},{8,6},{9,7},{10,12... | collective-permute-start | bytes 344072 | tf_op jit(solution)/shard_map/ppermute | solution.py:42
  8.4 0.0 copy-start
  8.4 3.4 %shard_map.87.stay_ref.after_ref = f32[512,256]{1,0:T(8,128)S(1)} custom-call(f32[6,128,128]{2,1,0:T(8,128)S(1)} %get-tuple-element.19.field_ref, f32[128,128]{1,0:T(8,128)S(1)} %get-tuple-element.20.slot_ref.refs_2_), custom_call_target="tpu_custom_call" | custom-call | tf_op jit(solution)/shard_map/pallas_call | solution.py:505
  11.9 0.0 collective-permute-done.recva_ref.refs_0_
  11.9 0.0 collective-permute-done.1.recvb_ref.refs_1_
  11.9 0.0 copy-done
  11.9 0.1 shard_map.89
  12.0 1.4 %collective-permute-start.2 = (f32[88,256]{1,0:T(8,128)S(1)}, f32[88,256]{1,0:T(8,128)S(1)}, u32[]{:S(2)}, u32[]{:S(2)}) collective-permute-start(f32[88,256]{1,0:T(8,128)S(1)} %shard_map.89), channel_id=1, source_target_pairs={{0,1},{1,0},{2,3},{3,2},{4,5},{5,4},{6,7},{7,6},{8,9},{9,8},{10,11... | collective-permute-start | bytes 270344 | tf_op jit(solution)/shard_map/ppermute | solution.py:42
  13.4 2.4 %shard_map.88.refs_0_ = f32[512,256]{1,0:T(8,128)S(1)} custom-call(f32[512,256]{1,0:T(8,128)S(1)} %shard_map.87.stay_ref.after_ref, f32[112,256]{1,0:T(8,128)S(1)} %collective-permute-done.recva_ref.refs_0_, f32[112,256]{1,0:T(8,128)S(1)} %collective-permute-done.1.recvb_ref.refs_1_, f32[6,128,128]{2,1,0:T(8,128)S(1)} %get-tuple-element.19.field_ref, ...), custom_call_target="tpu_custom_call" | custom-call | tf_op jit(solution)/shard_map/pallas_call | solution.py:505
  15.8 1.0 %collective-permute-done.2.refs_1_.refs_0_ = f32[88,256]{1,0:T(8,128)S(1)} collective-permute-done((f32[88,256]{1,0:T(8,128)S(1)}, f32[88,256]{1,0:T(8,128)S(1)}, u32[]{:S(2)}, u32[]{:S(2)}) %collective-permute-start.2) | collective-permute-done | bytes 90144 | tf_op jit(solution)/shard_map/ppermute | solution.py:42
  16.8 1.8 %shard_map.90 = (f32[8,32,256]{2,1,0:T(8,128)S(1)}, f32[8,8,256]{2,1,0:T(8,128)S(1)}, f32[8,8,256]{2,1,0:T(8,128)S(1)}) custom-call(f32[512,256]{1,0:T(8,128)S(1)} %shard_map.88.refs_0_, f32[88,256]{1,0:T(8,128)S(1)} %collective-permute-done.2.refs_1_.refs_0_), custom_call_target="tpu_custom_call" | custom-call | tf_op jit(solution)/shard_map/pallas_call | solution.py:505
  18.6 0.1 collective-permute-start.3
  18.7 1.6 %collective-permute-start.4 = (f32[8,8,256]{2,1,0:T(8,128)S(1)}, f32[8,8,256]{2,1,0:T(8,128)S(1)}, u32[]{:S(2)}, u32[]{:S(2)}) collective-permute-start(f32[8,8,256]{2,1,0:T(8,128)S(1)} %get-tuple-element.26), channel_id=1, source_target_pairs={{0,1},{1,0},{2,4},{3,5},{4,2},{5,3},{6,8},{7,9},{8,6},{9,7},{10,12... | collective-permute-start | bytes 196616 | tf_op jit(solution)/shard_map/ppermute | solution.py:42
  20.3 0.0 collective-permute-done.3.froma_ref
  20.3 2.8 %collective-permute-done.4.fromb_ref = f32[8,8,256]{2,1,0:T(8,128)S(1)} collective-permute-done((f32[8,8,256]{2,1,0:T(8,128)S(1)}, f32[8,8,256]{2,1,0:T(8,128)S(1)}, u32[]{:S(2)}, u32[]{:S(2)}) %collective-permute-start.4) | collective-permute-done | bytes 65568 | tf_op jit(solution)/shard_map/ppermute | solution.py:42
  23.0 0.0 copy-start.1
  23.0 0.1 shard_map.92
  23.2 1.6 %collective-permute-start.5 = (f32[16,256]{1,0:T(8,128)S(1)}, f32[16,256]{1,0:T(8,128)S(1)}, u32[]{:S(2)}, u32[]{:S(2)}) collective-permute-start(f32[16,256]{1,0:T(8,128)S(1)} %shard_map.92), channel_id=1, source_target_pairs={{0,1},{1,0},{2,3},{3,2},{4,5},{5,4},{6,7},{7,6},{8,9},{9,8},{10,11... | collective-permute-start | bytes 49160 | tf_op jit(solution)/shard_map/ppermute | solution.py:42
  24.7 0.0 copy-done.1
  24.7 1.4 %shard_map.91 = (f32[8,48,384]{2,1,0:T(8,128)S(1)}, f32[8,48,384]{2,1,0:T(8,128)S(1)}, f32[8,48,384]{2,1,0:T(8,128)S(1)}, f32[8,48,384]{2,1,0:T(8,128)S(1)}) custom-call(f32[8,32,256]{2,1,0:T(8,128)S(1)} %copy-done, f32[112,256]{1,0:T(8,128)S(1)} %collective-permute-done.recva_ref.refs_0_, f32[112,256]{1,0:T(8,128)S(1)} %collective-permute-done.1.recvb_ref.refs_1_, ...), custom_call_target="tpu_custom_call" | custom-call | tf_op jit(solution)/shard_map/pallas_call | solution.py:505
  26.2 0.8 %collective-permute-done.5.refs_0_ = f32[16,256]{1,0:T(8,128)S(1)} collective-permute-done((f32[16,256]{1,0:T(8,128)S(1)}, f32[16,256]{1,0:T(8,128)S(1)}, u32[]{:S(2)}, u32[]{:S(2)}) %collective-permute-start.5) | collective-permute-done | bytes 16416 | tf_op jit(solution)/shard_map/ppermute | solution.py:42
  27.0 4.3 %shard_map.93 = (f32[8,32,256]{2,1,0:T(8,128)}, bf16[1024,256]{1,0:T(8,128)(2,1)S(1)}) custom-call(f32[8,32,256]{2,1,0:T(8,128)S(1)} %get-tuple-element.24.grid_ref, f32[8,8,256]{2,1,0:T(8,128)S(1)} %collective-permute-done.3.froma_ref, f32[8,8,256]{2,1,0:T(8,128)S(1)} %collective-permute-done.4.fromb_ref, f32[8,48,384]{2,1,0:T(8,128)S(1)} %get-tuple-element.27.fc_ref, ...), custom_call_target="tpu_custom_call" | custom-call | tf_op jit(solution)/shard_map/pallas_call | solution.py:505
  31.2 3.7 %shard_map.95 = f32[48,256]{1,0:T(8,128)S(1)} custom-call(bf16[1024,256]{1,0:T(8,128)(2,1)S(1)} %get-tuple-element.32.slope_ref, f32[88,256]{1,0:T(8,128)S(1)} %collective-permute-done.2.refs_1_.refs_0_), custom_call_target="tpu_custom_call" | custom-call | tf_op jit(solution)/shard_map/pallas_call | solution.py:505
  34.9 1.6 %collective-permute-start.6 = (f32[48,256]{1,0:T(8,128)S(1)}, f32[48,256]{1,0:T(8,128)S(1)}, u32[]{:S(2)}, u32[]{:S(2)}) collective-permute-start(f32[48,256]{1,0:T(8,128)S(1)} %shard_map.95), channel_id=1, source_target_pairs={{0,1},{1,0},{2,3},{3,2},{4,5},{5,4},{6,7},{7,6},{8,9},{9,8},{10,11... | collective-permute-start | bytes 147464 | tf_op jit(solution)/shard_map/ppermute | solution.py:42
  36.5 2.4 %shard_map.94.near_ref = f32[32,256]{1,0:T(8,128)S(1)} custom-call(bf16[1024,256]{1,0:T(8,128)(2,1)S(1)} %get-tuple-element.32.slope_ref, f32[112,256]{1,0:T(8,128)S(1)} %collective-permute-done.recva_ref.refs_0_, f32[112,256]{1,0:T(8,128)S(1)} %collective-permute-done.1.recvb_ref.refs_1_), custom_call_target="tpu_custom_call" | custom-call | tf_op jit(solution)/shard_map/pallas_call | solution.py:505
  38.9 0.2 collective-permute-done.6.refs_0_
  39.1 0.0 collective-permute-start.7
  39.1 1.6 %collective-permute-start.8 = (f32[32,256]{1,0:T(8,128)S(1)}, f32[32,256]{1,0:T(8,128)S(1)}, u32[]{:S(2)}, u32[]{:S(2)}) collective-permute-start(f32[32,256]{1,0:T(8,128)S(1)} %get-tuple-element.34), channel_id=1, source_target_pairs={{0,1},{1,0},{2,4},{3,5},{4,2},{5,3},{6,8},{7,9},{8,6},{9,7},{10,12... | collective-permute-start | bytes 98312 | tf_op jit(solution)/shard_map/ppermute | solution.py:42
  40.7 9.4 %shard_map.97.refs_1_ = f32[2,16384]{1,0:T(2,128)S(1)} custom-call(bf16[1024,256]{1,0:T(8,128)(2,1)S(1)} %get-tuple-element.32.slope_ref, f32[6,128,128]{2,1,0:T(8,128)S(1)} %get-tuple-element.19.field_ref), custom_call_target="tpu_custom_call" | custom-call | tf_op jit(solution)/shard_map/pallas_call | solution.py:505
  50.1 0.0 collective-permute-done.7.backa_ref
  50.1 0.0 collective-permute-done.8.backb_ref
  50.1 2.9 %shard_map.98 = f32[2,16384]{1,0:T(2,128)} custom-call(f32[32,256]{1,0:T(8,128)S(1)} %collective-permute-done.7.backa_ref, f32[32,256]{1,0:T(8,128)S(1)} %collective-permute-done.8.backb_ref, f32[48,256]{1,0:T(8,128)S(1)} %collective-permute-done.6.refs_0_, f32[2,16384]{1,0:T(2,128)S(1)} %shard_map.97.refs_1_, ...), custom_call_target="tpu_custom_call" | custom-call | tf_op jit(solution)/shard_map/pallas_call | solution.py:505
  (1 shorter events, 0.0 us)
Async XLA Ops:
  5.3 6.5 %collective-permute-start = (f32[112,256]{1,0:T(8,128)S(1)}, f32[112,256]{1,0:T(8,128)S(1)}, u32[]{:S(2)}, u32[]{:S(2)}) collective-permute-start(f32[112,256]{1,0:T(8,128)S(1)} %get-tuple-element.21), channel_id=1, source_target_pairs={{0,2},{1,3},{2,0},{3,1},{4,6},{5,7},{6,4},{7,5},{8,10},{9,11},{10,... | collective-permute-start | bytes 344072 | tf_op jit(solution)/shard_map/ppermute | solution.py:42
  5.9 6.0 %collective-permute-start.1 = (f32[112,256]{1,0:T(8,128)S(1)}, f32[112,256]{1,0:T(8,128)S(1)}, u32[]{:S(2)}, u32[]{:S(2)}) collective-permute-start(f32[112,256]{1,0:T(8,128)S(1)} %get-tuple-element.22), channel_id=1, source_target_pairs={{0,1},{1,0},{2,4},{3,5},{4,2},{5,3},{6,8},{7,9},{8,6},{9,7},{10,12... | collective-permute-start | bytes 344072 | tf_op jit(solution)/shard_map/ppermute | solution.py:42
  8.4 3.5 %copy-start = (f32[8,32,256]{2,1,0:T(8,128)S(1)}, f32[8,32,256]{2,1,0:T(8,128)}, u32[]{:S(2)}) copy-start(f32[8,32,256]{2,1,0:T(8,128)} %cond_ref.3) | copy-start | bytes 786436
  12.0 4.7 %collective-permute-start.2 = (f32[88,256]{1,0:T(8,128)S(1)}, f32[88,256]{1,0:T(8,128)S(1)}, u32[]{:S(2)}, u32[]{:S(2)}) collective-permute-start(f32[88,256]{1,0:T(8,128)S(1)} %shard_map.89), channel_id=1, source_target_pairs={{0,1},{1,0},{2,3},{3,2},{4,5},{5,4},{6,7},{7,6},{8,9},{9,8},{10,11... | collective-permute-start | bytes 270344 | tf_op jit(solution)/shard_map/ppermute | solution.py:42
  18.6 1.7 %collective-permute-start.3 = (f32[8,8,256]{2,1,0:T(8,128)S(1)}, f32[8,8,256]{2,1,0:T(8,128)S(1)}, u32[]{:S(2)}, u32[]{:S(2)}) collective-permute-start(f32[8,8,256]{2,1,0:T(8,128)S(1)} %get-tuple-element.25), channel_id=1, source_target_pairs={{0,2},{1,3},{2,0},{3,1},{4,6},{5,7},{6,4},{7,5},{8,10},{9,11},{10,... | collective-permute-start | bytes 196616 | tf_op jit(solution)/shard_map/ppermute | solution.py:42
  18.7 4.3 %collective-permute-start.4 = (f32[8,8,256]{2,1,0:T(8,128)S(1)}, f32[8,8,256]{2,1,0:T(8,128)S(1)}, u32[]{:S(2)}, u32[]{:S(2)}) collective-permute-start(f32[8,8,256]{2,1,0:T(8,128)S(1)} %get-tuple-element.26), channel_id=1, source_target_pairs={{0,1},{1,0},{2,4},{3,5},{4,2},{5,3},{6,8},{7,9},{8,6},{9,7},{10,12... | collective-permute-start | bytes 196616 | tf_op jit(solution)/shard_map/ppermute | solution.py:42
  23.0 1.7 %copy-start.1 = (f32[7]{0:T(128)S(1)}, f32[7]{0:T(128)}, u32[]{:S(2)}) copy-start(f32[7]{0:T(128)} %coupling_ref.1) | copy-start | bytes 88
  23.2 3.8 %collective-permute-start.5 = (f32[16,256]{1,0:T(8,128)S(1)}, f32[16,256]{1,0:T(8,128)S(1)}, u32[]{:S(2)}, u32[]{:S(2)}) collective-permute-start(f32[16,256]{1,0:T(8,128)S(1)} %shard_map.92), channel_id=1, source_target_pairs={{0,1},{1,0},{2,3},{3,2},{4,5},{5,4},{6,7},{7,6},{8,9},{9,8},{10,11... | collective-permute-start | bytes 49160 | tf_op jit(solution)/shard_map/ppermute | solution.py:42
  34.9 4.2 %collective-permute-start.6 = (f32[48,256]{1,0:T(8,128)S(1)}, f32[48,256]{1,0:T(8,128)S(1)}, u32[]{:S(2)}, u32[]{:S(2)}) collective-permute-start(f32[48,256]{1,0:T(8,128)S(1)} %shard_map.95), channel_id=1, source_target_pairs={{0,1},{1,0},{2,3},{3,2},{4,5},{5,4},{6,7},{7,6},{8,9},{9,8},{10,11... | collective-permute-start | bytes 147464 | tf_op jit(solution)/shard_map/ppermute | solution.py:42
  39.1 11.0 %collective-permute-start.7 = (f32[32,256]{1,0:T(8,128)S(1)}, f32[32,256]{1,0:T(8,128)S(1)}, u32[]{:S(2)}, u32[]{:S(2)}) collective-permute-start(f32[32,256]{1,0:T(8,128)S(1)} %get-tuple-element.33), channel_id=1, source_target_pairs={{0,2},{1,3},{2,0},{3,1},{4,6},{5,7},{6,4},{7,5},{8,10},{9,11},{10,... | collective-permute-start | bytes 98312 | tf_op jit(solution)/shard_map/ppermute | solution.py:42
  39.1 11.0 %collective-permute-start.8 = (f32[32,256]{1,0:T(8,128)S(1)}, f32[32,256]{1,0:T(8,128)S(1)}, u32[]{:S(2)}, u32[]{:S(2)}) collective-permute-start(f32[32,256]{1,0:T(8,128)S(1)} %get-tuple-element.34), channel_id=1, source_target_pairs={{0,1},{1,0},{2,4},{3,5},{4,2},{5,3},{6,8},{7,9},{8,6},{9,7},{10,12... | collective-permute-start | bytes 98312 | tf_op jit(solution)/shard_map/ppermute | solution.py:42

commit v5 on v4

--- a/solution.py
+++ b/solution.py
@@ -15,6 +15,7 @@
 
 WIDE = 256
 GROUP = CAP // WIDE
+BLOCK = 32
 HALO = 8
 F32, BF16 = jnp.float32, jnp.bfloat16
 
@@ -292,7 +293,7 @@
     y_edges(msgy_refs, 3 * size, wide.reshape(-1, rows))
 
 
-def power_edge_kernel(grid_ref, froma_ref, fromb_ref, *edge_refs):
+def power_edge_kernel(grid_ref, froma_ref, fromb_ref, after_ref, *edge_refs):
     wide = with_columns(grid_ref[...], froma_ref[...], fromb_ref[...])
     y_edges(edge_refs, 0, wide.reshape(-1, grid_ref.shape[2]))
 
@@ -370,7 +371,7 @@
     sigma = middle / spread
     now = 1.0 / sigma
     for l in range(layers):
-        start = p_ref[l] / middle
+        start = p_ref[l] * (1.0 / middle)
         v_ref[0, l] = start
         u_ref[l] = start
     for sweep in range(ITERS):
@@ -393,61 +394,112 @@
             v_ref[new, l] = v + advance
         now = later
     final = ITERS % 2
-    cells = layers * cols
     for l in range(layers):
         v = v_ref[final, l]
         warmth_ref[l] = v[HALO : HALO + cols, :rows]
         for f, slope in enumerate((0.5 * (next_c(v) - prev_c(v)), 0.5 * (next_r(v) - prev_r(v)))):
             high, low = pieces(slope[HALO : HALO + cols, :rows])
             for part, piece in enumerate((high, low)):
-                at = (part * 2 + f) * cells + l * cols
+                at = ((l * 2 + part) * 2 + f) * cols
                 slope_ref[at : at + cols, :] = piece.astype(BF16)
 
 
-def gather_block(slope, lc, r):
-    cells = slope.shape[0] // 4
-    found = dot(slope, onehot(r, slope.shape[1]))
-    here = row_iota(cells, lc.shape[1]) == lc
+def pick(found, lc, first):
+    cols = found.shape[0] // 4
+    here = row_iota(cols, lc.shape[1]) == lc - first
     return [
-        jnp.sum(
-            jnp.where(
-                here,
-                found[f * cells : (f + 1) * cells] + found[(2 + f) * cells : (3 + f) * cells],
-                0.0,
-            ),
-            axis=0,
-            keepdims=True,
-        )
+        jnp.where(here, found[f * cols : (f + 1) * cols] + found[(2 + f) * cols : (3 + f) * cols], 0.0)
         for f in range(2)
     ]
 
 
-def gather_kernel(sources, slope_ref, *refs):
+def gather_block(slope, lc, r, layers):
+    size = slope.shape[0] // layers
+    found = dot(slope, onehot(r, slope.shape[1]))
+    parts = [pick(found[l * size : (l + 1) * size], lc, l * (size // 4)) for l in range(layers)]
+    return [jnp.sum(sum(p[f] for p in parts), axis=0, keepdims=True) for f in range(2)]
+
+
+def gather_kernel(layers, sources, slope_ref, *refs):
     ins, out_ref = refs[:-1], refs[-1]
     rows = slope_ref.shape[1]
     for g, (which, at) in enumerate(sources):
         for t in range(GROUP):
             code = ins[which][at + t : at + t + 1, :]
             lc = jnp.floor(code * (1.0 / rows))
-            for f, value in enumerate(gather_block(slope_ref[...], lc, code - lc * rows)):
+            for f, value in enumerate(gather_block(slope_ref[...], lc, code - lc * rows, layers)):
                 row = (g * 2 + f) * GROUP + t
                 out_ref[row : row + 1, :] = value
 
 
-def stay_gather_kernel(slope_ref, field_ref, out_ref):
-    step = 32
-
-    def body(j, carry):
-        base = pl.multiple_of(j * step, step)
-        lcs, rs = field_ref[0, pl.ds(base, step), :], field_ref[1, pl.ds(base, step), :]
-        for i in range(0, step, 4):
-            many = lambda x: lanes([x[i + k : i + k + 1] for k in range(4)])
-            at = pl.multiple_of(base * 128 + i * 128, 512)
-            for f, value in enumerate(gather_block(slope_ref[...], many(lcs), many(rs))):
-                out_ref[f : f + 1, pl.ds(at, 512)] = value
+def sort_kernel(layers, cols, table, field_ref, slot_ref, after_ref, order_ref, place_ref, unit_ref):
+    size = slot_ref.shape[0]
+    span = BLOCK * size // WIDE
+    r_i = lax.broadcasted_iota(jnp.int32, (size, size), 0)
+    c_i = lax.broadcasted_iota(jnp.int32, (size, size), 1)
+    flag = lambda x: jnp.where(x, 1.0, 0.0).astype(BF16)
+    upper, ones = flag(r_i < c_i), jnp.ones((size, size), BF16)
+    same = (r_i // BLOCK) == (c_i // BLOCK)
+    both = jnp.concatenate([flag(same & (r_i > c_i)), flag(same)], axis=1)
+    layer = jnp.floor(field_ref[0] * (1.0 / cols))
+    ahead = jnp.zeros((size, size), F32)
+    rank = jnp.zeros((size, size), F32)
+    lane = lax.broadcasted_iota(jnp.int32, (size, size), 1).astype(F32)
+    passed = jnp.zeros((size, size), F32)
+    for l in range(layers):
+        mine = layer == float(l)
+        mask = flag(mine)
+        totals = dot(mask, ones)
+        stack = jnp.concatenate([totals.astype(BF16), ahead.astype(BF16)], axis=0)
+        rank = jnp.where(mine, dot(mask, upper) + dot(both, stack), rank)
+        ahead = ahead + totals
+        if l + 1 < layers:
+            end = jnp.floor(dot(both[:, size:], ahead.astype(BF16)) * (1.0 / WIDE))
+            passed = passed + jnp.where(jnp.minimum(end, span - 1.0) + l < lane, 1.0, 0.0)
+    unit_ref[...] = ((lane - passed) * layers + passed).astype(jnp.int32)
+    row = jnp.floor(rank * (1.0 / WIDE))
+    lam = rank - row * WIDE
+    slot = slot_ref[...]
+    place_ref[...] = jnp.where(slot >= 0.0, slot, (row + layer + table) * WIDE + lam)
+    for k in range(size // BLOCK):
+        picks, marks = [], []
+        for i in range(k * BLOCK, (k + 1) * BLOCK):
+            hit = row_iota(span) == row[i : i + 1]
+            picks.append(
+                jnp.concatenate(
+                    [jnp.where(hit, field_ref[f, i : i + 1, :], 0.0) for f in range(2)], axis=0
+                ).astype(BF16)
+            )
+            marks.append(onehot(lam[i : i + 1], WIDE))
+        sorted_rows = transposed_dot(lanes(picks), lanes(marks))
+        for f in range(2):
+            order_ref[f, k * span : (k + 1) * span, :] = sorted_rows[f * span : (f + 1) * span]
+
+
+def units_of(layers, size):
+    return BLOCK * size // WIDE + layers
+
+
+def stay_gather_kernel(layers, slope_ref, order_ref, unit_ref, out_ref):
+    blocks = unit_ref.shape[0] // BLOCK
+    span = order_ref.shape[1] // blocks
+    size = slope_ref.shape[0] // layers
+    units = units_of(layers, unit_ref.shape[0])
+
+    def body(k, carry):
+        for u in range(units - 1):
+            code = unit_ref[k * BLOCK, u]
+            layer, at = lax.rem(code, layers), k * span + code // layers
+            lc, r = order_ref[0, pl.ds(at, 1), :], order_ref[1, pl.ds(at, 1), :]
+            rows = slope_ref[pl.ds(pl.multiple_of(layer * size, size), size), :]
+            first = (layer * (size // 4)).astype(F32)
+            for f, part in enumerate(pick(dot(rows, onehot(r, slope_ref.shape[1])), lc, first)):
+                out_ref[k, f * units + u : f * units + u + 1, :] = jnp.sum(part, axis=0, keepdims=True)
+        for f in range(2):
+            out_ref[k, (f + 1) * units - 1 : (f + 1) * units, :] = jnp.zeros((1, WIDE), F32)
         return carry
 
-    lax.fori_loop(0, field_ref.shape[1] // step, body, 0)
+    lax.fori_loop(0, blocks, body, 0)
 
 
 def reply_kernel(nyc, near_ref, *refs):
@@ -461,41 +513,42 @@
 
 
 def unpack_kernel(nyc, backa_ref, backb_ref, *refs):
-    backy, (stay_ref, slot_ref, power_ref, out_ref, table_ref) = refs[: nyc - 1], refs[nyc - 1 :]
+    backy, (stay_ref, place_ref, power_ref, out_ref, table_ref) = refs[: nyc - 1], refs[nyc - 1 :]
     groups = [(backa_ref, y) for y in range(nyc)] + [(backb_ref, y) for y in range(nyc)]
     groups += [(ref, 0) for ref in backy]
-    table = len(groups) * GROUP
+    sent, units = len(groups) * GROUP, stay_ref.shape[1] // 2
+    table = sent + units
     for f in range(2):
         whole = jnp.concatenate(
             [ref[(2 * at + f) * GROUP : (2 * at + f + 1) * GROUP, :] for ref, at in groups], axis=0
         )
         for part, piece in enumerate(pieces(whole)):
             at = (part * 2 + f) * table
-            table_ref[at : at + table, :] = piece
-    source = table_ref[...].astype(BF16)
-    step = 32
-
-    def body(j, carry):
-        base = pl.multiple_of(j * step, step)
-        slots = slot_ref[pl.ds(base, step), :]
-        qs = jnp.floor(slots * (1.0 / WIDE))
-        lams = slots - qs * WIDE
-        powers = power_ref[pl.ds(base, step), :]
-        for i in range(0, step, 8):
-            many = lambda x: lanes([x[i + k : i + k + 1] for k in range(8)])
+            table_ref[at : at + sent, :] = piece
+
+    def body(k, carry):
+        base = pl.multiple_of(k * BLOCK, BLOCK)
+        for f in range(2):
+            for part, piece in enumerate(pieces(stay_ref[k, f * units : (f + 1) * units, :])):
+                at = (part * 2 + f) * table + sent
+                table_ref[at : at + units, :] = piece
+        source = table_ref[...].astype(BF16)
+        places = place_ref[pl.ds(base, BLOCK), :]
+        qs = jnp.floor(places * (1.0 / WIDE))
+        lams = places - qs * WIDE
+        powers = power_ref[pl.ds(base, BLOCK), :]
+        for i in range(0, BLOCK, 8):
+            many = lambda x: lanes([x[i + j : i + j + 1] for j in range(8)])
             at = pl.multiple_of(base * 128 + i * 128, 1024)
-            mark = onehot(many(lams), WIDE)
-            found = dot(source, mark)
-            place = many(qs)
-            here = row_iota(table, 1024) == place
+            found = dot(source, onehot(many(lams), WIDE))
+            here = row_iota(table, 1024) == many(qs)
             for f in range(2):
                 both = found[f * table : (f + 1) * table] + found[(2 + f) * table : (3 + f) * table]
                 value = jnp.sum(jnp.where(here, both, 0.0), axis=0, keepdims=True)
-                value = jnp.where(place >= 0.0, value, stay_ref[f : f + 1, pl.ds(at, 1024)])
                 out_ref[f : f + 1, pl.ds(at, 1024)] = -many(powers) * value
         return carry
 
-    lax.fori_loop(0, slot_ref.shape[0] // step, body, 0)
+    lax.fori_loop(0, place_ref.shape[0] // BLOCK, body, 0)
 
 
 def call(kernel, outs, scratch, *args, spaces={}):
@@ -577,8 +630,20 @@
         near_grid, *recv_y,
     )
     from_a, from_b = exchange(edge_a, 1, 0), exchange(edge_b, 2, 0)
+    table = groups * GROUP
+    order, place, unit = call(
+        partial(sort_kernel, layers, cols, table),
+        [((2, cells // WIDE, WIDE), F32), (square, F32), (square, jnp.int32)],
+        [],
+        fields, slot, grid,
+        spaces={2: pl.ANY},
+    )
     edges = call(
-        power_edge_kernel, [((2 * HALO, WIDE), F32)] * (nyc - 1), [], grid, from_a, from_b
+        power_edge_kernel,
+        [((2 * HALO, WIDE), F32)] * (nyc - 1),
+        [],
+        grid, from_a, from_b, order,
+        spaces={3: pl.ANY},
     )
     from_y = [exchange(e, 0, i + 1) for i, e in enumerate(edges)]
     big = (layers, cols + 2 * HALO, rows + 128)
@@ -597,7 +662,7 @@
     )
     answer_y = [
         call(
-            partial(gather_kernel, [(0, own * i) for i in range(3)]),
+            partial(gather_kernel, layers, [(0, own * i) for i in range(3)]),
             [((6 * GROUP, WIDE), F32)],
             [],
             slope, r,
@@ -606,7 +671,7 @@
     ]
     back_y = [exchange(m, 0, i + 1) for i, m in enumerate(answer_y)]
     (near_answer,) = call(
-        partial(gather_kernel, [(0, 0), (1, 0)]),
+        partial(gather_kernel, layers, [(0, 0), (1, 0)]),
         [((4 * GROUP, WIDE), F32)],
         [],
         slope, recv_a, recv_b,
@@ -618,12 +683,19 @@
         near_answer, *back_y,
     )
     back_a, back_b = exchange(answer_a, 1, 0), exchange(answer_b, 2, 0)
-    (stay_value,) = call(stay_gather_kernel, [((2, cells), F32)], [], slope, fields)
+    units = units_of(layers, square[0])
+    (stay_value,) = call(
+        partial(stay_gather_kernel, layers),
+        [((square[0] // BLOCK, 2 * units, WIDE), F32)],
+        [],
+        slope, order, unit,
+        spaces={2: pltpu.SMEM},
+    )
     (pull,) = call(
         partial(unpack_kernel, nyc),
         [((2, cells), F32)],
-        [vmem(4 * groups * GROUP, WIDE)],
-        back_a, back_b, *back_y, stay_value, slot, power,
+        [vmem(4 * (table + units), WIDE)],
+        back_a, back_b, *back_y, stay_value, place, power,
     )
     return final_warmth, pull
 

time: 53.3 us -> 48.8 us (0.916)
  starting transfers between devices: 10.8 us -> 8.17 us
  waiting for transfers between devices: 4.76 us -> 3.8 us
  Pallas kernels: 36.7 us -> 35.9 us
    ppermute x9, starting transfers between devices: 10.8 us -> 8.17 us  [exchange(): return lax.ppermute(value, ('gx', 'gy'), pairs)]
    ppermute x9, waiting for transfers between devices: 4.76 us -> 3.8 us  [exchange(): return lax.ppermute(value, ('gx', 'gy'), pairs)]
    pallas_call x13 -> x14, Pallas kernels: 36.7 us -> 35.9 us  [call(): pl.pallas_call(kernel, out_shape=shapes, in_specs=specs, out_specs=[space...]
  transfers between devices with their start and end apart: 9 -> 9, of which waited for: 4 -> 3; matrix products, arithmetic and copies ran while one was open for 0% -> 0% of each run, Pallas kernels for 36% -> 36%
where the time goes in v5:
time: 48.8 us; the launch traced here: 48.7 us
  Pallas kernels  35.9 us (74%)
  starting transfers between devices  8.17 us (17%)
  waiting for transfers between devices  3.8 us (8%)
  between operations  0.79 us (2%)
    pallas_call x14, Pallas kernels, call(): pl.pallas_call(kernel, out_shape=shapes, in_specs=specs, out_specs=[space...  35.9 us
    ppermute x9, starting transfers between devices, exchange(): return lax.ppermute(value, ('gx', 'gy'), pairs)  8.17 us
    ppermute x9, waiting for transfers between devices, exchange(): return lax.ppermute(value, ('gx', 'gy'), pairs)  3.8 us
  transfers between devices with their start and end apart: 9, of which 3 were waited for; matrix products, arithmetic and copies ran while one was open for 0% of the time, Pallas kernels for 36%

profile of v5, /device:TPU:0, one launch (start us, length us, event | category | flops | bytes accessed | tf_op | source)
XLA Modules:
  0.0 48.7 jit_solution(6753726607796696861)
XLA Ops:
  0.6 4.7 %shard_map.86 = (f32[112,256]{1,0:T(8,128)S(1)}, f32[112,256]{1,0:T(8,128)S(1)}, f32[24,256]{1,0:T(8,128)S(1)}, f32[128,128]{1,0:T(8,128)S(1)}, f32[6,128,128]{2,1,0:T(8,128)S(1)}, /*index=5*/f32[128,128]{1,0:T(8,128)S(1)}) custom-call(s32[128,128]{1,0:T(8,128)} %bitcast.5, s32[128,128]{1,0:T(8,128)} %bitcast.6, s32[128,128]{1,0:T(8,128)} %bitcast.7, ...), custom_call_target="tpu_custom_call" | custom-call | tf_op jit(solution)/shard_map/pallas_call | solution.py:558
  5.4 0.5 %collective-permute-start = (f32[112,256]{1,0:T(8,128)S(1)}, f32[112,256]{1,0:T(8,128)S(1)}, u32[]{:S(2)}, u32[]{:S(2)}) collective-permute-start(f32[112,256]{1,0:T(8,128)S(1)} %get-tuple-element.24), channel_id=1, source_target_pairs={{0,2},{1,3},{2,0},{3,1},{4,6},{5,7},{6,4},{7,5},{8,10},{9,11},{10,... | collective-permute-start | bytes 344072 | tf_op jit(solution)/shard_map/ppermute | solution.py:43
  5.9 2.6 %collective-permute-start.1 = (f32[112,256]{1,0:T(8,128)S(1)}, f32[112,256]{1,0:T(8,128)S(1)}, u32[]{:S(2)}, u32[]{:S(2)}) collective-permute-start(f32[112,256]{1,0:T(8,128)S(1)} %get-tuple-element.25), channel_id=1, source_target_pairs={{0,1},{1,0},{2,4},{3,5},{4,2},{5,3},{6,8},{7,9},{8,6},{9,7},{10,12... | collective-permute-start | bytes 344072 | tf_op jit(solution)/shard_map/ppermute | solution.py:43
  8.5 0.0 copy-start
  8.5 3.4 %shard_map.87.stay_ref.after_ref = f32[512,256]{1,0:T(8,128)S(1)} custom-call(f32[6,128,128]{2,1,0:T(8,128)S(1)} %get-tuple-element.22.field_ref, f32[128,128]{1,0:T(8,128)S(1)} %get-tuple-element.23.slot_ref), custom_call_target="tpu_custom_call" | custom-call | tf_op jit(solution)/shard_map/pallas_call | solution.py:558
  11.9 0.0 collective-permute-done.recva_ref.refs_0_
  11.9 0.0 collective-permute-done.1.recvb_ref.refs_1_
  11.9 0.0 copy-done
  11.9 0.1 shard_map.89
  12.1 1.4 %collective-permute-start.2 = (f32[88,256]{1,0:T(8,128)S(1)}, f32[88,256]{1,0:T(8,128)S(1)}, u32[]{:S(2)}, u32[]{:S(2)}) collective-permute-start(f32[88,256]{1,0:T(8,128)S(1)} %shard_map.89), channel_id=1, source_target_pairs={{0,1},{1,0},{2,3},{3,2},{4,5},{5,4},{6,7},{7,6},{8,9},{9,8},{10,11... | collective-permute-start | bytes 270344 | tf_op jit(solution)/shard_map/ppermute | solution.py:43
  13.4 2.4 %shard_map.88.refs_0_ = f32[512,256]{1,0:T(8,128)S(1)} custom-call(f32[512,256]{1,0:T(8,128)S(1)} %shard_map.87.stay_ref.after_ref, f32[112,256]{1,0:T(8,128)S(1)} %collective-permute-done.recva_ref.refs_0_, f32[112,256]{1,0:T(8,128)S(1)} %collective-permute-done.1.recvb_ref.refs_1_, f32[6,128,128]{2,1,0:T(8,128)S(1)} %get-tuple-element.22.field_ref, ...), custom_call_target="tpu_custom_call" | custom-call | tf_op jit(solution)/shard_map/pallas_call | solution.py:558
  15.8 1.0 %collective-permute-done.2.refs_1_.refs_0_ = f32[88,256]{1,0:T(8,128)S(1)} collective-permute-done((f32[88,256]{1,0:T(8,128)S(1)}, f32[88,256]{1,0:T(8,128)S(1)}, u32[]{:S(2)}, u32[]{:S(2)}) %collective-permute-start.2) | collective-permute-done | bytes 90144 | tf_op jit(solution)/shard_map/ppermute | solution.py:43
  16.8 1.8 %shard_map.90 = (f32[8,32,256]{2,1,0:T(8,128)S(1)}, f32[8,8,256]{2,1,0:T(8,128)S(1)}, f32[8,8,256]{2,1,0:T(8,128)S(1)}) custom-call(f32[512,256]{1,0:T(8,128)S(1)} %shard_map.88.refs_0_, f32[88,256]{1,0:T(8,128)S(1)} %collective-permute-done.2.refs_1_.refs_0_), custom_call_target="tpu_custom_call" | custom-call | tf_op jit(solution)/shard_map/pallas_call | solution.py:558
  18.7 0.1 collective-permute-start.3
  18.7 1.6 %collective-permute-start.4 = (f32[8,8,256]{2,1,0:T(8,128)S(1)}, f32[8,8,256]{2,1,0:T(8,128)S(1)}, u32[]{:S(2)}, u32[]{:S(2)}) collective-permute-start(f32[8,8,256]{2,1,0:T(8,128)S(1)} %get-tuple-element.29), channel_id=1, source_target_pairs={{0,1},{1,0},{2,4},{3,5},{4,2},{5,3},{6,8},{7,9},{8,6},{9,7},{10,12... | collective-permute-start | bytes 196616 | tf_op jit(solution)/shard_map/ppermute | solution.py:43
  20.3 3.9 %shard_map.92 = (f32[2,64,256]{2,1,0:T(8,128)S(1)}, f32[128,128]{1,0:T(8,128)S(1)}, s32[128,128]{1,0:T(8,128)S(1)}) custom-call(f32[6,128,128]{2,1,0:T(8,128)S(1)} %get-tuple-element.22.field_ref, f32[128,128]{1,0:T(8,128)S(1)} %get-tuple-element.23.slot_ref, f32[8,32,256]{2,1,0:T(8,128)S(1)} %get-tuple-element.27.after_ref.grid_ref), custom_call_target="tpu_custom_call" | custom-call | tf_op jit(solution)/shard_map/pallas_call | solution.py:558
  24.2 0.0 collective-permute-done.3.froma_ref
  24.2 0.0 collective-permute-done.4.fromb_ref
  24.2 0.0 copy-start.1
  24.2 0.1 shard_map.93
  24.3 0.6 %collective-permute-start.5 = (f32[16,256]{1,0:T(8,128)S(1)}, f32[16,256]{1,0:T(8,128)S(1)}, u32[]{:S(2)}, u32[]{:S(2)}) collective-permute-start(f32[16,256]{1,0:T(8,128)S(1)} %shard_map.93), channel_id=1, source_target_pairs={{0,1},{1,0},{2,3},{3,2},{4,5},{5,4},{6,7},{7,6},{8,9},{9,8},{10,11... | collective-permute-start | bytes 49160 | tf_op jit(solution)/shard_map/ppermute | solution.py:43
  24.9 0.0 copy-done.1
  24.9 1.4 %shard_map.91 = (f32[8,48,384]{2,1,0:T(8,128)S(1)}, f32[8,48,384]{2,1,0:T(8,128)S(1)}, f32[8,48,384]{2,1,0:T(8,128)S(1)}, f32[8,48,384]{2,1,0:T(8,128)S(1)}) custom-call(f32[8,32,256]{2,1,0:T(8,128)S(1)} %copy-done, f32[112,256]{1,0:T(8,128)S(1)} %collective-permute-done.recva_ref.refs_0_, f32[112,256]{1,0:T(8,128)S(1)} %collective-permute-done.1.recvb_ref.refs_1_, ...), custom_call_target="tpu_custom_call" | custom-call | tf_op jit(solution)/shard_map/pallas_call | solution.py:558
  26.4 1.8 %collective-permute-done.5.refs_0_ = f32[16,256]{1,0:T(8,128)S(1)} collective-permute-done((f32[16,256]{1,0:T(8,128)S(1)}, f32[16,256]{1,0:T(8,128)S(1)}, u32[]{:S(2)}, u32[]{:S(2)}) %collective-permute-start.5) | collective-permute-done | bytes 16416 | tf_op jit(solution)/shard_map/ppermute | solution.py:43
  28.1 4.5 %shard_map.94 = (f32[8,32,256]{2,1,0:T(8,128)}, bf16[1024,256]{1,0:T(8,128)(2,1)S(1)}) custom-call(f32[8,32,256]{2,1,0:T(8,128)S(1)} %get-tuple-element.27.after_ref.grid_ref, f32[8,8,256]{2,1,0:T(8,128)S(1)} %collective-permute-done.3.froma_ref, f32[8,8,256]{2,1,0:T(8,128)S(1)} %collective-permute-done.4.fromb_ref, ...), custom_call_target="tpu_custom_call" | custom-call | tf_op jit(solution)/shard_map/pallas_call | solution.py:558
  32.6 3.5 %shard_map.96 = f32[48,256]{1,0:T(8,128)S(1)} custom-call(bf16[1024,256]{1,0:T(8,128)(2,1)S(1)} %get-tuple-element.36.slope_ref, f32[88,256]{1,0:T(8,128)S(1)} %collective-permute-done.2.refs_1_.refs_0_), custom_call_target="tpu_custom_call" | custom-call | tf_op jit(solution)/shard_map/pallas_call | solution.py:558
  36.0 0.7 %collective-permute-start.6 = (f32[48,256]{1,0:T(8,128)S(1)}, f32[48,256]{1,0:T(8,128)S(1)}, u32[]{:S(2)}, u32[]{:S(2)}) collective-permute-start(f32[48,256]{1,0:T(8,128)S(1)} %shard_map.96), channel_id=1, source_target_pairs={{0,1},{1,0},{2,3},{3,2},{4,5},{5,4},{6,7},{7,6},{8,9},{9,8},{10,11... | collective-permute-start | bytes 147464 | tf_op jit(solution)/shard_map/ppermute | solution.py:43
  36.8 2.4 %shard_map.95.near_ref = f32[32,256]{1,0:T(8,128)S(1)} custom-call(bf16[1024,256]{1,0:T(8,128)(2,1)S(1)} %get-tuple-element.36.slope_ref, f32[112,256]{1,0:T(8,128)S(1)} %collective-permute-done.recva_ref.refs_0_, f32[112,256]{1,0:T(8,128)S(1)} %collective-permute-done.1.recvb_ref.refs_1_), custom_call_target="tpu_custom_call" | custom-call | tf_op jit(solution)/shard_map/pallas_call | solution.py:558
  39.2 1.0 %collective-permute-done.6.refs_0_ = f32[48,256]{1,0:T(8,128)S(1)} collective-permute-done((f32[48,256]{1,0:T(8,128)S(1)}, f32[48,256]{1,0:T(8,128)S(1)}, u32[]{:S(2)}, u32[]{:S(2)}) %collective-permute-start.6) | collective-permute-done | bytes 49184 | tf_op jit(solution)/shard_map/ppermute | solution.py:43
  40.2 0.0 collective-permute-start.7
  40.2 0.7 %collective-permute-start.8 = (f32[32,256]{1,0:T(8,128)S(1)}, f32[32,256]{1,0:T(8,128)S(1)}, u32[]{:S(2)}, u32[]{:S(2)}) collective-permute-start(f32[32,256]{1,0:T(8,128)S(1)} %get-tuple-element.38), channel_id=1, source_target_pairs={{0,1},{1,0},{2,4},{3,5},{4,2},{5,3},{6,8},{7,9},{8,6},{9,7},{10,12... | collective-permute-start | bytes 98312 | tf_op jit(solution)/shard_map/ppermute | solution.py:43
  41.0 4.0 %shard_map.98.refs_1_ = f32[4,48,256]{2,1,0:T(8,128)S(1)} custom-call(bf16[1024,256]{1,0:T(8,128)(2,1)S(1)} %get-tuple-element.36.slope_ref, f32[2,64,256]{2,1,0:T(8,128)S(1)} %get-tuple-element.34.after_ref.order_ref, s32[128,128]{1,0:T(8,128)S(1)} %get-tuple-element.39.unit_ref), custom_call_target="tpu_custom_call" | custom-call | tf_op jit(solution)/shard_map/pallas_call | solution.py:558
  45.0 0.0 collective-permute-done.7.backa_ref
  45.0 0.0 collective-permute-done.8.backb_ref
  45.0 3.7 %shard_map.99 = f32[2,16384]{1,0:T(2,128)} custom-call(f32[32,256]{1,0:T(8,128)S(1)} %collective-permute-done.7.backa_ref, f32[32,256]{1,0:T(8,128)S(1)} %collective-permute-done.8.backb_ref, f32[48,256]{1,0:T(8,128)S(1)} %collective-permute-done.6.refs_0_, f32[4,48,256]{2,1,0:T(8,128)S(1)} %shard_map.98.refs_1_, f32[128,128]{1,0:T(8,128)S(1)} %get-tuple-element.40.refs_2_, ...), custom_call_target="tpu_custom_call" | custom-call | tf_op jit(solution)/shard_map/pallas_call | solution.py:558
  (1 shorter events, 0.0 us)
Async XLA Ops:
  5.4 6.5 %collective-permute-start = (f32[112,256]{1,0:T(8,128)S(1)}, f32[112,256]{1,0:T(8,128)S(1)}, u32[]{:S(2)}, u32[]{:S(2)}) collective-permute-start(f32[112,256]{1,0:T(8,128)S(1)} %get-tuple-element.24), channel_id=1, source_target_pairs={{0,2},{1,3},{2,0},{3,1},{4,6},{5,7},{6,4},{7,5},{8,10},{9,11},{10,... | collective-permute-start | bytes 344072 | tf_op jit(solution)/shard_map/ppermute | solution.py:43
  5.9 6.1 %collective-permute-start.1 = (f32[112,256]{1,0:T(8,128)S(1)}, f32[112,256]{1,0:T(8,128)S(1)}, u32[]{:S(2)}, u32[]{:S(2)}) collective-permute-start(f32[112,256]{1,0:T(8,128)S(1)} %get-tuple-element.25), channel_id=1, source_target_pairs={{0,1},{1,0},{2,4},{3,5},{4,2},{5,3},{6,8},{7,9},{8,6},{9,7},{10,12... | collective-permute-start | bytes 344072 | tf_op jit(solution)/shard_map/ppermute | solution.py:43
  8.5 3.5 %copy-start = (f32[8,32,256]{2,1,0:T(8,128)S(1)}, f32[8,32,256]{2,1,0:T(8,128)}, u32[]{:S(2)}) copy-start(f32[8,32,256]{2,1,0:T(8,128)} %cond_ref.3) | copy-start | bytes 786436
  12.1 4.7 %collective-permute-start.2 = (f32[88,256]{1,0:T(8,128)S(1)}, f32[88,256]{1,0:T(8,128)S(1)}, u32[]{:S(2)}, u32[]{:S(2)}) collective-permute-start(f32[88,256]{1,0:T(8,128)S(1)} %shard_map.89), channel_id=1, source_target_pairs={{0,1},{1,0},{2,3},{3,2},{4,5},{5,4},{6,7},{7,6},{8,9},{9,8},{10,11... | collective-permute-start | bytes 270344 | tf_op jit(solution)/shard_map/ppermute | solution.py:43
  18.7 5.5 %collective-permute-start.3 = (f32[8,8,256]{2,1,0:T(8,128)S(1)}, f32[8,8,256]{2,1,0:T(8,128)S(1)}, u32[]{:S(2)}, u32[]{:S(2)}) collective-permute-start(f32[8,8,256]{2,1,0:T(8,128)S(1)} %get-tuple-element.28), channel_id=1, source_target_pairs={{0,2},{1,3},{2,0},{3,1},{4,6},{5,7},{6,4},{7,5},{8,10},{9,11},{10,... | collective-permute-start | bytes 196616 | tf_op jit(solution)/shard_map/ppermute | solution.py:43
  18.7 5.4 %collective-permute-start.4 = (f32[8,8,256]{2,1,0:T(8,128)S(1)}, f32[8,8,256]{2,1,0:T(8,128)S(1)}, u32[]{:S(2)}, u32[]{:S(2)}) collective-permute-start(f32[8,8,256]{2,1,0:T(8,128)S(1)} %get-tuple-element.29), channel_id=1, source_target_pairs={{0,1},{1,0},{2,4},{3,5},{4,2},{5,3},{6,8},{7,9},{8,6},{9,7},{10,12... | collective-permute-start | bytes 196616 | tf_op jit(solution)/shard_map/ppermute | solution.py:43
  24.2 0.7 %copy-start.1 = (f32[7]{0:T(128)S(1)}, f32[7]{0:T(128)}, u32[]{:S(2)}) copy-start(f32[7]{0:T(128)} %coupling_ref.1) | copy-start | bytes 88
  24.3 3.8 %collective-permute-start.5 = (f32[16,256]{1,0:T(8,128)S(1)}, f32[16,256]{1,0:T(8,128)S(1)}, u32[]{:S(2)}, u32[]{:S(2)}) collective-permute-start(f32[16,256]{1,0:T(8,128)S(1)} %shard_map.93), channel_id=1, source_target_pairs={{0,1},{1,0},{2,3},{3,2},{4,5},{5,4},{6,7},{7,6},{8,9},{9,8},{10,11... | collective-permute-start | bytes 49160 | tf_op jit(solution)/shard_map/ppermute | solution.py:43
  36.0 4.2 %collective-permute-start.6 = (f32[48,256]{1,0:T(8,128)S(1)}, f32[48,256]{1,0:T(8,128)S(1)}, u32[]{:S(2)}, u32[]{:S(2)}) collective-permute-start(f32[48,256]{1,0:T(8,128)S(1)} %shard_map.96), channel_id=1, source_target_pairs={{0,1},{1,0},{2,3},{3,2},{4,5},{5,4},{6,7},{7,6},{8,9},{9,8},{10,11... | collective-permute-start | bytes 147464 | tf_op jit(solution)/shard_map/ppermute | solution.py:43
  40.2 4.8 %collective-permute-start.7 = (f32[32,256]{1,0:T(8,128)S(1)}, f32[32,256]{1,0:T(8,128)S(1)}, u32[]{:S(2)}, u32[]{:S(2)}) collective-permute-start(f32[32,256]{1,0:T(8,128)S(1)} %get-tuple-element.37), channel_id=1, source_target_pairs={{0,2},{1,3},{2,0},{3,1},{4,6},{5,7},{6,4},{7,5},{8,10},{9,11},{10,... | collective-permute-start | bytes 98312 | tf_op jit(solution)/shard_map/ppermute | solution.py:43
  40.2 4.8 %collective-permute-start.8 = (f32[32,256]{1,0:T(8,128)S(1)}, f32[32,256]{1,0:T(8,128)S(1)}, u32[]{:S(2)}, u32[]{:S(2)}) collective-permute-start(f32[32,256]{1,0:T(8,128)S(1)} %get-tuple-element.38), channel_id=1, source_target_pairs={{0,1},{1,0},{2,4},{3,5},{4,2},{5,3},{6,8},{7,9},{8,6},{9,7},{10,12... | collective-permute-start | bytes 98312 | tf_op jit(solution)/shard_map/ppermute | solution.py:43

commit v6 on v5

--- a/solution.py
+++ b/solution.py
@@ -311,17 +311,8 @@
     return jnp.concatenate([wide, tile.reshape(layers, span, 128)], axis=2)
 
 
-def shifts(span, wide_rows):
-    return (
-        lambda x: pltpu.roll(x, span - 1, 0),
-        lambda x: pltpu.roll(x, 1, 0),
-        lambda x: pltpu.roll(x, wide_rows - 1, 1),
-        lambda x: pltpu.roll(x, 1, 1),
-    )
-
-
 def face_kernel(nyc, cond_ref, recva_ref, recvb_ref, coupling_ref, *refs):
-    recvy_refs, (fc_ref, fr_ref, fl_ref, e_ref, k_ref) = refs[: nyc - 1], refs[nyc - 1 :]
+    recvy_refs, (cn_ref, cp_ref, rn_ref, rp_ref, fl_ref, d_ref, k_ref) = refs[: nyc - 1], refs[nyc - 1 :]
     layers, cols, rows = cond_ref.shape
     span, wide_rows = cols + 2 * HALO, rows + 128
     count = layers * span
@@ -344,20 +335,31 @@
     r_high = jnp.where(b < ny - 1, rows + HALO, rows)
     r_low = jnp.where(b > 0, wide_rows - HALO, wide_rows)
     inside = jnp.where((c_i >= c_low) & (c_i < c_high) & ((r_i < r_high) | (r_i >= r_low)), 1.0, 0.0)
-    next_c, prev_c, next_r, prev_r = shifts(span, wide_rows)
+    next_c = lambda x: pltpu.roll(x, span - 1, 0)
+    prev_c = lambda x: pltpu.roll(x, 1, 0)
+    next_r = lambda x: pltpu.roll(x, wide_rows - 1, 1)
+    prev_r = lambda x: pltpu.roll(x, 1, 1)
     both_c, both_r = inside * next_c(inside), inside * next_r(inside)
+    below = None
     for l in range(layers):
         k = k_ref[l]
         face_c, face_r = 0.5 * (k + next_c(k)), 0.5 * (k + next_r(k))
         kept_c, kept_r = face_c * both_c, face_r * both_r
-        fc_ref[l], fr_ref[l] = kept_c, kept_r
-        lost_c, lost_r = face_c - kept_c, face_r - kept_r
-        e_ref[l] = SINK_RATE + ((lost_c + prev_c(lost_c)) + (lost_r + prev_r(lost_r)))
+        cn_ref[l], cp_ref[l] = kept_c, prev_c(kept_c)
+        rn_ref[l], rp_ref[l] = kept_r, prev_r(kept_r)
+        total = SINK_RATE + ((face_c + prev_c(face_c)) + (face_r + prev_r(face_r)))
+        if below is not None:
+            total = total + below
         if l + 1 < layers:
-            fl_ref[l] = coupling_ref[l] * (0.5 * (k + k_ref[l + 1])) * inside
-
-
-def solve_kernel(nyc, grid_ref, froma_ref, fromb_ref, fc_ref, fr_ref, fl_ref, e_ref, *refs):
+            below = coupling_ref[l] * (0.5 * (k + k_ref[l + 1]))
+            fl_ref[l] = below * inside
+            total = total + below
+        d_ref[l] = total
+
+
+def solve_kernel(
+    nyc, grid_ref, froma_ref, fromb_ref, cn_ref, cp_ref, rn_ref, rp_ref, fl_ref, d_ref, *refs
+):
     edge_refs, (warmth_ref, slope_ref, p_ref, v_ref, u_ref) = refs[: nyc - 1], refs[nyc - 1 :]
     layers, cols, rows = grid_ref.shape
     span, wide_rows = cols + 2 * HALO, rows + 128
@@ -365,43 +367,54 @@
         with_columns(grid_ref[...], froma_ref[...], fromb_ref[...]),
         [get_edges(ref, 0, layers * span) for ref in edge_refs],
     )
-    next_c, prev_c, next_r, prev_r = shifts(span, wide_rows)
+    next_r = lambda x: pltpu.roll(x, wide_rows - 1, 1)
+    prev_r = lambda x: pltpu.roll(x, 1, 1)
     middle = 0.5 * (HIGH_BOUND + LOW_BOUND)
     spread = 0.5 * (HIGH_BOUND - LOW_BOUND)
     sigma = middle / spread
     now = 1.0 / sigma
+    blank = jnp.zeros((8, wide_rows), F32)
     for l in range(layers):
-        start = p_ref[l] * (1.0 / middle)
-        v_ref[0, l] = start
-        u_ref[l] = start
+        for side in range(2):
+            v_ref[side, l, :8, :] = blank
+            v_ref[side, l, 8 + span :, :] = blank
+        v_ref[0, l, 8 : 8 + span, :] = p_ref[l] * (1.0 / middle)
     for sweep in range(ITERS):
         later = 1.0 / (2.0 * sigma - now)
         keep, gain = later * now, 2.0 * later / spread
         old, new = sweep % 2, (sweep + 1) % 2
-        below = None
-        for l in range(layers):
-            v = v_ref[old, l]
-            flow_c = fc_ref[l] * (v - next_c(v))
-            flow_r = fr_ref[l] * (v - next_r(v))
-            result = e_ref[l] * v + (flow_c - prev_c(flow_c)) + (flow_r - prev_r(flow_r))
-            if below is not None:
-                result = result - below
-            if l + 1 < layers:
-                below = fl_ref[l] * (v - v_ref[old, l + 1])
-                result = result + below
-            advance = keep * u_ref[l] + gain * (p_ref[l] - result)
-            u_ref[l] = advance
-            v_ref[new, l] = v + advance
+        for c in range(0, span, 8):
+            at, here = slice(c, c + 8), slice(c + 8, c + 16)
+            vs = [v_ref[old, l, here, :] for l in range(layers)]
+            for l in range(layers):
+                v = vs[l]
+                rest = p_ref[l, at, :] - d_ref[l, at, :] * v
+                rest = rest + cn_ref[l, at, :] * v_ref[old, l, c + 9 : c + 17, :]
+                rest = rest + cp_ref[l, at, :] * v_ref[old, l, c + 7 : c + 15, :]
+                rest = rest + rn_ref[l, at, :] * next_r(v) + rp_ref[l, at, :] * prev_r(v)
+                if l + 1 < layers:
+                    rest = rest + fl_ref[l, at, :] * vs[l + 1]
+                if l:
+                    rest = rest + fl_ref[l - 1, at, :] * vs[l - 1]
+                advance = keep * (u_ref[l, at, :] if sweep else v) + gain * rest
+                if sweep + 1 < ITERS:
+                    u_ref[l, at, :] = advance
+                v_ref[new, l, here, :] = v + advance
         now = later
     final = ITERS % 2
     for l in range(layers):
-        v = v_ref[final, l]
-        warmth_ref[l] = v[HALO : HALO + cols, :rows]
-        for f, slope in enumerate((0.5 * (next_c(v) - prev_c(v)), 0.5 * (next_r(v) - prev_r(v)))):
-            high, low = pieces(slope[HALO : HALO + cols, :rows])
-            for part, piece in enumerate((high, low)):
-                at = ((l * 2 + part) * 2 + f) * cols
-                slope_ref[at : at + cols, :] = piece.astype(BF16)
+        warmth_ref[l] = v_ref[final, l, 8 + HALO : 8 + HALO + cols, :rows]
+        for c in range(0, cols, 16):
+            at = 8 + HALO + c
+            v = v_ref[final, l, at : at + 16, :]
+            slopes = (
+                0.5 * (v_ref[final, l, at + 1 : at + 17, :rows] - v_ref[final, l, at - 1 : at + 15, :rows]),
+                0.5 * (next_r(v) - prev_r(v))[:, :rows],
+            )
+            for f, slope in enumerate(slopes):
+                for part, piece in enumerate(pieces(slope)):
+                    put = ((l * 2 + part) * 2 + f) * cols + c
+                    slope_ref[put : put + 16, :] = piece.astype(BF16)
 
 
 def pick(found, lc, first):
@@ -649,7 +662,7 @@
     big = (layers, cols + 2 * HALO, rows + 128)
     faces = call(
         partial(face_kernel, nyc),
-        [(big, F32)] * 4,
+        [(big, F32)] * 6,
         [vmem(*big)],
         conductivity, recv_a, recv_b, layer_coupling, *recv_y,
         spaces={3: pltpu.SMEM},
@@ -657,7 +670,7 @@
     final_warmth, slope = call(
         partial(solve_kernel, nyc),
         [(tile, F32), ((4 * count, rows), BF16)],
-        [vmem(*big), vmem(2, *big), vmem(*big)],
+        [vmem(*big), vmem(2, layers, big[1] + 16, big[2]), vmem(*big)],
         grid, from_a, from_b, *faces, *from_y,
     )
     answer_y = [

time: 48.8 us -> 48 us (0.984)
  Pallas kernels: 35.9 us -> 35.2 us
    pallas_call x14, Pallas kernels: 35.9 us -> 35.2 us  [call(): pl.pallas_call(kernel, out_shape=shapes, in_specs=specs, out_specs=[space...]
  transfers between devices with their start and end apart: 9 -> 9, of which waited for: 3 -> 3; matrix products, arithmetic and copies ran while one was open for 0% -> 0% of each run, Pallas kernels for 36% -> 37%
where the time goes in v6:
time: 48 us; the launch traced here: 47.8 us
  Pallas kernels  35.2 us (73%)
  starting transfers between devices  8.2 us (17%)
  waiting for transfers between devices  3.58 us (7%)
  between operations  0.79 us (2%)
    pallas_call x14, Pallas kernels, call(): pl.pallas_call(kernel, out_shape=shapes, in_specs=specs, out_specs=[space...  35.2 us
    ppermute x9, starting transfers between devices, exchange(): return lax.ppermute(value, ('gx', 'gy'), pairs)  8.2 us
    ppermute x9, waiting for transfers between devices, exchange(): return lax.ppermute(value, ('gx', 'gy'), pairs)  3.58 us
  transfers between devices with their start and end apart: 9, of which 3 were waited for; matrix products, arithmetic and copies ran while one was open for 0% of the time, Pallas kernels for 37%

profile of v6, /device:TPU:0, one launch (start us, length us, event | category | flops | bytes accessed | tf_op | source)
XLA Modules:
  0.0 47.8 jit_solution(5600076244380935770)
XLA Ops:
  0.6 4.7 %shard_map.86 = (f32[112,256]{1,0:T(8,128)S(1)}, f32[112,256]{1,0:T(8,128)S(1)}, f32[24,256]{1,0:T(8,128)S(1)}, f32[128,128]{1,0:T(8,128)S(1)}, f32[6,128,128]{2,1,0:T(8,128)S(1)}, /*index=5*/f32[128,128]{1,0:T(8,128)S(1)}) custom-call(s32[128,128]{1,0:T(8,128)} %bitcast.5, s32[128,128]{1,0:T(8,128)} %bitcast.6, s32[128,128]{1,0:T(8,128)} %bitcast.7, ...), custom_call_target="tpu_custom_call" | custom-call | tf_op jit(solution)/shard_map/pallas_call | solution.py:571
  5.3 0.5 %collective-permute-start = (f32[112,256]{1,0:T(8,128)S(1)}, f32[112,256]{1,0:T(8,128)S(1)}, u32[]{:S(2)}, u32[]{:S(2)}) collective-permute-start(f32[112,256]{1,0:T(8,128)S(1)} %get-tuple-element.26), channel_id=1, source_target_pairs={{0,2},{1,3},{2,0},{3,1},{4,6},{5,7},{6,4},{7,5},{8,10},{9,11},{10,... | collective-permute-start | bytes 344072 | tf_op jit(solution)/shard_map/ppermute | solution.py:43
  5.9 2.6 %collective-permute-start.1 = (f32[112,256]{1,0:T(8,128)S(1)}, f32[112,256]{1,0:T(8,128)S(1)}, u32[]{:S(2)}, u32[]{:S(2)}) collective-permute-start(f32[112,256]{1,0:T(8,128)S(1)} %get-tuple-element.27), channel_id=1, source_target_pairs={{0,1},{1,0},{2,4},{3,5},{4,2},{5,3},{6,8},{7,9},{8,6},{9,7},{10,12... | collective-permute-start | bytes 344072 | tf_op jit(solution)/shard_map/ppermute | solution.py:43
  8.4 0.0 copy-start
  8.4 3.4 %shard_map.87.stay_ref.after_ref = f32[512,256]{1,0:T(8,128)S(1)} custom-call(f32[6,128,128]{2,1,0:T(8,128)S(1)} %get-tuple-element.24.field_ref, f32[128,128]{1,0:T(8,128)S(1)} %get-tuple-element.25.slot_ref), custom_call_target="tpu_custom_call" | custom-call | tf_op jit(solution)/shard_map/pallas_call | solution.py:571
  11.9 0.0 collective-permute-done.recva_ref.refs_0_
  11.9 0.0 collective-permute-done.1.recvb_ref.refs_1_
  11.9 0.0 copy-done
  11.9 0.1 shard_map.89
  12.0 1.4 %collective-permute-start.2 = (f32[88,256]{1,0:T(8,128)S(1)}, f32[88,256]{1,0:T(8,128)S(1)}, u32[]{:S(2)}, u32[]{:S(2)}) collective-permute-start(f32[88,256]{1,0:T(8,128)S(1)} %shard_map.89), channel_id=1, source_target_pairs={{0,1},{1,0},{2,3},{3,2},{4,5},{5,4},{6,7},{7,6},{8,9},{9,8},{10,11... | collective-permute-start | bytes 270344 | tf_op jit(solution)/shard_map/ppermute | solution.py:43
  13.4 2.4 %shard_map.88.refs_0_ = f32[512,256]{1,0:T(8,128)S(1)} custom-call(f32[512,256]{1,0:T(8,128)S(1)} %shard_map.87.stay_ref.after_ref, f32[112,256]{1,0:T(8,128)S(1)} %collective-permute-done.recva_ref.refs_0_, f32[112,256]{1,0:T(8,128)S(1)} %collective-permute-done.1.recvb_ref.refs_1_, f32[6,128,128]{2,1,0:T(8,128)S(1)} %get-tuple-element.24.field_ref, ...), custom_call_target="tpu_custom_call" | custom-call | tf_op jit(solution)/shard_map/pallas_call | solution.py:571
  15.8 1.0 %collective-permute-done.2.refs_1_.refs_0_ = f32[88,256]{1,0:T(8,128)S(1)} collective-permute-done((f32[88,256]{1,0:T(8,128)S(1)}, f32[88,256]{1,0:T(8,128)S(1)}, u32[]{:S(2)}, u32[]{:S(2)}) %collective-permute-start.2) | collective-permute-done | bytes 90144 | tf_op jit(solution)/shard_map/ppermute | solution.py:43
  16.8 1.8 %shard_map.90 = (f32[8,32,256]{2,1,0:T(8,128)S(1)}, f32[8,8,256]{2,1,0:T(8,128)S(1)}, f32[8,8,256]{2,1,0:T(8,128)S(1)}) custom-call(f32[512,256]{1,0:T(8,128)S(1)} %shard_map.88.refs_0_, f32[88,256]{1,0:T(8,128)S(1)} %collective-permute-done.2.refs_1_.refs_0_), custom_call_target="tpu_custom_call" | custom-call | tf_op jit(solution)/shard_map/pallas_call | solution.py:571
  18.6 0.1 collective-permute-start.3
  18.7 1.6 %collective-permute-start.4 = (f32[8,8,256]{2,1,0:T(8,128)S(1)}, f32[8,8,256]{2,1,0:T(8,128)S(1)}, u32[]{:S(2)}, u32[]{:S(2)}) collective-permute-start(f32[8,8,256]{2,1,0:T(8,128)S(1)} %get-tuple-element.31), channel_id=1, source_target_pairs={{0,1},{1,0},{2,4},{3,5},{4,2},{5,3},{6,8},{7,9},{8,6},{9,7},{10,12... | collective-permute-start | bytes 196616 | tf_op jit(solution)/shard_map/ppermute | solution.py:43
  20.3 3.9 %shard_map.92 = (f32[2,64,256]{2,1,0:T(8,128)S(1)}, f32[128,128]{1,0:T(8,128)S(1)}, s32[128,128]{1,0:T(8,128)S(1)}) custom-call(f32[6,128,128]{2,1,0:T(8,128)S(1)} %get-tuple-element.24.field_ref, f32[128,128]{1,0:T(8,128)S(1)} %get-tuple-element.25.slot_ref, f32[8,32,256]{2,1,0:T(8,128)S(1)} %get-tuple-element.29.after_ref.grid_ref), custom_call_target="tpu_custom_call" | custom-call | tf_op jit(solution)/shard_map/pallas_call | solution.py:571
  24.1 0.0 collective-permute-done.3.froma_ref
  24.1 0.0 collective-permute-done.4.fromb_ref
  24.2 0.0 copy-start.1
  24.2 0.1 shard_map.93
  24.3 0.6 %collective-permute-start.5 = (f32[16,256]{1,0:T(8,128)S(1)}, f32[16,256]{1,0:T(8,128)S(1)}, u32[]{:S(2)}, u32[]{:S(2)}) collective-permute-start(f32[16,256]{1,0:T(8,128)S(1)} %shard_map.93), channel_id=1, source_target_pairs={{0,1},{1,0},{2,3},{3,2},{4,5},{5,4},{6,7},{7,6},{8,9},{9,8},{10,11... | collective-permute-start | bytes 49160 | tf_op jit(solution)/shard_map/ppermute | solution.py:43
  24.9 0.0 copy-done.1
  24.9 1.7 %shard_map.91 = (f32[8,48,384]{2,1,0:T(8,128)S(1)}, f32[8,48,384]{2,1,0:T(8,128)S(1)}, f32[8,48,384]{2,1,0:T(8,128)S(1)}, f32[8,48,384]{2,1,0:T(8,128)S(1)}, f32...) custom-call(f32[8,32,256]{2,1,0:T(8,128)S(1)} %copy-done, f32[112,256]{1,0:T(8,128)S(1)} %collective-permute-done.recva_ref.refs_0_, ...), custom_call_target="tpu_custom_call" | custom-call | tf_op jit(solution)/shard_map/pallas_call | solution.py:571
  26.6 1.5 %collective-permute-done.5.refs_0_ = f32[16,256]{1,0:T(8,128)S(1)} collective-permute-done((f32[16,256]{1,0:T(8,128)S(1)}, f32[16,256]{1,0:T(8,128)S(1)}, u32[]{:S(2)}, u32[]{:S(2)}) %collective-permute-start.5) | collective-permute-done | bytes 16416 | tf_op jit(solution)/shard_map/ppermute | solution.py:43
  28.1 3.6 %shard_map.94 = (f32[8,32,256]{2,1,0:T(8,128)}, bf16[1024,256]{1,0:T(8,128)(2,1)S(1)}) custom-call(f32[8,32,256]{2,1,0:T(8,128)S(1)} %get-tuple-element.29.after_ref.grid_ref, f32[8,8,256]{2,1,0:T(8,128)S(1)} %collective-permute-done.3.froma_ref, f32[8,8,256]{2,1,0:T(8,128)S(1)} %collective-permute-done.4.fromb_ref, ...), custom_call_target="tpu_custom_call" | custom-call | tf_op jit(solution)/shard_map/pallas_call | solution.py:571
  31.7 3.5 %shard_map.96 = f32[48,256]{1,0:T(8,128)S(1)} custom-call(bf16[1024,256]{1,0:T(8,128)(2,1)S(1)} %get-tuple-element.40.slope_ref, f32[88,256]{1,0:T(8,128)S(1)} %collective-permute-done.2.refs_1_.refs_0_), custom_call_target="tpu_custom_call" | custom-call | tf_op jit(solution)/shard_map/pallas_call | solution.py:571
  35.1 0.8 %collective-permute-start.6 = (f32[48,256]{1,0:T(8,128)S(1)}, f32[48,256]{1,0:T(8,128)S(1)}, u32[]{:S(2)}, u32[]{:S(2)}) collective-permute-start(f32[48,256]{1,0:T(8,128)S(1)} %shard_map.96), channel_id=1, source_target_pairs={{0,1},{1,0},{2,3},{3,2},{4,5},{5,4},{6,7},{7,6},{8,9},{9,8},{10,11... | collective-permute-start | bytes 147464 | tf_op jit(solution)/shard_map/ppermute | solution.py:43
  35.9 2.4 %shard_map.95.near_ref = f32[32,256]{1,0:T(8,128)S(1)} custom-call(bf16[1024,256]{1,0:T(8,128)(2,1)S(1)} %get-tuple-element.40.slope_ref, f32[112,256]{1,0:T(8,128)S(1)} %collective-permute-done.recva_ref.refs_0_, f32[112,256]{1,0:T(8,128)S(1)} %collective-permute-done.1.recvb_ref.refs_1_), custom_call_target="tpu_custom_call" | custom-call | tf_op jit(solution)/shard_map/pallas_call | solution.py:571
  38.3 1.0 %collective-permute-done.6.refs_0_ = f32[48,256]{1,0:T(8,128)S(1)} collective-permute-done((f32[48,256]{1,0:T(8,128)S(1)}, f32[48,256]{1,0:T(8,128)S(1)}, u32[]{:S(2)}, u32[]{:S(2)}) %collective-permute-start.6) | collective-permute-done | bytes 49184 | tf_op jit(solution)/shard_map/ppermute | solution.py:43
  39.3 0.0 collective-permute-start.7
  39.3 0.8 %collective-permute-start.8 = (f32[32,256]{1,0:T(8,128)S(1)}, f32[32,256]{1,0:T(8,128)S(1)}, u32[]{:S(2)}, u32[]{:S(2)}) collective-permute-start(f32[32,256]{1,0:T(8,128)S(1)} %get-tuple-element.42), channel_id=1, source_target_pairs={{0,1},{1,0},{2,4},{3,5},{4,2},{5,3},{6,8},{7,9},{8,6},{9,7},{10,12... | collective-permute-start | bytes 98312 | tf_op jit(solution)/shard_map/ppermute | solution.py:43
  40.1 4.0 %shard_map.98.refs_1_ = f32[4,48,256]{2,1,0:T(8,128)S(1)} custom-call(bf16[1024,256]{1,0:T(8,128)(2,1)S(1)} %get-tuple-element.40.slope_ref, f32[2,64,256]{2,1,0:T(8,128)S(1)} %get-tuple-element.38.after_ref.order_ref, s32[128,128]{1,0:T(8,128)S(1)} %get-tuple-element.43.unit_ref), custom_call_target="tpu_custom_call" | custom-call | tf_op jit(solution)/shard_map/pallas_call | solution.py:571
  44.1 0.0 collective-permute-done.7.backa_ref
  44.1 0.0 collective-permute-done.8.backb_ref
  44.1 3.7 %shard_map.99 = f32[2,16384]{1,0:T(2,128)} custom-call(f32[32,256]{1,0:T(8,128)S(1)} %collective-permute-done.7.backa_ref, f32[32,256]{1,0:T(8,128)S(1)} %collective-permute-done.8.backb_ref, f32[48,256]{1,0:T(8,128)S(1)} %collective-permute-done.6.refs_0_, f32[4,48,256]{2,1,0:T(8,128)S(1)} %shard_map.98.refs_1_, f32[128,128]{1,0:T(8,128)S(1)} %get-tuple-element.44.refs_2_, ...), custom_call_target="tpu_custom_call" | custom-call | tf_op jit(solution)/shard_map/pallas_call | solution.py:571
  (1 shorter events, 0.0 us)
Async XLA Ops:
  5.3 6.5 %collective-permute-start = (f32[112,256]{1,0:T(8,128)S(1)}, f32[112,256]{1,0:T(8,128)S(1)}, u32[]{:S(2)}, u32[]{:S(2)}) collective-permute-start(f32[112,256]{1,0:T(8,128)S(1)} %get-tuple-element.26), channel_id=1, source_target_pairs={{0,2},{1,3},{2,0},{3,1},{4,6},{5,7},{6,4},{7,5},{8,10},{9,11},{10,... | collective-permute-start | bytes 344072 | tf_op jit(solution)/shard_map/ppermute | solution.py:43
  5.9 6.0 %collective-permute-start.1 = (f32[112,256]{1,0:T(8,128)S(1)}, f32[112,256]{1,0:T(8,128)S(1)}, u32[]{:S(2)}, u32[]{:S(2)}) collective-permute-start(f32[112,256]{1,0:T(8,128)S(1)} %get-tuple-element.27), channel_id=1, source_target_pairs={{0,1},{1,0},{2,4},{3,5},{4,2},{5,3},{6,8},{7,9},{8,6},{9,7},{10,12... | collective-permute-start | bytes 344072 | tf_op jit(solution)/shard_map/ppermute | solution.py:43
  8.4 3.5 %copy-start = (f32[8,32,256]{2,1,0:T(8,128)S(1)}, f32[8,32,256]{2,1,0:T(8,128)}, u32[]{:S(2)}) copy-start(f32[8,32,256]{2,1,0:T(8,128)} %cond_ref.3) | copy-start | bytes 786436
  12.0 4.7 %collective-permute-start.2 = (f32[88,256]{1,0:T(8,128)S(1)}, f32[88,256]{1,0:T(8,128)S(1)}, u32[]{:S(2)}, u32[]{:S(2)}) collective-permute-start(f32[88,256]{1,0:T(8,128)S(1)} %shard_map.89), channel_id=1, source_target_pairs={{0,1},{1,0},{2,3},{3,2},{4,5},{5,4},{6,7},{7,6},{8,9},{9,8},{10,11... | collective-permute-start | bytes 270344 | tf_op jit(solution)/shard_map/ppermute | solution.py:43
  18.6 5.5 %collective-permute-start.3 = (f32[8,8,256]{2,1,0:T(8,128)S(1)}, f32[8,8,256]{2,1,0:T(8,128)S(1)}, u32[]{:S(2)}, u32[]{:S(2)}) collective-permute-start(f32[8,8,256]{2,1,0:T(8,128)S(1)} %get-tuple-element.30), channel_id=1, source_target_pairs={{0,2},{1,3},{2,0},{3,1},{4,6},{5,7},{6,4},{7,5},{8,10},{9,11},{10,... | collective-permute-start | bytes 196616 | tf_op jit(solution)/shard_map/ppermute | solution.py:43
  18.7 5.5 %collective-permute-start.4 = (f32[8,8,256]{2,1,0:T(8,128)S(1)}, f32[8,8,256]{2,1,0:T(8,128)S(1)}, u32[]{:S(2)}, u32[]{:S(2)}) collective-permute-start(f32[8,8,256]{2,1,0:T(8,128)S(1)} %get-tuple-element.31), channel_id=1, source_target_pairs={{0,1},{1,0},{2,4},{3,5},{4,2},{5,3},{6,8},{7,9},{8,6},{9,7},{10,12... | collective-permute-start | bytes 196616 | tf_op jit(solution)/shard_map/ppermute | solution.py:43
  24.2 0.7 %copy-start.1 = (f32[7]{0:T(128)S(1)}, f32[7]{0:T(128)}, u32[]{:S(2)}) copy-start(f32[7]{0:T(128)} %coupling_ref.1) | copy-start | bytes 88
  24.3 3.8 %collective-permute-start.5 = (f32[16,256]{1,0:T(8,128)S(1)}, f32[16,256]{1,0:T(8,128)S(1)}, u32[]{:S(2)}, u32[]{:S(2)}) collective-permute-start(f32[16,256]{1,0:T(8,128)S(1)} %shard_map.93), channel_id=1, source_target_pairs={{0,1},{1,0},{2,3},{3,2},{4,5},{5,4},{6,7},{7,6},{8,9},{9,8},{10,11... | collective-permute-start | bytes 49160 | tf_op jit(solution)/shard_map/ppermute | solution.py:43
  35.1 4.2 %collective-permute-start.6 = (f32[48,256]{1,0:T(8,128)S(1)}, f32[48,256]{1,0:T(8,128)S(1)}, u32[]{:S(2)}, u32[]{:S(2)}) collective-permute-start(f32[48,256]{1,0:T(8,128)S(1)} %shard_map.96), channel_id=1, source_target_pairs={{0,1},{1,0},{2,3},{3,2},{4,5},{5,4},{6,7},{7,6},{8,9},{9,8},{10,11... | collective-permute-start | bytes 147464 | tf_op jit(solution)/shard_map/ppermute | solution.py:43
  39.3 4.8 %collective-permute-start.7 = (f32[32,256]{1,0:T(8,128)S(1)}, f32[32,256]{1,0:T(8,128)S(1)}, u32[]{:S(2)}, u32[]{:S(2)}) collective-permute-start(f32[32,256]{1,0:T(8,128)S(1)} %get-tuple-element.41), channel_id=1, source_target_pairs={{0,2},{1,3},{2,0},{3,1},{4,6},{5,7},{6,4},{7,5},{8,10},{9,11},{10,... | collective-permute-start | bytes 98312 | tf_op jit(solution)/shard_map/ppermute | solution.py:43
  39.3 4.8 %collective-permute-start.8 = (f32[32,256]{1,0:T(8,128)S(1)}, f32[32,256]{1,0:T(8,128)S(1)}, u32[]{:S(2)}, u32[]{:S(2)}) collective-permute-start(f32[32,256]{1,0:T(8,128)S(1)} %get-tuple-element.42), channel_id=1, source_target_pairs={{0,1},{1,0},{2,4},{3,5},{4,2},{5,3},{6,8},{7,9},{8,6},{9,7},{10,12... | collective-permute-start | bytes 98312 | tf_op jit(solution)/shard_map/ppermute | solution.py:43

commit v7 on v6

--- a/solution.py
+++ b/solution.py
@@ -78,7 +78,7 @@
 
 
 def pack_kernel(
-    nyc, cols, rows,
+    nyc, layers, cols, rows,
     bin_hbm, layer_hbm, off_hbm, power_hbm, spill_hbm, cond_hbm,
     msga_ref, msgb_ref, owny_ref, slot_ref, field_ref, power_ref,
     bin_ref, layer_ref, off_ref, spill_ref, edge_ref, sems, acc_ref,
@@ -88,7 +88,7 @@
         pltpu.make_async_copy(src, dst, sems.at[i])
         for i, (src, dst) in enumerate(
             [
-                (off_hbm, off_ref), (bin_hbm, bin_ref), (layer_hbm, layer_ref),
+                (off_hbm, off_ref), (layer_hbm, layer_ref), (bin_hbm, bin_ref),
                 (power_hbm, power_ref), (spill_hbm, spill_ref),
                 (cond_hbm.at[:, :HALO, :], edge_ref.at[0]),
                 (cond_hbm.at[:, cols - HALO :, :], edge_ref.at[1]),
@@ -101,27 +101,37 @@
     groups = 3 * nyc - 1
     table = groups * GROUP
     copies[0].wait()
+    copies[1].wait()
     off = off_ref[...]
     col_code = (off >= 3).astype(jnp.int32) + (off >= 6).astype(jnp.int32)
     x_kind = kind_of(col_code - 1, a)
     y_kind = kind_of(off - 3 * col_code - 1, b)
     group = jnp.where(x_kind > 0, (x_kind - 1) * nyc + y_kind, 2 * nyc - 1 + y_kind)
-    group = jnp.where(off == 4, -1, group)
+    key = jnp.where(off == 4, -1, group * layers + layer_ref[...])
     size = off.shape[0]
     r_i = lax.broadcasted_iota(jnp.int32, (size, size), 0)
     c_i = lax.broadcasted_iota(jnp.int32, (size, size), 1)
-    upper = jnp.where(r_i < c_i, 1.0, 0.0).astype(BF16)
-    lower = jnp.where(r_i > c_i, 1.0, 0.0).astype(BF16)
+    flag = lambda x: jnp.where(x, 1.0, 0.0).astype(BF16)
     ones = jnp.ones((size, size), BF16)
-    slot = jnp.full(off.shape, -1.0, F32)
+    before = jnp.concatenate([flag(r_i < c_i), ones], axis=1)
+    rank = jnp.zeros((size, size), F32)
+    counts = jnp.zeros((size, size), F32)
     for g in range(groups):
-        mine = group == g
-        mask = jnp.where(mine, 1.0, 0.0).astype(BF16)
-        totals = dot(mask, ones).astype(BF16)
-        rank = dot(mask, upper) + dot(lower, totals)
-        slot = jnp.where(mine, rank + float(g * CAP), slot)
+        keys = range(g * layers, (g + 1) * layers)
+        counted = dot(jnp.concatenate([flag(key == k) for k in keys], axis=0), before)
+        for i, k in enumerate(keys):
+            block = counted[i * size : (i + 1) * size]
+            rank = jnp.where(key == k, block[:, :size], rank)
+            counts = jnp.where(c_i == k, block[:, size:], counts)
+    narrow = counts.astype(BF16)
+    ahead = dot(narrow, flag((r_i // layers == c_i // layers) & (r_i < c_i))).astype(BF16)
+    base = dot(
+        jnp.concatenate([flag(r_i > c_i), ones], axis=1), jnp.concatenate([narrow, ahead], axis=0)
+    )
+    base = jnp.take_along_axis(base, jnp.maximum(key, 0), axis=1, mode="promise_in_bounds")
+    slot = jnp.where(key >= 0, rank + base + (group * CAP).astype(F32), -1.0)
     slot_ref[...] = slot
-    for copy in copies[1:]:
+    for copy in copies[2:]:
         copy.wait()
     code = layer_ref[...] * (cols * rows) + bin_ref[...]
     field_ref[0] = (code // rows).astype(F32)
@@ -219,7 +229,25 @@
     grid_ref[...] += deposit_block(lc, r, main, spill, cols, count)
 
 
-def near_deposit_kernel(cols, split, stay_ref, recva_ref, recvb_ref, field_ref, slot_ref, grid_ref):
+def count_units(unit_ref, sources, layers, cells):
+    unit_ref[...] = jnp.zeros_like(unit_ref)
+    lane = lax.broadcasted_iota(jnp.int32, (1, 128), 1).astype(F32)
+    for g, (ref, at) in enumerate(sources):
+        layer = jnp.floor(ref[at : at + GROUP, :] * (1.0 / cells))
+        layer = jnp.where(ref[at + GROUP : at + 2 * GROUP, :] > 0.0, layer, float(layers))
+        passed = jnp.zeros((1, 128), F32)
+        for l in range(layers - 1):
+            end = jnp.sum(jnp.where(layer <= l, 1.0, 0.0), axis=0, keepdims=True)
+            end = jnp.floor(jnp.sum(end, axis=1, keepdims=True) * (1.0 / WIDE))
+            passed = passed + jnp.where(jnp.minimum(end, GROUP - 1.0) + l < lane, 1.0, 0.0)
+        unit_ref[g : g + 1, :] = ((lane - passed) * layers + passed).astype(jnp.int32)
+
+
+def near_deposit_kernel(
+    cols, split, stay_ref, recva_ref, recvb_ref, field_ref, slot_ref, grid_ref, unit_ref
+):
+    count, rows = grid_ref.shape[0] // 2, grid_ref.shape[1]
+    count_units(unit_ref, [(recva_ref, 0), (recvb_ref, 0)], count // cols, cols * rows)
     grid_ref[...] = stay_ref[...]
     deposit_stays(grid_ref, field_ref, slot_ref, split, slot_ref.shape[0], cols)
     deposit_groups(grid_ref, [(recva_ref, 0), (recvb_ref, 0)], cols)
@@ -312,11 +340,14 @@
 
 
 def face_kernel(nyc, cond_ref, recva_ref, recvb_ref, coupling_ref, *refs):
-    recvy_refs, (cn_ref, cp_ref, rn_ref, rp_ref, fl_ref, d_ref, k_ref) = refs[: nyc - 1], refs[nyc - 1 :]
+    recvy_refs = refs[: nyc - 1]
+    cn_ref, cp_ref, rn_ref, rp_ref, fl_ref, d_ref, unit_ref, k_ref = refs[nyc - 1 :]
     layers, cols, rows = cond_ref.shape
     span, wide_rows = cols + 2 * HALO, rows + 128
     count = layers * span
     top = nyc * 3 * GROUP
+    sources = [(ref, 3 * GROUP * i) for ref in recvy_refs for i in range(3)]
+    count_units(unit_ref, sources, layers, cols * rows)
     a, b = lax.axis_index("gx"), lax.axis_index("gy")
     nx, ny = lax.axis_size("gx"), lax.axis_size("gy")
     k_ref[...] = with_rows(
@@ -426,23 +457,30 @@
     ]
 
 
-def gather_block(slope, lc, r, layers):
-    size = slope.shape[0] // layers
-    found = dot(slope, onehot(r, slope.shape[1]))
-    parts = [pick(found[l * size : (l + 1) * size], lc, l * (size // 4)) for l in range(layers)]
-    return [jnp.sum(sum(p[f] for p in parts), axis=0, keepdims=True) for f in range(2)]
-
-
-def gather_kernel(layers, sources, slope_ref, *refs):
+def gather_unit(layers, slope_ref, code, lc, r):
+    size = slope_ref.shape[0] // layers
+    layer = lax.rem(code, layers)
+    rows = slope_ref[pl.ds(pl.multiple_of(layer * size, size), size), :]
+    found = dot(rows, onehot(r, slope_ref.shape[1]))
+    first = (layer * (size // 4)).astype(F32)
+    return [jnp.sum(part, axis=0, keepdims=True) for part in pick(found, lc, first)]
+
+
+def gather_kernel(layers, sources, slope_ref, unit_ref, *refs):
     ins, out_ref = refs[:-1], refs[-1]
     rows = slope_ref.shape[1]
-    for g, (which, at) in enumerate(sources):
-        for t in range(GROUP):
-            code = ins[which][at + t : at + t + 1, :]
-            lc = jnp.floor(code * (1.0 / rows))
-            for f, value in enumerate(gather_block(slope_ref[...], lc, code - lc * rows, layers)):
-                row = (g * 2 + f) * GROUP + t
-                out_ref[row : row + 1, :] = value
+    for g, (which, at, line) in enumerate(sources):
+        totals = [jnp.zeros((GROUP, WIDE), F32)] * 2
+        for u in range(GROUP + layers - 1):
+            code = unit_ref[line, u]
+            row = lax.div(code, layers)
+            slots = ins[which][pl.ds(at + row, 1), :]
+            lc = jnp.floor(slots * (1.0 / rows))
+            hit = row_iota(GROUP, WIDE) == row.astype(F32)
+            for f, value in enumerate(gather_unit(layers, slope_ref, code, lc, slots - lc * rows)):
+                totals[f] = totals[f] + jnp.where(hit, value, 0.0)
+        for f in range(2):
+            out_ref[(g * 2 + f) * GROUP : (g * 2 + f + 1) * GROUP, :] = totals[f]
 
 
 def sort_kernel(layers, cols, table, field_ref, slot_ref, after_ref, order_ref, place_ref, unit_ref):
@@ -469,7 +507,9 @@
         if l + 1 < layers:
             end = jnp.floor(dot(both[:, size:], ahead.astype(BF16)) * (1.0 / WIDE))
             passed = passed + jnp.where(jnp.minimum(end, span - 1.0) + l < lane, 1.0, 0.0)
-    unit_ref[...] = ((lane - passed) * layers + passed).astype(jnp.int32)
+    unit = ((lane - passed) * layers + passed).astype(jnp.int32)
+    for k in range(size // BLOCK):
+        unit_ref[k : k + 1, :] = unit[k * BLOCK : k * BLOCK + 1]
     row = jnp.floor(rank * (1.0 / WIDE))
     lam = rank - row * WIDE
     slot = slot_ref[...]
@@ -489,33 +529,26 @@
             order_ref[f, k * span : (k + 1) * span, :] = sorted_rows[f * span : (f + 1) * span]
 
 
-def units_of(layers, size):
-    return BLOCK * size // WIDE + layers
-
-
-def stay_gather_kernel(layers, slope_ref, order_ref, unit_ref, out_ref):
-    blocks = unit_ref.shape[0] // BLOCK
-    span = order_ref.shape[1] // blocks
-    size = slope_ref.shape[0] // layers
-    units = units_of(layers, unit_ref.shape[0])
-
-    def body(k, carry):
+def stay_gather_kernel(layers, start, slope_ref, order_ref, unit_ref, out_ref):
+    span = order_ref.shape[1] // unit_ref.shape[0]
+    units = span + layers
+
+    def body(j, carry):
+        k = j + start
         for u in range(units - 1):
-            code = unit_ref[k * BLOCK, u]
-            layer, at = lax.rem(code, layers), k * span + code // layers
+            code = unit_ref[k, u]
+            at = k * span + lax.div(code, layers)
             lc, r = order_ref[0, pl.ds(at, 1), :], order_ref[1, pl.ds(at, 1), :]
-            rows = slope_ref[pl.ds(pl.multiple_of(layer * size, size), size), :]
-            first = (layer * (size // 4)).astype(F32)
-            for f, part in enumerate(pick(dot(rows, onehot(r, slope_ref.shape[1])), lc, first)):
-                out_ref[k, f * units + u : f * units + u + 1, :] = jnp.sum(part, axis=0, keepdims=True)
+            for f, value in enumerate(gather_unit(layers, slope_ref, code, lc, r)):
+                out_ref[j, f * units + u : f * units + u + 1, :] = value
         for f in range(2):
-            out_ref[k, (f + 1) * units - 1 : (f + 1) * units, :] = jnp.zeros((1, WIDE), F32)
+            out_ref[j, (f + 1) * units - 1 : (f + 1) * units, :] = jnp.zeros((1, WIDE), F32)
         return carry
 
-    lax.fori_loop(0, blocks, body, 0)
-
-
-def reply_kernel(nyc, near_ref, *refs):
+    lax.fori_loop(0, out_ref.shape[0], body, 0)
+
+
+def reply_kernel(nyc, near_ref, after_ref, *refs):
     size = 2 * GROUP
     backs, (a_ref, b_ref) = refs[: nyc - 1], refs[nyc - 1 :]
     a_ref[:size, :] = near_ref[:size, :]
@@ -526,10 +559,11 @@
 
 
 def unpack_kernel(nyc, backa_ref, backb_ref, *refs):
-    backy, (stay_ref, place_ref, power_ref, out_ref, table_ref) = refs[: nyc - 1], refs[nyc - 1 :]
+    backy = refs[: nyc - 1]
+    early_ref, late_ref, place_ref, power_ref, out_ref, table_ref = refs[nyc - 1 :]
     groups = [(backa_ref, y) for y in range(nyc)] + [(backb_ref, y) for y in range(nyc)]
     groups += [(ref, 0) for ref in backy]
-    sent, units = len(groups) * GROUP, stay_ref.shape[1] // 2
+    sent, units = len(groups) * GROUP, early_ref.shape[1] // 2
     table = sent + units
     for f in range(2):
         whole = jnp.concatenate(
@@ -539,8 +573,8 @@
             at = (part * 2 + f) * table
             table_ref[at : at + sent, :] = piece
 
-    def body(k, carry):
-        base = pl.multiple_of(k * BLOCK, BLOCK)
+    def body(stay_ref, start, k, carry):
+        base = pl.multiple_of((k + start) * BLOCK, BLOCK)
         for f in range(2):
             for part, piece in enumerate(pieces(stay_ref[k, f * units : (f + 1) * units, :])):
                 at = (part * 2 + f) * table + sent
@@ -561,7 +595,9 @@
                 out_ref[f : f + 1, pl.ds(at, 1024)] = -many(powers) * value
         return carry
 
-    lax.fori_loop(0, place_ref.shape[0] // BLOCK, body, 0)
+    early = early_ref.shape[0]
+    lax.fori_loop(0, early, functools.partial(body, early_ref, 0), 0)
+    lax.fori_loop(0, late_ref.shape[0], functools.partial(body, late_ref, early), 0)
 
 
 def call(kernel, outs, scratch, *args, spaces={}):
@@ -598,7 +634,7 @@
 
     tile = conductivity.shape
     msg_a, msg_b, own_y, slot, fields, power = call(
-        partial(pack_kernel, nyc, cols, rows),
+        partial(pack_kernel, nyc, layers, cols, rows),
         [
             (message, F32), (message, F32), (((nyc - 1) * own, WIDE), F32),
             (square, F32), ((6, *square), F32), (square, F32),
@@ -629,9 +665,9 @@
         spaces={4: pl.ANY},
     )
     recv_y = [exchange(m, 0, i + 1) for i, m in enumerate(msg_y)]
-    (near_grid,) = call(
+    near_grid, near_unit = call(
         partial(near_deposit_kernel, cols, split),
-        [((2 * count, rows), F32)],
+        [((2 * count, rows), F32), ((8, 128), jnp.int32)],
         [],
         stay_grid, recv_a, recv_b, fields, slot,
     )
@@ -646,7 +682,7 @@
     table = groups * GROUP
     order, place, unit = call(
         partial(sort_kernel, layers, cols, table),
-        [((2, cells // WIDE, WIDE), F32), (square, F32), (square, jnp.int32)],
+        [((2, cells // WIDE, WIDE), F32), (square, F32), ((square[0] // BLOCK, 128), jnp.int32)],
         [],
         fields, slot, grid,
         spaces={2: pl.ANY},
@@ -660,9 +696,9 @@
     )
     from_y = [exchange(e, 0, i + 1) for i, e in enumerate(edges)]
     big = (layers, cols + 2 * HALO, rows + 128)
-    faces = call(
+    *faces, far_unit = call(
         partial(face_kernel, nyc),
-        [(big, F32)] * 6,
+        [(big, F32)] * 6 + [((8, 128), jnp.int32)],
         [vmem(*big)],
         conductivity, recv_a, recv_b, layer_coupling, *recv_y,
         spaces={3: pltpu.SMEM},
@@ -675,40 +711,50 @@
     )
     answer_y = [
         call(
-            partial(gather_kernel, layers, [(0, own * i) for i in range(3)]),
+            partial(gather_kernel, layers, [(0, own * i, 3 * y + i) for i in range(3)]),
             [((6 * GROUP, WIDE), F32)],
             [],
-            slope, r,
+            slope, far_unit, r,
+            spaces={1: pltpu.SMEM},
         )[0]
-        for r in recv_y
+        for y, r in enumerate(recv_y)
     ]
     back_y = [exchange(m, 0, i + 1) for i, m in enumerate(answer_y)]
     (near_answer,) = call(
-        partial(gather_kernel, layers, [(0, 0), (1, 0)]),
+        partial(gather_kernel, layers, [(0, 0, 0), (1, 0, 1)]),
         [((4 * GROUP, WIDE), F32)],
         [],
-        slope, recv_a, recv_b,
-    )
+        slope, near_unit, recv_a, recv_b,
+        spaces={1: pltpu.SMEM},
+    )
+    blocks, early = square[0] // BLOCK, 1
+    units = order.shape[1] // blocks + layers
+    stay_values = [
+        functools.partial(
+            call,
+            partial(stay_gather_kernel, layers, start),
+            [((size, 2 * units, WIDE), F32)],
+            [],
+            slope, order, unit,
+            spaces={2: pltpu.SMEM},
+        )
+        for start, size in ((0, early), (early, blocks - early))
+    ]
+    (early_value,) = stay_values[0]()
     answer_a, answer_b = call(
         partial(reply_kernel, nyc),
         [((2 * nyc * GROUP, WIDE), F32)] * 2,
         [],
-        near_answer, *back_y,
+        near_answer, early_value, *back_y,
+        spaces={1: pl.ANY},
     )
     back_a, back_b = exchange(answer_a, 1, 0), exchange(answer_b, 2, 0)
-    units = units_of(layers, square[0])
-    (stay_value,) = call(
-        partial(stay_gather_kernel, layers),
-        [((square[0] // BLOCK, 2 * units, WIDE), F32)],
-        [],
-        slope, order, unit,
-        spaces={2: pltpu.SMEM},
-    )
+    (late_value,) = stay_values[1]()
     (pull,) = call(
         partial(unpack_kernel, nyc),
         [((2, cells), F32)],
         [vmem(4 * (table + units), WIDE)],
-        back_a, back_b, *back_y, stay_value, place, power,
+        back_a, back_b, *back_y, early_value, late_value, place, power,
     )
     return final_warmth, pull
 

time: 48 us -> 45.9 us (0.956)
  Pallas kernels: 35.2 us -> 32.6 us
  waiting for transfers between devices: 3.58 us -> 4.21 us
    pallas_call x14 -> x15, Pallas kernels: 35.2 us -> 32.6 us  [call(): pl.pallas_call(kernel, out_shape=shapes, in_specs=specs, out_specs=[space...]
    ppermute x9, waiting for transfers between devices: 3.58 us -> 4.21 us  [exchange(): return lax.ppermute(value, ('gx', 'gy'), pairs)]
  transfers between devices with their start and end apart: 9 -> 9, of which waited for: 3 -> 4; matrix products, arithmetic and copies ran while one was open for 0% -> 0% of each run, Pallas kernels for 37% -> 35%
where the time goes in v7:
time: 45.9 us; the launch traced here: 45.8 us
  Pallas kernels  32.6 us (71%)
  starting transfers between devices  8.17 us (18%)
  waiting for transfers between devices  4.21 us (9%)
  between operations  0.8 us (2%)
    pallas_call x15, Pallas kernels, call(): pl.pallas_call(kernel, out_shape=shapes, in_specs=specs, out_specs=[space...  32.6 us
    ppermute x9, starting transfers between devices, exchange(): return lax.ppermute(value, ('gx', 'gy'), pairs)  8.17 us
    ppermute x9, waiting for transfers between devices, exchange(): return lax.ppermute(value, ('gx', 'gy'), pairs)  4.21 us
  transfers between devices with their start and end apart: 9, of which 4 were waited for; matrix products, arithmetic and copies ran while one was open for 0% of the time, Pallas kernels for 35%

profile of v7, /device:TPU:0, one launch (start us, length us, event | category | flops | bytes accessed | tf_op | source)
XLA Modules:
  0.0 45.8 jit_solution(1594057768578751814)
XLA Ops:
  0.6 5.3 %shard_map.86 = (f32[112,256]{1,0:T(8,128)S(1)}, f32[112,256]{1,0:T(8,128)S(1)}, f32[24,256]{1,0:T(8,128)S(1)}, f32[128,128]{1,0:T(8,128)S(1)}, f32[6,128,128]{2,1,0:T(8,128)S(1)}, /*index=5*/f32[128,128]{1,0:T(8,128)S(1)}) custom-call(s32[128,128]{1,0:T(8,128)} %bitcast.5, s32[128,128]{1,0:T(8,128)} %bitcast.6, s32[128,128]{1,0:T(8,128)} %bitcast.7, ...), custom_call_target="tpu_custom_call" | custom-call | tf_op jit(solution)/shard_map/pallas_call | solution.py:607
  6.0 0.5 %collective-permute-start = (f32[112,256]{1,0:T(8,128)S(1)}, f32[112,256]{1,0:T(8,128)S(1)}, u32[]{:S(2)}, u32[]{:S(2)}) collective-permute-start(f32[112,256]{1,0:T(8,128)S(1)} %get-tuple-element.29), channel_id=1, source_target_pairs={{0,2},{1,3},{2,0},{3,1},{4,6},{5,7},{6,4},{7,5},{8,10},{9,11},{10,... | collective-permute-start | bytes 344072 | tf_op jit(solution)/shard_map/ppermute | solution.py:43
  6.5 2.6 %collective-permute-start.1 = (f32[112,256]{1,0:T(8,128)S(1)}, f32[112,256]{1,0:T(8,128)S(1)}, u32[]{:S(2)}, u32[]{:S(2)}) collective-permute-start(f32[112,256]{1,0:T(8,128)S(1)} %get-tuple-element.30), channel_id=1, source_target_pairs={{0,1},{1,0},{2,4},{3,5},{4,2},{5,3},{6,8},{7,9},{8,6},{9,7},{10,12... | collective-permute-start | bytes 344072 | tf_op jit(solution)/shard_map/ppermute | solution.py:43
  9.0 0.0 copy-start
  9.0 3.4 %shard_map.87.stay_ref.after_ref = f32[512,256]{1,0:T(8,128)S(1)} custom-call(f32[6,128,128]{2,1,0:T(8,128)S(1)} %get-tuple-element.27.field_ref, f32[128,128]{1,0:T(8,128)S(1)} %get-tuple-element.28.slot_ref), custom_call_target="tpu_custom_call" | custom-call | tf_op jit(solution)/shard_map/pallas_call | solution.py:607
  12.5 0.0 collective-permute-done.recva_ref.refs_0_
  12.5 0.0 collective-permute-done.1.recvb_ref.refs_1_
  12.5 0.0 copy-done
  12.5 0.1 shard_map.89
  12.7 1.4 %collective-permute-start.2 = (f32[88,256]{1,0:T(8,128)S(1)}, f32[88,256]{1,0:T(8,128)S(1)}, u32[]{:S(2)}, u32[]{:S(2)}) collective-permute-start(f32[88,256]{1,0:T(8,128)S(1)} %shard_map.89), channel_id=1, source_target_pairs={{0,1},{1,0},{2,3},{3,2},{4,5},{5,4},{6,7},{7,6},{8,9},{9,8},{10,11... | collective-permute-start | bytes 270344 | tf_op jit(solution)/shard_map/ppermute | solution.py:43
  14.0 2.4 %shard_map.88 = (f32[512,256]{1,0:T(8,128)S(1)}, s32[8,128]{1,0:T(8,128)S(1)}) custom-call(f32[512,256]{1,0:T(8,128)S(1)} %shard_map.87.stay_ref.after_ref, f32[112,256]{1,0:T(8,128)S(1)} %collective-permute-done.recva_ref.refs_0_, f32[112,256]{1,0:T(8,128)S(1)} %collective-permute-done.1.recvb_ref.refs_1_, f32[6,128,128]{2,1,0:T(8,128)S(1)} %get-tuple-element.27.field_ref, ...), custom_call_target="tpu_custom_call" | custom-call | tf_op jit(solution)/shard_map/pallas_call | solution.py:607
  16.4 1.0 %collective-permute-done.2.refs_1_.refs_0_ = f32[88,256]{1,0:T(8,128)S(1)} collective-permute-done((f32[88,256]{1,0:T(8,128)S(1)}, f32[88,256]{1,0:T(8,128)S(1)}, u32[]{:S(2)}, u32[]{:S(2)}) %collective-permute-start.2) | collective-permute-done | bytes 90144 | tf_op jit(solution)/shard_map/ppermute | solution.py:43
  17.4 1.8 %shard_map.90 = (f32[8,32,256]{2,1,0:T(8,128)S(1)}, f32[8,8,256]{2,1,0:T(8,128)S(1)}, f32[8,8,256]{2,1,0:T(8,128)S(1)}) custom-call(f32[512,256]{1,0:T(8,128)S(1)} %get-tuple-element.31.refs_0_, f32[88,256]{1,0:T(8,128)S(1)} %collective-permute-done.2.refs_1_.refs_0_), custom_call_target="tpu_custom_call" | custom-call | tf_op jit(solution)/shard_map/pallas_call | solution.py:607
  19.2 0.1 collective-permute-start.3
  19.3 1.6 %collective-permute-start.4 = (f32[8,8,256]{2,1,0:T(8,128)S(1)}, f32[8,8,256]{2,1,0:T(8,128)S(1)}, u32[]{:S(2)}, u32[]{:S(2)}) collective-permute-start(f32[8,8,256]{2,1,0:T(8,128)S(1)} %get-tuple-element.35), channel_id=1, source_target_pairs={{0,1},{1,0},{2,4},{3,5},{4,2},{5,3},{6,8},{7,9},{8,6},{9,7},{10,12... | collective-permute-start | bytes 196616 | tf_op jit(solution)/shard_map/ppermute | solution.py:43
  20.9 3.9 %shard_map.92 = (f32[2,64,256]{2,1,0:T(8,128)S(1)}, f32[128,128]{1,0:T(8,128)S(1)}, s32[4,128]{1,0:T(4,128)S(1)}) custom-call(f32[6,128,128]{2,1,0:T(8,128)S(1)} %get-tuple-element.27.field_ref, f32[128,128]{1,0:T(8,128)S(1)} %get-tuple-element.28.slot_ref, f32[8,32,256]{2,1,0:T(8,128)S(1)} %get-tuple-element.33.after_ref.grid_ref), custom_call_target="tpu_custom_call" | custom-call | tf_op jit(solution)/shard_map/pallas_call | solution.py:607
  24.7 0.0 collective-permute-done.3.froma_ref
  24.7 0.0 collective-permute-done.4.fromb_ref
  24.7 0.0 copy-start.1
  24.8 0.1 shard_map.93
  24.9 0.6 %collective-permute-start.5 = (f32[16,256]{1,0:T(8,128)S(1)}, f32[16,256]{1,0:T(8,128)S(1)}, u32[]{:S(2)}, u32[]{:S(2)}) collective-permute-start(f32[16,256]{1,0:T(8,128)S(1)} %shard_map.93), channel_id=1, source_target_pairs={{0,1},{1,0},{2,3},{3,2},{4,5},{5,4},{6,7},{7,6},{8,9},{9,8},{10,11... | collective-permute-start | bytes 49160 | tf_op jit(solution)/shard_map/ppermute | solution.py:43
  25.5 0.0 copy-done.1
  25.5 1.7 %shard_map.91 = (f32[8,48,384]{2,1,0:T(8,128)S(1)}, f32[8,48,384]{2,1,0:T(8,128)S(1)}, f32[8,48,384]{2,1,0:T(8,128)S(1)}, f32[8,48,384]{2,1,0:T(8,128)S(1)}, f32...) custom-call(f32[8,32,256]{2,1,0:T(8,128)S(1)} %copy-done, ...), custom_call_target="tpu_custom_call" | custom-call | tf_op jit(solution)/shard_map/pallas_call | solution.py:607
  27.2 1.5 %collective-permute-done.5.refs_0_ = f32[16,256]{1,0:T(8,128)S(1)} collective-permute-done((f32[16,256]{1,0:T(8,128)S(1)}, f32[16,256]{1,0:T(8,128)S(1)}, u32[]{:S(2)}, u32[]{:S(2)}) %collective-permute-start.5) | collective-permute-done | bytes 16416 | tf_op jit(solution)/shard_map/ppermute | solution.py:43
  28.7 3.6 %shard_map.94 = (f32[8,32,256]{2,1,0:T(8,128)}, bf16[1024,256]{1,0:T(8,128)(2,1)S(1)}) custom-call(f32[8,32,256]{2,1,0:T(8,128)S(1)} %get-tuple-element.33.after_ref.grid_ref, f32[8,8,256]{2,1,0:T(8,128)S(1)} %collective-permute-done.3.froma_ref, f32[8,8,256]{2,1,0:T(8,128)S(1)} %collective-permute-done.4.fromb_ref, ...), custom_call_target="tpu_custom_call" | custom-call | tf_op jit(solution)/shard_map/pallas_call | solution.py:607
  32.3 1.7 %shard_map.97 = f32[48,256]{1,0:T(8,128)S(1)} custom-call(bf16[1024,256]{1,0:T(8,128)(2,1)S(1)} %get-tuple-element.44.slope_ref, s32[8,128]{1,0:T(8,128)S(1)} %get-tuple-element.47.unit_ref, f32[88,256]{1,0:T(8,128)S(1)} %collective-permute-done.2.refs_1_.refs_0_), custom_call_target="tpu_custom_call" | custom-call | tf_op jit(solution)/shard_map/pallas_call | solution.py:607
  34.0 0.7 %collective-permute-start.6 = (f32[48,256]{1,0:T(8,128)S(1)}, f32[48,256]{1,0:T(8,128)S(1)}, u32[]{:S(2)}, u32[]{:S(2)}) collective-permute-start(f32[48,256]{1,0:T(8,128)S(1)} %shard_map.97), channel_id=1, source_target_pairs={{0,1},{1,0},{2,3},{3,2},{4,5},{5,4},{6,7},{7,6},{8,9},{9,8},{10,11... | collective-permute-start | bytes 147464 | tf_op jit(solution)/shard_map/ppermute | solution.py:43
  34.7 1.2 %shard_map.96.after_ref.refs_1_ = f32[1,48,256]{2,1,0:T(8,128)S(1)} custom-call(bf16[1024,256]{1,0:T(8,128)(2,1)S(1)} %get-tuple-element.44.slope_ref, f32[2,64,256]{2,1,0:T(8,128)S(1)} %get-tuple-element.42.after_ref.order_ref, s32[4,128]{1,0:T(4,128)S(1)} %get-tuple-element.46.unit_ref), custom_call_target="tpu_custom_call" | custom-call | tf_op jit(solution)/shard_map/pallas_call | solution.py:607
  35.9 1.4 %shard_map.95.near_ref = f32[32,256]{1,0:T(8,128)S(1)} custom-call(bf16[1024,256]{1,0:T(8,128)(2,1)S(1)} %get-tuple-element.44.slope_ref, s32[8,128]{1,0:T(8,128)S(1)} %get-tuple-element.45.unit_ref, f32[112,256]{1,0:T(8,128)S(1)} %collective-permute-done.recva_ref.refs_0_, f32[112,256]{1,0:T(8,128)S(1)} %collective-permute-done.1.recvb_ref.refs_1_), custom_call_target="tpu_custom_call" | custom-call | tf_op jit(solution)/shard_map/pallas_call | solution.py:607
  37.3 0.9 %collective-permute-done.6.refs_0_ = f32[48,256]{1,0:T(8,128)S(1)} collective-permute-done((f32[48,256]{1,0:T(8,128)S(1)}, f32[48,256]{1,0:T(8,128)S(1)}, u32[]{:S(2)}, u32[]{:S(2)}) %collective-permute-start.6) | collective-permute-done | bytes 49184 | tf_op jit(solution)/shard_map/ppermute | solution.py:43
  38.2 0.0 collective-permute-start.7
  38.2 0.7 %collective-permute-start.8 = (f32[32,256]{1,0:T(8,128)S(1)}, f32[32,256]{1,0:T(8,128)S(1)}, u32[]{:S(2)}, u32[]{:S(2)}) collective-permute-start(f32[32,256]{1,0:T(8,128)S(1)} %get-tuple-element.49), channel_id=1, source_target_pairs={{0,1},{1,0},{2,4},{3,5},{4,2},{5,3},{6,8},{7,9},{8,6},{9,7},{10,12... | collective-permute-start | bytes 98312 | tf_op jit(solution)/shard_map/ppermute | solution.py:43
  38.9 2.4 %shard_map.99.refs_2_ = f32[3,48,256]{2,1,0:T(8,128)S(1)} custom-call(bf16[1024,256]{1,0:T(8,128)(2,1)S(1)} %get-tuple-element.44.slope_ref, f32[2,64,256]{2,1,0:T(8,128)S(1)} %get-tuple-element.42.after_ref.order_ref, s32[4,128]{1,0:T(4,128)S(1)} %get-tuple-element.46.unit_ref), custom_call_target="tpu_custom_call" | custom-call | tf_op jit(solution)/shard_map/pallas_call | solution.py:607
  41.3 0.0 collective-permute-done.7.backa_ref
  41.3 0.8 %collective-permute-done.8.backb_ref = f32[32,256]{1,0:T(8,128)S(1)} collective-permute-done((f32[32,256]{1,0:T(8,128)S(1)}, f32[32,256]{1,0:T(8,128)S(1)}, u32[]{:S(2)}, u32[]{:S(2)}) %collective-permute-start.8) | collective-permute-done | bytes 32800 | tf_op jit(solution)/shard_map/ppermute | solution.py:43
  42.1 3.6 %shard_map.100 = f32[2,16384]{1,0:T(2,128)} custom-call(f32[32,256]{1,0:T(8,128)S(1)} %collective-permute-done.7.backa_ref, f32[32,256]{1,0:T(8,128)S(1)} %collective-permute-done.8.backb_ref, f32[48,256]{1,0:T(8,128)S(1)} %collective-permute-done.6.refs_0_, f32[1,48,256]{2,1,0:T(8,128)S(1)} %shard_map.96.after_ref.refs_1_, ...), custom_call_target="tpu_custom_call" | custom-call | tf_op jit(solution)/shard_map/pallas_call | solution.py:607
  (1 shorter events, 0.0 us)
Async XLA Ops:
  6.0 6.5 %collective-permute-start = (f32[112,256]{1,0:T(8,128)S(1)}, f32[112,256]{1,0:T(8,128)S(1)}, u32[]{:S(2)}, u32[]{:S(2)}) collective-permute-start(f32[112,256]{1,0:T(8,128)S(1)} %get-tuple-element.29), channel_id=1, source_target_pairs={{0,2},{1,3},{2,0},{3,1},{4,6},{5,7},{6,4},{7,5},{8,10},{9,11},{10,... | collective-permute-start | bytes 344072 | tf_op jit(solution)/shard_map/ppermute | solution.py:43
  6.5 6.0 %collective-permute-start.1 = (f32[112,256]{1,0:T(8,128)S(1)}, f32[112,256]{1,0:T(8,128)S(1)}, u32[]{:S(2)}, u32[]{:S(2)}) collective-permute-start(f32[112,256]{1,0:T(8,128)S(1)} %get-tuple-element.30), channel_id=1, source_target_pairs={{0,1},{1,0},{2,4},{3,5},{4,2},{5,3},{6,8},{7,9},{8,6},{9,7},{10,12... | collective-permute-start | bytes 344072 | tf_op jit(solution)/shard_map/ppermute | solution.py:43
  9.0 3.5 %copy-start = (f32[8,32,256]{2,1,0:T(8,128)S(1)}, f32[8,32,256]{2,1,0:T(8,128)}, u32[]{:S(2)}) copy-start(f32[8,32,256]{2,1,0:T(8,128)} %cond_ref.3) | copy-start | bytes 786436
  12.7 4.7 %collective-permute-start.2 = (f32[88,256]{1,0:T(8,128)S(1)}, f32[88,256]{1,0:T(8,128)S(1)}, u32[]{:S(2)}, u32[]{:S(2)}) collective-permute-start(f32[88,256]{1,0:T(8,128)S(1)} %shard_map.89), channel_id=1, source_target_pairs={{0,1},{1,0},{2,3},{3,2},{4,5},{5,4},{6,7},{7,6},{8,9},{9,8},{10,11... | collective-permute-start | bytes 270344 | tf_op jit(solution)/shard_map/ppermute | solution.py:43
  19.2 5.5 %collective-permute-start.3 = (f32[8,8,256]{2,1,0:T(8,128)S(1)}, f32[8,8,256]{2,1,0:T(8,128)S(1)}, u32[]{:S(2)}, u32[]{:S(2)}) collective-permute-start(f32[8,8,256]{2,1,0:T(8,128)S(1)} %get-tuple-element.34), channel_id=1, source_target_pairs={{0,2},{1,3},{2,0},{3,1},{4,6},{5,7},{6,4},{7,5},{8,10},{9,11},{10,... | collective-permute-start | bytes 196616 | tf_op jit(solution)/shard_map/ppermute | solution.py:43
  19.3 5.4 %collective-permute-start.4 = (f32[8,8,256]{2,1,0:T(8,128)S(1)}, f32[8,8,256]{2,1,0:T(8,128)S(1)}, u32[]{:S(2)}, u32[]{:S(2)}) collective-permute-start(f32[8,8,256]{2,1,0:T(8,128)S(1)} %get-tuple-element.35), channel_id=1, source_target_pairs={{0,1},{1,0},{2,4},{3,5},{4,2},{5,3},{6,8},{7,9},{8,6},{9,7},{10,12... | collective-permute-start | bytes 196616 | tf_op jit(solution)/shard_map/ppermute | solution.py:43
  24.7 0.8 %copy-start.1 = (f32[7]{0:T(128)S(1)}, f32[7]{0:T(128)}, u32[]{:S(2)}) copy-start(f32[7]{0:T(128)} %coupling_ref.1) | copy-start | bytes 88
  24.9 3.8 %collective-permute-start.5 = (f32[16,256]{1,0:T(8,128)S(1)}, f32[16,256]{1,0:T(8,128)S(1)}, u32[]{:S(2)}, u32[]{:S(2)}) collective-permute-start(f32[16,256]{1,0:T(8,128)S(1)} %shard_map.93), channel_id=1, source_target_pairs={{0,1},{1,0},{2,3},{3,2},{4,5},{5,4},{6,7},{7,6},{8,9},{9,8},{10,11... | collective-permute-start | bytes 49160 | tf_op jit(solution)/shard_map/ppermute | solution.py:43
  34.0 4.2 %collective-permute-start.6 = (f32[48,256]{1,0:T(8,128)S(1)}, f32[48,256]{1,0:T(8,128)S(1)}, u32[]{:S(2)}, u32[]{:S(2)}) collective-permute-start(f32[48,256]{1,0:T(8,128)S(1)} %shard_map.97), channel_id=1, source_target_pairs={{0,1},{1,0},{2,3},{3,2},{4,5},{5,4},{6,7},{7,6},{8,9},{9,8},{10,11... | collective-permute-start | bytes 147464 | tf_op jit(solution)/shard_map/ppermute | solution.py:43
  38.2 3.1 %collective-permute-start.7 = (f32[32,256]{1,0:T(8,128)S(1)}, f32[32,256]{1,0:T(8,128)S(1)}, u32[]{:S(2)}, u32[]{:S(2)}) collective-permute-start(f32[32,256]{1,0:T(8,128)S(1)} %get-tuple-element.48), channel_id=1, source_target_pairs={{0,2},{1,3},{2,0},{3,1},{4,6},{5,7},{6,4},{7,5},{8,10},{9,11},{10,... | collective-permute-start | bytes 98312 | tf_op jit(solution)/shard_map/ppermute | solution.py:43
  38.2 4.0 %collective-permute-start.8 = (f32[32,256]{1,0:T(8,128)S(1)}, f32[32,256]{1,0:T(8,128)S(1)}, u32[]{:S(2)}, u32[]{:S(2)}) collective-permute-start(f32[32,256]{1,0:T(8,128)S(1)} %get-tuple-element.49), channel_id=1, source_target_pairs={{0,1},{1,0},{2,4},{3,5},{4,2},{5,3},{6,8},{7,9},{8,6},{9,7},{10,12... | collective-permute-start | bytes 98312 | tf_op jit(solution)/shard_map/ppermute | solution.py:43

commit v8 on v7

--- a/solution.py
+++ b/solution.py
@@ -140,7 +140,7 @@
     spill = spill_ref[...]
     field_ref[2], field_ref[3] = pieces(power * (1.0 - spill))
     field_ref[4], field_ref[5] = pieces(power * spill)
-    step = 32
+    step = 64
 
     def body(j, carry):
         base = pl.multiple_of(j * step, step)
@@ -181,14 +181,31 @@
     msgb_ref[top:, :] = jnp.where(even, first, last).reshape(flat)
 
 
-def deposit_block(lc, r, main, spill, cols, cells):
+def deposit_block(lc, r, main, spill, cols, cells, part=None):
     picks, marks = [], []
     zero = jnp.zeros((), BF16)
     narrow = lambda x: x.astype(BF16)
+    quarter = cols // 4
+    count = cells if part is None else cells // 2
     for lc_i, r_i, (mh, ml), (sh, sl) in zip(lc, r, main, spill):
-        spot = narrow(row_iota(cells, lc_i.shape[1]))
-        other = jnp.where(lc_i >= float(cells - cols), lc_i - cols, lc_i + cols)
-        here, there = spot == narrow(lc_i), spot == narrow(other)
+        spot = narrow(row_iota(count, lc_i.shape[1]))
+        step = cols
+        other = lambda at: jnp.where(lc_i >= float(cells - cols), at - step, at + step)
+        if part is None:
+            there_i = other(lc_i)
+        else:
+            step = cols // 2
+            layer = jnp.floor(lc_i * (1.0 / cols))
+            column = lc_i - layer * cols
+            inner = (column >= quarter) & (column < 3 * quarter)
+            if part == "inner":
+                mine, at = inner, layer * step + (column - quarter)
+            else:
+                mine = jnp.logical_not(inner)
+                at = layer * step + jnp.where(column < quarter, column, column - step)
+            there_i = jnp.where(mine, other(at), -1.0)
+            lc_i = jnp.where(mine, at, -1.0)
+        here, there = spot == narrow(lc_i), spot == narrow(there_i)
         high = jnp.where(here, narrow(mh), jnp.where(there, narrow(sh), zero))
         low = jnp.where(here, narrow(ml), jnp.where(there, narrow(sl), zero))
         picks.append(jnp.concatenate([high, low], axis=0))
@@ -215,10 +232,10 @@
     deposit_stays(grid_ref, field_ref, slot_ref, 0, split, cols)
 
 
-def deposit_groups(grid_ref, sources, cols):
-    count, rows = grid_ref.shape[0] // 2, grid_ref.shape[1]
+def group_deposit(sources, cols, count, part=None):
     lc, r, main, spill = [], [], [], []
     for ref, at in sources:
+        rows = ref.shape[1]
         for row in range(at, at + GROUP):
             code = ref[row : row + 1, :]
             lc_i = jnp.floor(code * (1.0 / rows))
@@ -226,7 +243,7 @@
             r.append(code - lc_i * rows)
             main.append(pieces(ref[row + GROUP : row + GROUP + 1, :]))
             spill.append(pieces(ref[row + 2 * GROUP : row + 2 * GROUP + 1, :]))
-    grid_ref[...] += deposit_block(lc, r, main, spill, cols, count)
+    return deposit_block(lc, r, main, spill, cols, count, part)
 
 
 def count_units(unit_ref, sources, layers, cells):
@@ -250,22 +267,39 @@
     count_units(unit_ref, [(recva_ref, 0), (recvb_ref, 0)], count // cols, cols * rows)
     grid_ref[...] = stay_ref[...]
     deposit_stays(grid_ref, field_ref, slot_ref, split, slot_ref.shape[0], cols)
-    deposit_groups(grid_ref, [(recva_ref, 0), (recvb_ref, 0)], cols)
-
-
-def far_deposit_kernel(cols, nyc, *refs):
-    near_ref, recvy = refs[0], refs[1:nyc]
-    grid_ref, edgea_ref, edgeb_ref, acc_ref = refs[nyc:]
-    acc_ref[...] = near_ref[...]
-    sources = [(ref, 3 * GROUP * i) for ref in recvy for i in range(3)]
-    deposit_groups(acc_ref, sources, cols)
-    count = acc_ref.shape[0] // 2
-    grid = (acc_ref[:count, :] + acc_ref[count:, :]).reshape(grid_ref.shape)
-    grid_ref[...] = grid
-    first, last = grid[:, :HALO, :], grid[:, cols - HALO :, :]
+    grid_ref[...] += group_deposit([(recva_ref, 0), (recvb_ref, 0)], cols, count)
+
+
+def half_deposit(near_ref, recvy, cols, part):
+    count, rows = near_ref.shape[0] // 2, near_ref.shape[1]
+    layers = count // cols
+    far = group_deposit([(ref, 3 * GROUP * i) for ref in recvy for i in range(3)], cols, count, part)
+    far = far[: count // 2] + far[count // 2 :]
+    near = (near_ref[:count, :] + near_ref[count:, :]).reshape(layers, cols, rows)
+    quarter = cols // 4
+    if part == "inner":
+        near = near[:, quarter : 3 * quarter]
+    else:
+        near = jnp.concatenate([near[:, :quarter], near[:, 3 * quarter :]], axis=1)
+    return near + far.reshape(layers, cols // 2, rows)
+
+
+def edge_deposit_kernel(cols, near_ref, after_ref, *refs):
+    recvy, (outer_ref, edgea_ref, edgeb_ref) = refs[:-3], refs[-3:]
+    outer = half_deposit(near_ref, recvy, cols, "edge")
+    outer_ref[...] = outer
+    first, last = outer[:, :HALO], outer[:, cols // 2 - HALO :]
     even = lax.rem(lax.axis_index("gx"), 2) == 0
     edgea_ref[...] = jnp.where(even, last, first)
     edgeb_ref[...] = jnp.where(even, first, last)
+
+
+def inner_deposit_kernel(cols, near_ref, outer_ref, *refs):
+    recvy, grid_ref = refs[:-1], refs[-1]
+    quarter = cols // 4
+    grid_ref[:, :quarter, :] = outer_ref[:, :quarter, :]
+    grid_ref[:, 3 * quarter :, :] = outer_ref[:, quarter:, :]
+    grid_ref[:, quarter : 3 * quarter, :] = half_deposit(near_ref, recvy, cols, "inner")
 
 
 def with_columns(own, from_a, from_b):
@@ -341,7 +375,7 @@
 
 def face_kernel(nyc, cond_ref, recva_ref, recvb_ref, coupling_ref, *refs):
     recvy_refs = refs[: nyc - 1]
-    cn_ref, cp_ref, rn_ref, rp_ref, fl_ref, d_ref, unit_ref, k_ref = refs[nyc - 1 :]
+    cn_ref, cp_ref, rn_ref, fl_ref, d_ref, unit_ref, k_ref = refs[nyc - 1 :]
     layers, cols, rows = cond_ref.shape
     span, wide_rows = cols + 2 * HALO, rows + 128
     count = layers * span
@@ -377,7 +411,7 @@
         face_c, face_r = 0.5 * (k + next_c(k)), 0.5 * (k + next_r(k))
         kept_c, kept_r = face_c * both_c, face_r * both_r
         cn_ref[l], cp_ref[l] = kept_c, prev_c(kept_c)
-        rn_ref[l], rp_ref[l] = kept_r, prev_r(kept_r)
+        rn_ref[l] = kept_r
         total = SINK_RATE + ((face_c + prev_c(face_c)) + (face_r + prev_r(face_r)))
         if below is not None:
             total = total + below
@@ -389,7 +423,7 @@
 
 
 def solve_kernel(
-    nyc, grid_ref, froma_ref, fromb_ref, cn_ref, cp_ref, rn_ref, rp_ref, fl_ref, d_ref, *refs
+    nyc, grid_ref, froma_ref, fromb_ref, cn_ref, cp_ref, rn_ref, fl_ref, d_ref, *refs
 ):
     edge_refs, (warmth_ref, slope_ref, p_ref, v_ref, u_ref) = refs[: nyc - 1], refs[nyc - 1 :]
     layers, cols, rows = grid_ref.shape
@@ -422,7 +456,8 @@
                 rest = p_ref[l, at, :] - d_ref[l, at, :] * v
                 rest = rest + cn_ref[l, at, :] * v_ref[old, l, c + 9 : c + 17, :]
                 rest = rest + cp_ref[l, at, :] * v_ref[old, l, c + 7 : c + 15, :]
-                rest = rest + rn_ref[l, at, :] * next_r(v) + rp_ref[l, at, :] * prev_r(v)
+                after = rn_ref[l, at, :]
+                rest = rest + (after * next_r(v) + prev_r(after * v))
                 if l + 1 < layers:
                     rest = rest + fl_ref[l, at, :] * vs[l + 1]
                 if l:
@@ -483,7 +518,7 @@
             out_ref[(g * 2 + f) * GROUP : (g * 2 + f + 1) * GROUP, :] = totals[f]
 
 
-def sort_kernel(layers, cols, table, field_ref, slot_ref, after_ref, order_ref, place_ref, unit_ref):
+def rank_kernel(layers, cols, table, field_ref, slot_ref, after_ref, place_ref, unit_ref, row_ref, lam_ref):
     size = slot_ref.shape[0]
     span = BLOCK * size // WIDE
     r_i = lax.broadcasted_iota(jnp.int32, (size, size), 0)
@@ -514,6 +549,13 @@
     lam = rank - row * WIDE
     slot = slot_ref[...]
     place_ref[...] = jnp.where(slot >= 0.0, slot, (row + layer + table) * WIDE + lam)
+    row_ref[...], lam_ref[...] = row, lam
+
+
+def sort_kernel(field_ref, row_ref, lam_ref, after_ref, order_ref):
+    size = row_ref.shape[0]
+    span = BLOCK * size // WIDE
+    row, lam = row_ref[...], lam_ref[...]
     for k in range(size // BLOCK):
         picks, marks = [], []
         for i in range(k * BLOCK, (k + 1) * BLOCK):
@@ -671,21 +713,32 @@
         [],
         stay_grid, recv_a, recv_b, fields, slot,
     )
+    table = groups * GROUP
+    place, unit, row, lam = call(
+        partial(rank_kernel, layers, cols, table),
+        [(square, F32), ((square[0] // BLOCK, 128), jnp.int32), (square, F32), (square, F32)],
+        [],
+        fields, slot, near_grid,
+        spaces={2: pl.ANY},
+    )
     edge = (layers, HALO, rows)
-    grid, edge_a, edge_b = call(
-        partial(far_deposit_kernel, cols, nyc),
-        [(conductivity.shape, F32), (edge, F32), (edge, F32)],
-        [vmem(2 * count, rows)],
-        near_grid, *recv_y,
+    outer, edge_a, edge_b = call(
+        partial(edge_deposit_kernel, cols),
+        [((layers, cols // 2, rows), F32), (edge, F32), (edge, F32)],
+        [],
+        near_grid, row, *recv_y,
+        spaces={1: pl.ANY},
     )
     from_a, from_b = exchange(edge_a, 1, 0), exchange(edge_b, 2, 0)
-    table = groups * GROUP
-    order, place, unit = call(
-        partial(sort_kernel, layers, cols, table),
-        [((2, cells // WIDE, WIDE), F32), (square, F32), ((square[0] // BLOCK, 128), jnp.int32)],
+    (grid,) = call(
+        partial(inner_deposit_kernel, cols), [(tile, F32)], [], near_grid, outer, *recv_y
+    )
+    (order,) = call(
+        sort_kernel,
+        [((2, cells // WIDE, WIDE), F32)],
         [],
-        fields, slot, grid,
-        spaces={2: pl.ANY},
+        fields, row, lam, grid,
+        spaces={3: pl.ANY},
     )
     edges = call(
         power_edge_kernel,
@@ -698,7 +751,7 @@
     big = (layers, cols + 2 * HALO, rows + 128)
     *faces, far_unit = call(
         partial(face_kernel, nyc),
-        [(big, F32)] * 6 + [((8, 128), jnp.int32)],
+        [(big, F32)] * 5 + [((8, 128), jnp.int32)],
         [vmem(*big)],
         conductivity, recv_a, recv_b, layer_coupling, *recv_y,
         spaces={3: pltpu.SMEM},

time: 45.9 us -> 44.4 us (0.967)
  waiting for transfers between devices: 4.21 us -> 1.92 us
  starting transfers between devices: 8.17 us -> 9.11 us
    ppermute x9, waiting for transfers between devices: 4.21 us -> 1.92 us  [exchange(): return lax.ppermute(value, ('gx', 'gy'), pairs)]
    ppermute x9, starting transfers between devices: 8.17 us -> 9.11 us  [exchange(): return lax.ppermute(value, ('gx', 'gy'), pairs)]
    pallas_call x15 -> x17, Pallas kernels: 32.6 us -> 32.4 us  [call(): pl.pallas_call(kernel, out_shape=shapes, in_specs=specs, out_specs=[space...]
  transfers between devices with their start and end apart: 9 -> 9, of which waited for: 4 -> 3; matrix products, arithmetic and copies ran while one was open for 0% -> 0% of each run, Pallas kernels for 35% -> 39%
where the time goes in v8:
time: 44.4 us; the launch traced here: 44.3 us
  Pallas kernels  32.4 us (73%)
  starting transfers between devices  9.11 us (21%)
  waiting for transfers between devices  1.92 us (4%)
  between operations  0.8 us (2%)
    pallas_call x17, Pallas kernels, call(): pl.pallas_call(kernel, out_shape=shapes, in_specs=specs, out_specs=[space...  32.4 us
    ppermute x9, starting transfers between devices, exchange(): return lax.ppermute(value, ('gx', 'gy'), pairs)  9.11 us
    ppermute x9, waiting for transfers between devices, exchange(): return lax.ppermute(value, ('gx', 'gy'), pairs)  1.92 us
  transfers between devices with their start and end apart: 9, of which 3 were waited for; matrix products, arithmetic and copies ran while one was open for 0% of the time, Pallas kernels for 39%

profile of v8, /device:TPU:0, one launch (start us, length us, event | category | flops | bytes accessed | tf_op | source)
XLA Modules:
  0.0 44.3 jit_solution(2919663816531770023)
XLA Ops:
  0.6 4.9 %shard_map.86 = (f32[112,256]{1,0:T(8,128)S(1)}, f32[112,256]{1,0:T(8,128)S(1)}, f32[24,256]{1,0:T(8,128)S(1)}, f32[128,128]{1,0:T(8,128)S(1)}, f32[6,128,128]{2,1,0:T(8,128)S(1)}, /*index=5*/f32[128,128]{1,0:T(8,128)S(1)}) custom-call(s32[128,128]{1,0:T(8,128)} %bitcast.5, s32[128,128]{1,0:T(8,128)} %bitcast.6, s32[128,128]{1,0:T(8,128)} %bitcast.7, ...), custom_call_target="tpu_custom_call" | custom-call | tf_op jit(solution)/shard_map/pallas_call | solution.py:649
  5.5 0.5 %collective-permute-start = (f32[112,256]{1,0:T(8,128)S(1)}, f32[112,256]{1,0:T(8,128)S(1)}, u32[]{:S(2)}, u32[]{:S(2)}) collective-permute-start(f32[112,256]{1,0:T(8,128)S(1)} %get-tuple-element.29), channel_id=1, source_target_pairs={{0,2},{1,3},{2,0},{3,1},{4,6},{5,7},{6,4},{7,5},{8,10},{9,11},{10,... | collective-permute-start | bytes 344072 | tf_op jit(solution)/shard_map/ppermute | solution.py:43
  6.0 2.6 %collective-permute-start.1 = (f32[112,256]{1,0:T(8,128)S(1)}, f32[112,256]{1,0:T(8,128)S(1)}, u32[]{:S(2)}, u32[]{:S(2)}) collective-permute-start(f32[112,256]{1,0:T(8,128)S(1)} %get-tuple-element.30), channel_id=1, source_target_pairs={{0,1},{1,0},{2,4},{3,5},{4,2},{5,3},{6,8},{7,9},{8,6},{9,7},{10,12... | collective-permute-start | bytes 344072 | tf_op jit(solution)/shard_map/ppermute | solution.py:43
  8.6 0.0 copy-start
  8.6 3.4 %shard_map.87.stay_ref.after_ref = f32[512,256]{1,0:T(8,128)S(1)} custom-call(f32[6,128,128]{2,1,0:T(8,128)S(1)} %get-tuple-element.27.field_ref, f32[128,128]{1,0:T(8,128)S(1)} %get-tuple-element.28.slot_ref), custom_call_target="tpu_custom_call" | custom-call | tf_op jit(solution)/shard_map/pallas_call | solution.py:649
  12.0 0.0 collective-permute-done.recva_ref.refs_0_
  12.1 0.0 collective-permute-done.1.recvb_ref.refs_1_
  12.1 0.0 copy-done
  12.1 0.1 shard_map.90
  12.2 1.4 %collective-permute-start.2 = (f32[88,256]{1,0:T(8,128)S(1)}, f32[88,256]{1,0:T(8,128)S(1)}, u32[]{:S(2)}, u32[]{:S(2)}) collective-permute-start(f32[88,256]{1,0:T(8,128)S(1)} %shard_map.90), channel_id=1, source_target_pairs={{0,1},{1,0},{2,3},{3,2},{4,5},{5,4},{6,7},{7,6},{8,9},{9,8},{10,11... | collective-permute-start | bytes 270344 | tf_op jit(solution)/shard_map/ppermute | solution.py:43
  13.6 2.4 %shard_map.88 = (f32[512,256]{1,0:T(8,128)S(1)}, s32[8,128]{1,0:T(8,128)S(1)}) custom-call(f32[512,256]{1,0:T(8,128)S(1)} %shard_map.87.stay_ref.after_ref, f32[112,256]{1,0:T(8,128)S(1)} %collective-permute-done.recva_ref.refs_0_, f32[112,256]{1,0:T(8,128)S(1)} %collective-permute-done.1.recvb_ref.refs_1_, f32[6,128,128]{2,1,0:T(8,128)S(1)} %get-tuple-element.27.field_ref, ...), custom_call_target="tpu_custom_call" | custom-call | tf_op jit(solution)/shard_map/pallas_call | solution.py:649
  16.0 1.5 %shard_map.89 = (f32[128,128]{1,0:T(8,128)S(1)}, s32[4,128]{1,0:T(4,128)S(1)}, f32[128,128]{1,0:T(8,128)S(1)}, f32[128,128]{1,0:T(8,128)S(1)}) custom-call(f32[6,128,128]{2,1,0:T(8,128)S(1)} %get-tuple-element.27.field_ref, f32[128,128]{1,0:T(8,128)S(1)} %get-tuple-element.28.slot_ref, f32[512,256]{1,0:T(8,128)S(1)} %get-tuple-element.31.after_ref.near_ref), custom_call_target="tpu_custom_call" | custom-call | tf_op jit(solution)/shard_map/pallas_call | solution.py:649
  17.5 0.0 collective-permute-done.2.refs_0_
  17.5 1.1 %shard_map.91 = (f32[8,16,256]{2,1,0:T(8,128)S(1)}, f32[8,8,256]{2,1,0:T(8,128)S(1)}, f32[8,8,256]{2,1,0:T(8,128)S(1)}) custom-call(f32[512,256]{1,0:T(8,128)S(1)} %get-tuple-element.31.after_ref.near_ref, f32[128,128]{1,0:T(8,128)S(1)} %get-tuple-element.32.after_ref.row_ref, f32[88,256]{1,0:T(8,128)S(1)} %collective-permute-done.2.refs_0_), custom_call_target="tpu_custom_call" | custom-call | tf_op jit(solution)/shard_map/pallas_call | solution.py:649
  18.6 0.1 collective-permute-start.3
  18.7 0.9 %collective-permute-start.4 = (f32[8,8,256]{2,1,0:T(8,128)S(1)}, f32[8,8,256]{2,1,0:T(8,128)S(1)}, u32[]{:S(2)}, u32[]{:S(2)}) collective-permute-start(f32[8,8,256]{2,1,0:T(8,128)S(1)} %get-tuple-element.36), channel_id=1, source_target_pairs={{0,1},{1,0},{2,4},{3,5},{4,2},{5,3},{6,8},{7,9},{8,6},{9,7},{10,12... | collective-permute-start | bytes 196616 | tf_op jit(solution)/shard_map/ppermute | solution.py:43
  19.6 1.1 %shard_map.92.after_ref.grid_ref = f32[8,32,256]{2,1,0:T(8,128)S(1)} custom-call(f32[512,256]{1,0:T(8,128)S(1)} %get-tuple-element.31.after_ref.near_ref, f32[8,16,256]{2,1,0:T(8,128)S(1)} %get-tuple-element.34.outer_ref, f32[88,256]{1,0:T(8,128)S(1)} %collective-permute-done.2.refs_0_), custom_call_target="tpu_custom_call" | custom-call | tf_op jit(solution)/shard_map/pallas_call | solution.py:649
  20.7 2.5 %shard_map.94.after_ref.order_ref = f32[2,64,256]{2,1,0:T(8,128)S(1)} custom-call(f32[6,128,128]{2,1,0:T(8,128)S(1)} %get-tuple-element.27.field_ref, f32[128,128]{1,0:T(8,128)S(1)} %get-tuple-element.32.after_ref.row_ref, f32[128,128]{1,0:T(8,128)S(1)} %get-tuple-element.42.lam_ref, f32[8,32,256]{2,1,0:T(8,128)S(1)} %shard_map.92.after_ref.grid_ref), custom_call_target="tpu_custom_call" | custom-call | tf_op jit(solution)/shard_map/pallas_call | solution.py:649
  23.2 0.0 copy-start.1
  23.2 0.0 collective-permute-done.3.froma_ref
  23.3 0.0 collective-permute-done.4.fromb_ref
  23.3 0.1 shard_map.95
  23.4 1.2 %collective-permute-start.5 = (f32[16,256]{1,0:T(8,128)S(1)}, f32[16,256]{1,0:T(8,128)S(1)}, u32[]{:S(2)}, u32[]{:S(2)}) collective-permute-start(f32[16,256]{1,0:T(8,128)S(1)} %shard_map.95), channel_id=1, source_target_pairs={{0,1},{1,0},{2,3},{3,2},{4,5},{5,4},{6,7},{7,6},{8,9},{9,8},{10,11... | collective-permute-start | bytes 49160 | tf_op jit(solution)/shard_map/ppermute | solution.py:43
  24.6 0.0 copy-done.1
  24.6 1.5 %shard_map.93 = (f32[8,48,384]{2,1,0:T(8,128)S(1)}, f32[8,48,384]{2,1,0:T(8,128)S(1)}, f32[8,48,384]{2,1,0:T(8,128)S(1)}, f32[8,48,384]{2,1,0:T(8,128)S(1)}, f32...) custom-call(f32[8,32,256]{2,1,0:T(8,128)S(1)} %copy-done, f32[112,256]{1,0:T(8,128)S(1)} %collective-permute-done.recva_ref.refs_0_, ...), custom_call_target="tpu_custom_call" | custom-call | tf_op jit(solution)/shard_map/pallas_call | solution.py:649
  26.1 1.1 %collective-permute-done.5.refs_0_ = f32[16,256]{1,0:T(8,128)S(1)} collective-permute-done((f32[16,256]{1,0:T(8,128)S(1)}, f32[16,256]{1,0:T(8,128)S(1)}, u32[]{:S(2)}, u32[]{:S(2)}) %collective-permute-start.5) | collective-permute-done | bytes 16416 | tf_op jit(solution)/shard_map/ppermute | solution.py:43
  27.2 3.6 %shard_map.96 = (f32[8,32,256]{2,1,0:T(8,128)}, bf16[1024,256]{1,0:T(8,128)(2,1)S(1)}) custom-call(f32[8,32,256]{2,1,0:T(8,128)S(1)} %shard_map.92.after_ref.grid_ref, f32[8,8,256]{2,1,0:T(8,128)S(1)} %collective-permute-done.3.froma_ref, f32[8,8,256]{2,1,0:T(8,128)S(1)} %collective-permute-done.4.fromb_ref, f32[8,48,384]{2,1,0:T(8,128)S(1)} %get-tuple-element.37.cn_ref, ...), custom_call_target="tpu_custom_call" | custom-call | tf_op jit(solution)/shard_map/pallas_call | solution.py:649
  30.8 1.7 %shard_map.99 = f32[48,256]{1,0:T(8,128)S(1)} custom-call(bf16[1024,256]{1,0:T(8,128)(2,1)S(1)} %get-tuple-element.44.slope_ref, s32[8,128]{1,0:T(8,128)S(1)} %get-tuple-element.47.unit_ref, f32[88,256]{1,0:T(8,128)S(1)} %collective-permute-done.2.refs_0_), custom_call_target="tpu_custom_call" | custom-call | tf_op jit(solution)/shard_map/pallas_call | solution.py:649
  32.5 1.2 %collective-permute-start.6 = (f32[48,256]{1,0:T(8,128)S(1)}, f32[48,256]{1,0:T(8,128)S(1)}, u32[]{:S(2)}, u32[]{:S(2)}) collective-permute-start(f32[48,256]{1,0:T(8,128)S(1)} %shard_map.99), channel_id=1, source_target_pairs={{0,1},{1,0},{2,3},{3,2},{4,5},{5,4},{6,7},{7,6},{8,9},{9,8},{10,11... | collective-permute-start | bytes 147464 | tf_op jit(solution)/shard_map/ppermute | solution.py:43
  33.7 1.2 %shard_map.98.after_ref.refs_1_ = f32[1,48,256]{2,1,0:T(8,128)S(1)} custom-call(bf16[1024,256]{1,0:T(8,128)(2,1)S(1)} %get-tuple-element.44.slope_ref, f32[2,64,256]{2,1,0:T(8,128)S(1)} %shard_map.94.after_ref.order_ref, s32[4,128]{1,0:T(4,128)S(1)} %get-tuple-element.46.unit_ref), custom_call_target="tpu_custom_call" | custom-call | tf_op jit(solution)/shard_map/pallas_call | solution.py:649
  34.9 1.4 %shard_map.97.near_ref = f32[32,256]{1,0:T(8,128)S(1)} custom-call(bf16[1024,256]{1,0:T(8,128)(2,1)S(1)} %get-tuple-element.44.slope_ref, s32[8,128]{1,0:T(8,128)S(1)} %get-tuple-element.45.unit_ref, f32[112,256]{1,0:T(8,128)S(1)} %collective-permute-done.recva_ref.refs_0_, f32[112,256]{1,0:T(8,128)S(1)} %collective-permute-done.1.recvb_ref.refs_1_), custom_call_target="tpu_custom_call" | custom-call | tf_op jit(solution)/shard_map/pallas_call | solution.py:649
  36.2 0.4 collective-permute-done.6.refs_0_
  36.6 0.0 collective-permute-start.7
  36.7 1.2 %collective-permute-start.8 = (f32[32,256]{1,0:T(8,128)S(1)}, f32[32,256]{1,0:T(8,128)S(1)}, u32[]{:S(2)}, u32[]{:S(2)}) collective-permute-start(f32[32,256]{1,0:T(8,128)S(1)} %get-tuple-element.49), channel_id=1, source_target_pairs={{0,1},{1,0},{2,4},{3,5},{4,2},{5,3},{6,8},{7,9},{8,6},{9,7},{10,12... | collective-permute-start | bytes 98312 | tf_op jit(solution)/shard_map/ppermute | solution.py:43
  37.9 2.4 %shard_map.101.refs_2_ = f32[3,48,256]{2,1,0:T(8,128)S(1)} custom-call(bf16[1024,256]{1,0:T(8,128)(2,1)S(1)} %get-tuple-element.44.slope_ref, f32[2,64,256]{2,1,0:T(8,128)S(1)} %shard_map.94.after_ref.order_ref, s32[4,128]{1,0:T(4,128)S(1)} %get-tuple-element.46.unit_ref), custom_call_target="tpu_custom_call" | custom-call | tf_op jit(solution)/shard_map/pallas_call | solution.py:649
  40.3 0.0 collective-permute-done.7.backa_ref
  40.3 0.4 collective-permute-done.8.backb_ref
  40.6 3.6 %shard_map.102 = f32[2,16384]{1,0:T(2,128)} custom-call(f32[32,256]{1,0:T(8,128)S(1)} %collective-permute-done.7.backa_ref, f32[32,256]{1,0:T(8,128)S(1)} %collective-permute-done.8.backb_ref, f32[48,256]{1,0:T(8,128)S(1)} %collective-permute-done.6.refs_0_, f32[1,48,256]{2,1,0:T(8,128)S(1)} %shard_map.98.after_ref.refs_1_, ...), custom_call_target="tpu_custom_call" | custom-call | tf_op jit(solution)/shard_map/pallas_call | solution.py:649
  (1 shorter events, 0.0 us)
Async XLA Ops:
  5.5 6.5 %collective-permute-start = (f32[112,256]{1,0:T(8,128)S(1)}, f32[112,256]{1,0:T(8,128)S(1)}, u32[]{:S(2)}, u32[]{:S(2)}) collective-permute-start(f32[112,256]{1,0:T(8,128)S(1)} %get-tuple-element.29), channel_id=1, source_target_pairs={{0,2},{1,3},{2,0},{3,1},{4,6},{5,7},{6,4},{7,5},{8,10},{9,11},{10,... | collective-permute-start | bytes 344072 | tf_op jit(solution)/shard_map/ppermute | solution.py:43
  6.0 6.0 %collective-permute-start.1 = (f32[112,256]{1,0:T(8,128)S(1)}, f32[112,256]{1,0:T(8,128)S(1)}, u32[]{:S(2)}, u32[]{:S(2)}) collective-permute-start(f32[112,256]{1,0:T(8,128)S(1)} %get-tuple-element.30), channel_id=1, source_target_pairs={{0,1},{1,0},{2,4},{3,5},{4,2},{5,3},{6,8},{7,9},{8,6},{9,7},{10,12... | collective-permute-start | bytes 344072 | tf_op jit(solution)/shard_map/ppermute | solution.py:43
  8.6 3.5 %copy-start = (f32[8,32,256]{2,1,0:T(8,128)S(1)}, f32[8,32,256]{2,1,0:T(8,128)}, u32[]{:S(2)}) copy-start(f32[8,32,256]{2,1,0:T(8,128)} %cond_ref.3) | copy-start | bytes 786436
  12.2 5.3 %collective-permute-start.2 = (f32[88,256]{1,0:T(8,128)S(1)}, f32[88,256]{1,0:T(8,128)S(1)}, u32[]{:S(2)}, u32[]{:S(2)}) collective-permute-start(f32[88,256]{1,0:T(8,128)S(1)} %shard_map.90), channel_id=1, source_target_pairs={{0,1},{1,0},{2,3},{3,2},{4,5},{5,4},{6,7},{7,6},{8,9},{9,8},{10,11... | collective-permute-start | bytes 270344 | tf_op jit(solution)/shard_map/ppermute | solution.py:43
  18.6 4.6 %collective-permute-start.3 = (f32[8,8,256]{2,1,0:T(8,128)S(1)}, f32[8,8,256]{2,1,0:T(8,128)S(1)}, u32[]{:S(2)}, u32[]{:S(2)}) collective-permute-start(f32[8,8,256]{2,1,0:T(8,128)S(1)} %get-tuple-element.35), channel_id=1, source_target_pairs={{0,2},{1,3},{2,0},{3,1},{4,6},{5,7},{6,4},{7,5},{8,10},{9,11},{10,... | collective-permute-start | bytes 196616 | tf_op jit(solution)/shard_map/ppermute | solution.py:43
  18.7 4.6 %collective-permute-start.4 = (f32[8,8,256]{2,1,0:T(8,128)S(1)}, f32[8,8,256]{2,1,0:T(8,128)S(1)}, u32[]{:S(2)}, u32[]{:S(2)}) collective-permute-start(f32[8,8,256]{2,1,0:T(8,128)S(1)} %get-tuple-element.36), channel_id=1, source_target_pairs={{0,1},{1,0},{2,4},{3,5},{4,2},{5,3},{6,8},{7,9},{8,6},{9,7},{10,12... | collective-permute-start | bytes 196616 | tf_op jit(solution)/shard_map/ppermute | solution.py:43
  23.2 1.4 %copy-start.1 = (f32[7]{0:T(128)S(1)}, f32[7]{0:T(128)}, u32[]{:S(2)}) copy-start(f32[7]{0:T(128)} %coupling_ref.1) | copy-start | bytes 88
  23.4 3.8 %collective-permute-start.5 = (f32[16,256]{1,0:T(8,128)S(1)}, f32[16,256]{1,0:T(8,128)S(1)}, u32[]{:S(2)}, u32[]{:S(2)}) collective-permute-start(f32[16,256]{1,0:T(8,128)S(1)} %shard_map.95), channel_id=1, source_target_pairs={{0,1},{1,0},{2,3},{3,2},{4,5},{5,4},{6,7},{7,6},{8,9},{9,8},{10,11... | collective-permute-start | bytes 49160 | tf_op jit(solution)/shard_map/ppermute | solution.py:43
  32.5 4.2 %collective-permute-start.6 = (f32[48,256]{1,0:T(8,128)S(1)}, f32[48,256]{1,0:T(8,128)S(1)}, u32[]{:S(2)}, u32[]{:S(2)}) collective-permute-start(f32[48,256]{1,0:T(8,128)S(1)} %shard_map.99), channel_id=1, source_target_pairs={{0,1},{1,0},{2,3},{3,2},{4,5},{5,4},{6,7},{7,6},{8,9},{9,8},{10,11... | collective-permute-start | bytes 147464 | tf_op jit(solution)/shard_map/ppermute | solution.py:43
  36.6 3.6 %collective-permute-start.7 = (f32[32,256]{1,0:T(8,128)S(1)}, f32[32,256]{1,0:T(8,128)S(1)}, u32[]{:S(2)}, u32[]{:S(2)}) collective-permute-start(f32[32,256]{1,0:T(8,128)S(1)} %get-tuple-element.48), channel_id=1, source_target_pairs={{0,2},{1,3},{2,0},{3,1},{4,6},{5,7},{6,4},{7,5},{8,10},{9,11},{10,... | collective-permute-start | bytes 98312 | tf_op jit(solution)/shard_map/ppermute | solution.py:43
  36.7 4.0 %collective-permute-start.8 = (f32[32,256]{1,0:T(8,128)S(1)}, f32[32,256]{1,0:T(8,128)S(1)}, u32[]{:S(2)}, u32[]{:S(2)}) collective-permute-start(f32[32,256]{1,0:T(8,128)S(1)} %get-tuple-element.49), channel_id=1, source_target_pairs={{0,1},{1,0},{2,4},{3,5},{4,2},{5,3},{6,8},{7,9},{8,6},{9,7},{10,12... | collective-permute-start | bytes 98312 | tf_op jit(solution)/shard_map/ppermute | solution.py:43

commit v9 on v8

--- a/solution.py
+++ b/solution.py
@@ -590,6 +590,13 @@
     lax.fori_loop(0, out_ref.shape[0], body, 0)
 
 
+def late_gather_kernel(layers, start, slope_ref, order_ref, unit_ref, value_ref, out_ref, value_hbm, sem):
+    copy = pltpu.make_async_copy(value_ref, value_hbm, sem)
+    copy.start()
+    stay_gather_kernel(layers, start, slope_ref, order_ref, unit_ref, out_ref)
+    copy.wait()
+
+
 def reply_kernel(nyc, near_ref, after_ref, *refs):
     size = 2 * GROUP
     backs, (a_ref, b_ref) = refs[: nyc - 1], refs[nyc - 1 :]
@@ -642,15 +649,16 @@
     lax.fori_loop(0, late_ref.shape[0], functools.partial(body, late_ref, early), 0)
 
 
-def call(kernel, outs, scratch, *args, spaces={}):
-    space = pl.BlockSpec(memory_space=pltpu.VMEM)
+def call(kernel, outs, scratch, *args, spaces={}, out_spaces={}):
     specs = [pl.BlockSpec(memory_space=spaces.get(i, pltpu.VMEM)) for i in range(len(args))]
     shapes = [jax.ShapeDtypeStruct(shape, dtype) for shape, dtype in outs]
     return pl.pallas_call(
         kernel,
         out_shape=shapes,
         in_specs=specs,
-        out_specs=[space] * len(shapes),
+        out_specs=[
+            pl.BlockSpec(memory_space=out_spaces.get(i, pltpu.VMEM)) for i in range(len(shapes))
+        ],
         scratch_shapes=scratch,
         compiler_params=pltpu.CompilerParams(vmem_limit_bytes=48 * 1024 * 1024),
     )(*args)
@@ -756,7 +764,7 @@
         conductivity, recv_a, recv_b, layer_coupling, *recv_y,
         spaces={3: pltpu.SMEM},
     )
-    final_warmth, slope = call(
+    warmth, slope = call(
         partial(solve_kernel, nyc),
         [(tile, F32), ((4 * count, rows), BF16)],
         [vmem(*big), vmem(2, layers, big[1] + 16, big[2]), vmem(*big)],
@@ -782,18 +790,13 @@
     )
     blocks, early = square[0] // BLOCK, 1
     units = order.shape[1] // blocks + layers
-    stay_values = [
-        functools.partial(
-            call,
-            partial(stay_gather_kernel, layers, start),
-            [((size, 2 * units, WIDE), F32)],
-            [],
-            slope, order, unit,
-            spaces={2: pltpu.SMEM},
-        )
-        for start, size in ((0, early), (early, blocks - early))
-    ]
-    (early_value,) = stay_values[0]()
+    (early_value,) = call(
+        partial(stay_gather_kernel, layers, 0),
+        [((early, 2 * units, WIDE), F32)],
+        [],
+        slope, order, unit,
+        spaces={2: pltpu.SMEM},
+    )
     answer_a, answer_b = call(
         partial(reply_kernel, nyc),
         [((2 * nyc * GROUP, WIDE), F32)] * 2,
@@ -802,7 +805,14 @@
         spaces={1: pl.ANY},
     )
     back_a, back_b = exchange(answer_a, 1, 0), exchange(answer_b, 2, 0)
-    (late_value,) = stay_values[1]()
+    late_value, final_warmth = call(
+        partial(late_gather_kernel, layers, early),
+        [((blocks - early, 2 * units, WIDE), F32), (tile, F32)],
+        [pltpu.SemaphoreType.DMA(())],
+        slope, order, unit, warmth,
+        spaces={2: pltpu.SMEM},
+        out_spaces={1: pltpu.HBM},
+    )
     (pull,) = call(
         partial(unpack_kernel, nyc),
         [((2, cells), F32)],

time: 44.4 us -> 43.8 us (0.986)
  Pallas kernels: 32.4 us -> 31.8 us
    pallas_call x17, Pallas kernels: 32.4 us -> 31.8 us  [call(): pl.pallas_call(kernel, out_shape=shapes, in_specs=specs, out_specs=[pl.Bl...]
  transfers between devices with their start and end apart: 9 -> 9, of which waited for: 3 -> 3; matrix products, arithmetic and copies ran while one was open for 0% -> 0% of each run, Pallas kernels for 39% -> 40%
where the time goes in v9:
time: 43.8 us; the launch traced here: 43.6 us
  Pallas kernels  31.8 us (73%)
  starting transfers between devices  9.11 us (21%)
  waiting for transfers between devices  1.91 us (4%)
  between operations  0.8 us (2%)
    pallas_call x17, Pallas kernels, call(): pl.pallas_call(kernel, out_shape=shapes, in_specs=specs, out_specs=[pl.Bl...  31.8 us
    ppermute x9, starting transfers between devices, exchange(): return lax.ppermute(value, ('gx', 'gy'), pairs)  9.11 us
    ppermute x9, waiting for transfers between devices, exchange(): return lax.ppermute(value, ('gx', 'gy'), pairs)  1.91 us
  transfers between devices with their start and end apart: 9, of which 3 were waited for; matrix products, arithmetic and copies ran while one was open for 0% of the time, Pallas kernels for 40%

profile of v9, /device:TPU:0, one launch (start us, length us, event | category | flops | bytes accessed | tf_op | source)
XLA Modules:
  0.0 43.6 jit_solution(5622426842607678820)
XLA Ops:
  0.6 4.9 %shard_map.86 = (f32[112,256]{1,0:T(8,128)S(1)}, f32[112,256]{1,0:T(8,128)S(1)}, f32[24,256]{1,0:T(8,128)S(1)}, f32[128,128]{1,0:T(8,128)S(1)}, f32[6,128,128]{2,1,0:T(8,128)S(1)}, /*index=5*/f32[128,128]{1,0:T(8,128)S(1)}) custom-call(s32[128,128]{1,0:T(8,128)} %bitcast.5, s32[128,128]{1,0:T(8,128)} %bitcast.6, s32[128,128]{1,0:T(8,128)} %bitcast.7, ...), custom_call_target="tpu_custom_call" | custom-call | tf_op jit(solution)/shard_map/pallas_call | solution.py:655
  5.5 0.5 %collective-permute-start = (f32[112,256]{1,0:T(8,128)S(1)}, f32[112,256]{1,0:T(8,128)S(1)}, u32[]{:S(2)}, u32[]{:S(2)}) collective-permute-start(f32[112,256]{1,0:T(8,128)S(1)} %get-tuple-element.31), channel_id=1, source_target_pairs={{0,2},{1,3},{2,0},{3,1},{4,6},{5,7},{6,4},{7,5},{8,10},{9,11},{10,... | collective-permute-start | bytes 344072 | tf_op jit(solution)/shard_map/ppermute | solution.py:43
  6.0 2.6 %collective-permute-start.1 = (f32[112,256]{1,0:T(8,128)S(1)}, f32[112,256]{1,0:T(8,128)S(1)}, u32[]{:S(2)}, u32[]{:S(2)}) collective-permute-start(f32[112,256]{1,0:T(8,128)S(1)} %get-tuple-element.32), channel_id=1, source_target_pairs={{0,1},{1,0},{2,4},{3,5},{4,2},{5,3},{6,8},{7,9},{8,6},{9,7},{10,12... | collective-permute-start | bytes 344072 | tf_op jit(solution)/shard_map/ppermute | solution.py:43
  8.6 0.0 copy-start
  8.6 3.4 %shard_map.87.stay_ref.after_ref = f32[512,256]{1,0:T(8,128)S(1)} custom-call(f32[6,128,128]{2,1,0:T(8,128)S(1)} %get-tuple-element.29.field_ref, f32[128,128]{1,0:T(8,128)S(1)} %get-tuple-element.30.slot_ref), custom_call_target="tpu_custom_call" | custom-call | tf_op jit(solution)/shard_map/pallas_call | solution.py:655
  12.0 0.0 collective-permute-done.recva_ref.refs_0_
  12.1 0.0 collective-permute-done.1.recvb_ref.refs_1_
  12.1 0.0 copy-done
  12.1 0.1 shard_map.90
  12.2 1.4 %collective-permute-start.2 = (f32[88,256]{1,0:T(8,128)S(1)}, f32[88,256]{1,0:T(8,128)S(1)}, u32[]{:S(2)}, u32[]{:S(2)}) collective-permute-start(f32[88,256]{1,0:T(8,128)S(1)} %shard_map.90), channel_id=1, source_target_pairs={{0,1},{1,0},{2,3},{3,2},{4,5},{5,4},{6,7},{7,6},{8,9},{9,8},{10,11... | collective-permute-start | bytes 270344 | tf_op jit(solution)/shard_map/ppermute | solution.py:43
  13.6 2.4 %shard_map.88 = (f32[512,256]{1,0:T(8,128)S(1)}, s32[8,128]{1,0:T(8,128)S(1)}) custom-call(f32[512,256]{1,0:T(8,128)S(1)} %shard_map.87.stay_ref.after_ref, f32[112,256]{1,0:T(8,128)S(1)} %collective-permute-done.recva_ref.refs_0_, f32[112,256]{1,0:T(8,128)S(1)} %collective-permute-done.1.recvb_ref.refs_1_, f32[6,128,128]{2,1,0:T(8,128)S(1)} %get-tuple-element.29.field_ref, ...), custom_call_target="tpu_custom_call" | custom-call | tf_op jit(solution)/shard_map/pallas_call | solution.py:655
  16.0 1.5 %shard_map.89 = (f32[128,128]{1,0:T(8,128)S(1)}, s32[4,128]{1,0:T(4,128)S(1)}, f32[128,128]{1,0:T(8,128)S(1)}, f32[128,128]{1,0:T(8,128)S(1)}) custom-call(f32[6,128,128]{2,1,0:T(8,128)S(1)} %get-tuple-element.29.field_ref, f32[128,128]{1,0:T(8,128)S(1)} %get-tuple-element.30.slot_ref, f32[512,256]{1,0:T(8,128)S(1)} %get-tuple-element.33.after_ref.near_ref), custom_call_target="tpu_custom_call" | custom-call | tf_op jit(solution)/shard_map/pallas_call | solution.py:655
  17.5 0.0 collective-permute-done.2.refs_0_
  17.5 1.1 %shard_map.91 = (f32[8,16,256]{2,1,0:T(8,128)S(1)}, f32[8,8,256]{2,1,0:T(8,128)S(1)}, f32[8,8,256]{2,1,0:T(8,128)S(1)}) custom-call(f32[512,256]{1,0:T(8,128)S(1)} %get-tuple-element.33.after_ref.near_ref, f32[128,128]{1,0:T(8,128)S(1)} %get-tuple-element.34.after_ref.row_ref, f32[88,256]{1,0:T(8,128)S(1)} %collective-permute-done.2.refs_0_), custom_call_target="tpu_custom_call" | custom-call | tf_op jit(solution)/shard_map/pallas_call | solution.py:655
  18.6 0.1 collective-permute-start.3
  18.7 0.9 %collective-permute-start.4 = (f32[8,8,256]{2,1,0:T(8,128)S(1)}, f32[8,8,256]{2,1,0:T(8,128)S(1)}, u32[]{:S(2)}, u32[]{:S(2)}) collective-permute-start(f32[8,8,256]{2,1,0:T(8,128)S(1)} %get-tuple-element.38), channel_id=1, source_target_pairs={{0,1},{1,0},{2,4},{3,5},{4,2},{5,3},{6,8},{7,9},{8,6},{9,7},{10,12... | collective-permute-start | bytes 196616 | tf_op jit(solution)/shard_map/ppermute | solution.py:43
  19.6 1.1 %shard_map.92.after_ref.grid_ref = f32[8,32,256]{2,1,0:T(8,128)S(1)} custom-call(f32[512,256]{1,0:T(8,128)S(1)} %get-tuple-element.33.after_ref.near_ref, f32[8,16,256]{2,1,0:T(8,128)S(1)} %get-tuple-element.36.outer_ref, f32[88,256]{1,0:T(8,128)S(1)} %collective-permute-done.2.refs_0_), custom_call_target="tpu_custom_call" | custom-call | tf_op jit(solution)/shard_map/pallas_call | solution.py:655
  20.7 2.5 %shard_map.94.after_ref.order_ref = f32[2,64,256]{2,1,0:T(8,128)S(1)} custom-call(f32[6,128,128]{2,1,0:T(8,128)S(1)} %get-tuple-element.29.field_ref, f32[128,128]{1,0:T(8,128)S(1)} %get-tuple-element.34.after_ref.row_ref, f32[128,128]{1,0:T(8,128)S(1)} %get-tuple-element.44.lam_ref, f32[8,32,256]{2,1,0:T(8,128)S(1)} %shard_map.92.after_ref.grid_ref), custom_call_target="tpu_custom_call" | custom-call | tf_op jit(solution)/shard_map/pallas_call | solution.py:655
  23.2 0.0 copy-start.1
  23.2 0.0 collective-permute-done.3.froma_ref
  23.3 0.0 collective-permute-done.4.fromb_ref
  23.3 0.1 shard_map.95
  23.4 1.2 %collective-permute-start.5 = (f32[16,256]{1,0:T(8,128)S(1)}, f32[16,256]{1,0:T(8,128)S(1)}, u32[]{:S(2)}, u32[]{:S(2)}) collective-permute-start(f32[16,256]{1,0:T(8,128)S(1)} %shard_map.95), channel_id=1, source_target_pairs={{0,1},{1,0},{2,3},{3,2},{4,5},{5,4},{6,7},{7,6},{8,9},{9,8},{10,11... | collective-permute-start | bytes 49160 | tf_op jit(solution)/shard_map/ppermute | solution.py:43
  24.6 0.0 copy-done.1
  24.6 1.5 %shard_map.93 = (f32[8,48,384]{2,1,0:T(8,128)S(1)}, f32[8,48,384]{2,1,0:T(8,128)S(1)}, f32[8,48,384]{2,1,0:T(8,128)S(1)}, f32[8,48,384]{2,1,0:T(8,128)S(1)}, f32...) custom-call(f32[8,32,256]{2,1,0:T(8,128)S(1)} %copy-done, f32[112,256]{1,0:T(8,128)S(1)} %collective-permute-done.recva_ref.refs_0_, ...), custom_call_target="tpu_custom_call" | custom-call | tf_op jit(solution)/shard_map/pallas_call | solution.py:655
  26.1 1.1 %collective-permute-done.5.refs_0_ = f32[16,256]{1,0:T(8,128)S(1)} collective-permute-done((f32[16,256]{1,0:T(8,128)S(1)}, f32[16,256]{1,0:T(8,128)S(1)}, u32[]{:S(2)}, u32[]{:S(2)}) %collective-permute-start.5) | collective-permute-done | bytes 16416 | tf_op jit(solution)/shard_map/ppermute | solution.py:43
  27.2 3.0 %shard_map.96 = (f32[8,32,256]{2,1,0:T(8,128)S(1)}, bf16[1024,256]{1,0:T(8,128)(2,1)S(1)}) custom-call(f32[8,32,256]{2,1,0:T(8,128)S(1)} %shard_map.92.after_ref.grid_ref, f32[8,8,256]{2,1,0:T(8,128)S(1)} %collective-permute-done.3.froma_ref, f32[8,8,256]{2,1,0:T(8,128)S(1)} %collective-permute-done.4.fromb_ref, f32[8,48,384]{2,1,0:T(8,128)S(1)} %get-tuple-element.39.cn_ref, ...), custom_call_target="tpu_custom_call" | custom-call | tf_op jit(solution)/shard_map/pallas_call | solution.py:655
  30.2 1.7 %shard_map.100 = f32[48,256]{1,0:T(8,128)S(1)} custom-call(bf16[1024,256]{1,0:T(8,128)(2,1)S(1)} %get-tuple-element.45.slope_ref, s32[8,128]{1,0:T(8,128)S(1)} %get-tuple-element.50.unit_ref, f32[88,256]{1,0:T(8,128)S(1)} %collective-permute-done.2.refs_0_), custom_call_target="tpu_custom_call" | custom-call | tf_op jit(solution)/shard_map/pallas_call | solution.py:655
  31.9 1.2 %collective-permute-start.6 = (f32[48,256]{1,0:T(8,128)S(1)}, f32[48,256]{1,0:T(8,128)S(1)}, u32[]{:S(2)}, u32[]{:S(2)}) collective-permute-start(f32[48,256]{1,0:T(8,128)S(1)} %shard_map.100), channel_id=1, source_target_pairs={{0,1},{1,0},{2,3},{3,2},{4,5},{5,4},{6,7},{7,6},{8,9},{9,8},{10,11... | collective-permute-start | bytes 147464 | tf_op jit(solution)/shard_map/ppermute | solution.py:43
  33.1 1.2 %shard_map.99.after_ref.refs_1_ = f32[1,48,256]{2,1,0:T(8,128)S(1)} custom-call(bf16[1024,256]{1,0:T(8,128)(2,1)S(1)} %get-tuple-element.45.slope_ref, f32[2,64,256]{2,1,0:T(8,128)S(1)} %shard_map.94.after_ref.order_ref, s32[4,128]{1,0:T(4,128)S(1)} %get-tuple-element.46.unit_ref), custom_call_target="tpu_custom_call" | custom-call | tf_op jit(solution)/shard_map/pallas_call | solution.py:655
  34.2 1.4 %shard_map.98.near_ref = f32[32,256]{1,0:T(8,128)S(1)} custom-call(bf16[1024,256]{1,0:T(8,128)(2,1)S(1)} %get-tuple-element.45.slope_ref, s32[8,128]{1,0:T(8,128)S(1)} %get-tuple-element.49.unit_ref, f32[112,256]{1,0:T(8,128)S(1)} %collective-permute-done.recva_ref.refs_0_, f32[112,256]{1,0:T(8,128)S(1)} %collective-permute-done.1.recvb_ref.refs_1_), custom_call_target="tpu_custom_call" | custom-call | tf_op jit(solution)/shard_map/pallas_call | solution.py:655
  35.6 0.4 collective-permute-done.6.refs_0_
  36.0 0.0 collective-permute-start.7
  36.0 1.2 %collective-permute-start.8 = (f32[32,256]{1,0:T(8,128)S(1)}, f32[32,256]{1,0:T(8,128)S(1)}, u32[]{:S(2)}, u32[]{:S(2)}) collective-permute-start(f32[32,256]{1,0:T(8,128)S(1)} %get-tuple-element.52), channel_id=1, source_target_pairs={{0,1},{1,0},{2,4},{3,5},{4,2},{5,3},{6,8},{7,9},{8,6},{9,7},{10,12... | collective-permute-start | bytes 98312 | tf_op jit(solution)/shard_map/ppermute | solution.py:43
  37.2 2.4 %shard_map.97 = (f32[3,48,256]{2,1,0:T(8,128)S(1)}, f32[8,32,256]{2,1,0:T(8,128)}) custom-call(bf16[1024,256]{1,0:T(8,128)(2,1)S(1)} %get-tuple-element.45.slope_ref, f32[2,64,256]{2,1,0:T(8,128)S(1)} %shard_map.94.after_ref.order_ref, s32[4,128]{1,0:T(4,128)S(1)} %get-tuple-element.46.unit_ref, f32[8,32,256]{2,1,0:T(8,128)S(1)} %get-tuple-element.47.value_ref), custom_call_target="tpu_custom_call" | custom-call | tf_op jit(solution)/shard_map/pallas_call | solution.py:655
  39.6 0.0 collective-permute-done.7.backa_ref
  39.7 0.4 collective-permute-done.8.backb_ref
  40.0 3.6 %shard_map.102 = f32[2,16384]{1,0:T(2,128)} custom-call(f32[32,256]{1,0:T(8,128)S(1)} %collective-permute-done.7.backa_ref, f32[32,256]{1,0:T(8,128)S(1)} %collective-permute-done.8.backb_ref, f32[48,256]{1,0:T(8,128)S(1)} %collective-permute-done.6.refs_0_, f32[1,48,256]{2,1,0:T(8,128)S(1)} %shard_map.99.after_ref.refs_1_, ...), custom_call_target="tpu_custom_call" | custom-call | tf_op jit(solution)/shard_map/pallas_call | solution.py:655
  (1 shorter events, 0.0 us)
Async XLA Ops:
  5.5 6.5 %collective-permute-start = (f32[112,256]{1,0:T(8,128)S(1)}, f32[112,256]{1,0:T(8,128)S(1)}, u32[]{:S(2)}, u32[]{:S(2)}) collective-permute-start(f32[112,256]{1,0:T(8,128)S(1)} %get-tuple-element.31), channel_id=1, source_target_pairs={{0,2},{1,3},{2,0},{3,1},{4,6},{5,7},{6,4},{7,5},{8,10},{9,11},{10,... | collective-permute-start | bytes 344072 | tf_op jit(solution)/shard_map/ppermute | solution.py:43
  6.0 6.0 %collective-permute-start.1 = (f32[112,256]{1,0:T(8,128)S(1)}, f32[112,256]{1,0:T(8,128)S(1)}, u32[]{:S(2)}, u32[]{:S(2)}) collective-permute-start(f32[112,256]{1,0:T(8,128)S(1)} %get-tuple-element.32), channel_id=1, source_target_pairs={{0,1},{1,0},{2,4},{3,5},{4,2},{5,3},{6,8},{7,9},{8,6},{9,7},{10,12... | collective-permute-start | bytes 344072 | tf_op jit(solution)/shard_map/ppermute | solution.py:43
  8.6 3.5 %copy-start = (f32[8,32,256]{2,1,0:T(8,128)S(1)}, f32[8,32,256]{2,1,0:T(8,128)}, u32[]{:S(2)}) copy-start(f32[8,32,256]{2,1,0:T(8,128)} %cond_ref.3) | copy-start | bytes 786436
  12.2 5.3 %collective-permute-start.2 = (f32[88,256]{1,0:T(8,128)S(1)}, f32[88,256]{1,0:T(8,128)S(1)}, u32[]{:S(2)}, u32[]{:S(2)}) collective-permute-start(f32[88,256]{1,0:T(8,128)S(1)} %shard_map.90), channel_id=1, source_target_pairs={{0,1},{1,0},{2,3},{3,2},{4,5},{5,4},{6,7},{7,6},{8,9},{9,8},{10,11... | collective-permute-start | bytes 270344 | tf_op jit(solution)/shard_map/ppermute | solution.py:43
  18.6 4.6 %collective-permute-start.3 = (f32[8,8,256]{2,1,0:T(8,128)S(1)}, f32[8,8,256]{2,1,0:T(8,128)S(1)}, u32[]{:S(2)}, u32[]{:S(2)}) collective-permute-start(f32[8,8,256]{2,1,0:T(8,128)S(1)} %get-tuple-element.37), channel_id=1, source_target_pairs={{0,2},{1,3},{2,0},{3,1},{4,6},{5,7},{6,4},{7,5},{8,10},{9,11},{10,... | collective-permute-start | bytes 196616 | tf_op jit(solution)/shard_map/ppermute | solution.py:43
  18.7 4.6 %collective-permute-start.4 = (f32[8,8,256]{2,1,0:T(8,128)S(1)}, f32[8,8,256]{2,1,0:T(8,128)S(1)}, u32[]{:S(2)}, u32[]{:S(2)}) collective-permute-start(f32[8,8,256]{2,1,0:T(8,128)S(1)} %get-tuple-element.38), channel_id=1, source_target_pairs={{0,1},{1,0},{2,4},{3,5},{4,2},{5,3},{6,8},{7,9},{8,6},{9,7},{10,12... | collective-permute-start | bytes 196616 | tf_op jit(solution)/shard_map/ppermute | solution.py:43
  23.2 1.4 %copy-start.1 = (f32[7]{0:T(128)S(1)}, f32[7]{0:T(128)}, u32[]{:S(2)}) copy-start(f32[7]{0:T(128)} %coupling_ref.1) | copy-start | bytes 88
  23.4 3.8 %collective-permute-start.5 = (f32[16,256]{1,0:T(8,128)S(1)}, f32[16,256]{1,0:T(8,128)S(1)}, u32[]{:S(2)}, u32[]{:S(2)}) collective-permute-start(f32[16,256]{1,0:T(8,128)S(1)} %shard_map.95), channel_id=1, source_target_pairs={{0,1},{1,0},{2,3},{3,2},{4,5},{5,4},{6,7},{7,6},{8,9},{9,8},{10,11... | collective-permute-start | bytes 49160 | tf_op jit(solution)/shard_map/ppermute | solution.py:43
  31.9 4.2 %collective-permute-start.6 = (f32[48,256]{1,0:T(8,128)S(1)}, f32[48,256]{1,0:T(8,128)S(1)}, u32[]{:S(2)}, u32[]{:S(2)}) collective-permute-start(f32[48,256]{1,0:T(8,128)S(1)} %shard_map.100), channel_id=1, source_target_pairs={{0,1},{1,0},{2,3},{3,2},{4,5},{5,4},{6,7},{7,6},{8,9},{9,8},{10,11... | collective-permute-start | bytes 147464 | tf_op jit(solution)/shard_map/ppermute | solution.py:43
  36.0 3.6 %collective-permute-start.7 = (f32[32,256]{1,0:T(8,128)S(1)}, f32[32,256]{1,0:T(8,128)S(1)}, u32[]{:S(2)}, u32[]{:S(2)}) collective-permute-start(f32[32,256]{1,0:T(8,128)S(1)} %get-tuple-element.51), channel_id=1, source_target_pairs={{0,2},{1,3},{2,0},{3,1},{4,6},{5,7},{6,4},{7,5},{8,10},{9,11},{10,... | collective-permute-start | bytes 98312 | tf_op jit(solution)/shard_map/ppermute | solution.py:43
  36.0 4.0 %collective-permute-start.8 = (f32[32,256]{1,0:T(8,128)S(1)}, f32[32,256]{1,0:T(8,128)S(1)}, u32[]{:S(2)}, u32[]{:S(2)}) collective-permute-start(f32[32,256]{1,0:T(8,128)S(1)} %get-tuple-element.52), channel_id=1, source_target_pairs={{0,1},{1,0},{2,4},{3,5},{4,2},{5,3},{6,8},{7,9},{8,6},{9,7},{10,12... | collective-permute-start | bytes 98312 | tf_op jit(solution)/shard_map/ppermute | solution.py:43

commit v10 on v9

--- a/solution.py
+++ b/solution.py
@@ -214,7 +214,7 @@
 
 
 def deposit_stays(grid_ref, field_ref, slot_ref, first, last, cols):
-    count, step = grid_ref.shape[0] // 2, 32
+    count, step = grid_ref.shape[0] // 2, last - first
     stays = slot_ref[first:last, :] < 0.0
     vals = [jnp.where(stays, field_ref[2 + f, first:last, :], 0.0) for f in range(4)]
     lcs, rs = field_ref[0, first:last, :], field_ref[1, first:last, :]
@@ -676,7 +676,7 @@
     bins, layer, off = flat(cell_bin), flat(cell_layer), flat(cell_offset)
     power, spill = flat(cell_power), flat(spill_weight)
     square = bins.shape
-    split = square[0] * 3 // 4
+    split = square[0] * 13 // 16
     own = 3 * GROUP
     message = (nyc * own + layers * HALO, WIDE)
     vmem = lambda *shape: pltpu.VMEM(shape, F32)

time: 43.8 us -> 44.1 us (level)
  waiting for transfers between devices: 1.91 us -> 2.89 us
  starting transfers between devices: 9.11 us -> 8.39 us
    ppermute x9, waiting for transfers between devices: 1.91 us -> 2.89 us  [exchange(): return lax.ppermute(value, ('gx', 'gy'), pairs)]
    ppermute x9, starting transfers between devices: 9.11 us -> 8.39 us  [exchange(): return lax.ppermute(value, ('gx', 'gy'), pairs)]
where the time goes in v10:
time: 44.1 us; the launch traced here: 43.9 us
  Pallas kernels  31.8 us (72%)
  starting transfers between devices  8.39 us (19%)
  waiting for transfers between devices  2.89 us (7%)
  between operations  0.8 us (2%)
    pallas_call x17, Pallas kernels, call(): pl.pallas_call(kernel, out_shape=shapes, in_specs=specs, out_specs=[pl.Bl...  31.8 us
    ppermute x9, starting transfers between devices, exchange(): return lax.ppermute(value, ('gx', 'gy'), pairs)  8.39 us
    ppermute x9, waiting for transfers between devices, exchange(): return lax.ppermute(value, ('gx', 'gy'), pairs)  2.89 us
  transfers between devices with their start and end apart: 9, of which 3 were waited for; matrix products, arithmetic and copies ran while one was open for 0% of the time, Pallas kernels for 40%

profile of v10, /device:TPU:0, one launch (start us, length us, event | category | flops | bytes accessed | tf_op | source)
XLA Modules:
  0.0 43.9 jit_solution(3491068213165037982)
XLA Ops:
  0.6 4.9 %shard_map.86 = (f32[112,256]{1,0:T(8,128)S(1)}, f32[112,256]{1,0:T(8,128)S(1)}, f32[24,256]{1,0:T(8,128)S(1)}, f32[128,128]{1,0:T(8,128)S(1)}, f32[6,128,128]{2,1,0:T(8,128)S(1)}, /*index=5*/f32[128,128]{1,0:T(8,128)S(1)}) custom-call(s32[128,128]{1,0:T(8,128)} %bitcast.5, s32[128,128]{1,0:T(8,128)} %bitcast.6, s32[128,128]{1,0:T(8,128)} %bitcast.7, ...), custom_call_target="tpu_custom_call" | custom-call | tf_op jit(solution)/shard_map/pallas_call | solution.py:655
  5.5 0.5 %collective-permute-start = (f32[112,256]{1,0:T(8,128)S(1)}, f32[112,256]{1,0:T(8,128)S(1)}, u32[]{:S(2)}, u32[]{:S(2)}) collective-permute-start(f32[112,256]{1,0:T(8,128)S(1)} %get-tuple-element.31), channel_id=1, source_target_pairs={{0,2},{1,3},{2,0},{3,1},{4,6},{5,7},{6,4},{7,5},{8,10},{9,11},{10,... | collective-permute-start | bytes 344072 | tf_op jit(solution)/shard_map/ppermute | solution.py:43
  6.0 2.6 %collective-permute-start.1 = (f32[112,256]{1,0:T(8,128)S(1)}, f32[112,256]{1,0:T(8,128)S(1)}, u32[]{:S(2)}, u32[]{:S(2)}) collective-permute-start(f32[112,256]{1,0:T(8,128)S(1)} %get-tuple-element.32), channel_id=1, source_target_pairs={{0,1},{1,0},{2,4},{3,5},{4,2},{5,3},{6,8},{7,9},{8,6},{9,7},{10,12... | collective-permute-start | bytes 344072 | tf_op jit(solution)/shard_map/ppermute | solution.py:43
  8.6 0.0 copy-start
  8.6 3.7 %shard_map.87.stay_ref.after_ref = f32[512,256]{1,0:T(8,128)S(1)} custom-call(f32[6,128,128]{2,1,0:T(8,128)S(1)} %get-tuple-element.29.field_ref, f32[128,128]{1,0:T(8,128)S(1)} %get-tuple-element.30.slot_ref), custom_call_target="tpu_custom_call" | custom-call | tf_op jit(solution)/shard_map/pallas_call | solution.py:655
  12.3 0.0 collective-permute-done.recva_ref.refs_0_
  12.3 0.0 collective-permute-done.1.recvb_ref.refs_1_
  12.3 0.0 copy-done
  12.3 0.1 shard_map.90
  12.5 1.1 %collective-permute-start.2 = (f32[88,256]{1,0:T(8,128)S(1)}, f32[88,256]{1,0:T(8,128)S(1)}, u32[]{:S(2)}, u32[]{:S(2)}) collective-permute-start(f32[88,256]{1,0:T(8,128)S(1)} %shard_map.90), channel_id=1, source_target_pairs={{0,1},{1,0},{2,3},{3,2},{4,5},{5,4},{6,7},{7,6},{8,9},{9,8},{10,11... | collective-permute-start | bytes 270344 | tf_op jit(solution)/shard_map/ppermute | solution.py:43
  13.6 2.1 %shard_map.88 = (f32[512,256]{1,0:T(8,128)S(1)}, s32[8,128]{1,0:T(8,128)S(1)}) custom-call(f32[512,256]{1,0:T(8,128)S(1)} %shard_map.87.stay_ref.after_ref, f32[112,256]{1,0:T(8,128)S(1)} %collective-permute-done.recva_ref.refs_0_, f32[112,256]{1,0:T(8,128)S(1)} %collective-permute-done.1.recvb_ref.refs_1_, f32[6,128,128]{2,1,0:T(8,128)S(1)} %get-tuple-element.29.field_ref, ...), custom_call_target="tpu_custom_call" | custom-call | tf_op jit(solution)/shard_map/pallas_call | solution.py:655
  15.7 1.5 %shard_map.89 = (f32[128,128]{1,0:T(8,128)S(1)}, s32[4,128]{1,0:T(4,128)S(1)}, f32[128,128]{1,0:T(8,128)S(1)}, f32[128,128]{1,0:T(8,128)S(1)}) custom-call(f32[6,128,128]{2,1,0:T(8,128)S(1)} %get-tuple-element.29.field_ref, f32[128,128]{1,0:T(8,128)S(1)} %get-tuple-element.30.slot_ref, f32[512,256]{1,0:T(8,128)S(1)} %get-tuple-element.33.after_ref.near_ref), custom_call_target="tpu_custom_call" | custom-call | tf_op jit(solution)/shard_map/pallas_call | solution.py:655
  17.2 0.0 collective-permute-done.2.refs_0_
  17.2 1.1 %shard_map.91 = (f32[8,16,256]{2,1,0:T(8,128)S(1)}, f32[8,8,256]{2,1,0:T(8,128)S(1)}, f32[8,8,256]{2,1,0:T(8,128)S(1)}) custom-call(f32[512,256]{1,0:T(8,128)S(1)} %get-tuple-element.33.after_ref.near_ref, f32[128,128]{1,0:T(8,128)S(1)} %get-tuple-element.34.after_ref.row_ref, f32[88,256]{1,0:T(8,128)S(1)} %collective-permute-done.2.refs_0_), custom_call_target="tpu_custom_call" | custom-call | tf_op jit(solution)/shard_map/pallas_call | solution.py:655
  18.3 0.4 collective-permute-start.3
  18.7 1.2 %collective-permute-start.4 = (f32[8,8,256]{2,1,0:T(8,128)S(1)}, f32[8,8,256]{2,1,0:T(8,128)S(1)}, u32[]{:S(2)}, u32[]{:S(2)}) collective-permute-start(f32[8,8,256]{2,1,0:T(8,128)S(1)} %get-tuple-element.38), channel_id=1, source_target_pairs={{0,1},{1,0},{2,4},{3,5},{4,2},{5,3},{6,8},{7,9},{8,6},{9,7},{10,12... | collective-permute-start | bytes 196616 | tf_op jit(solution)/shard_map/ppermute | solution.py:43
  19.9 1.1 %shard_map.92.after_ref.grid_ref = f32[8,32,256]{2,1,0:T(8,128)S(1)} custom-call(f32[512,256]{1,0:T(8,128)S(1)} %get-tuple-element.33.after_ref.near_ref, f32[8,16,256]{2,1,0:T(8,128)S(1)} %get-tuple-element.36.outer_ref, f32[88,256]{1,0:T(8,128)S(1)} %collective-permute-done.2.refs_0_), custom_call_target="tpu_custom_call" | custom-call | tf_op jit(solution)/shard_map/pallas_call | solution.py:655
  21.0 2.5 %shard_map.94.after_ref.order_ref = f32[2,64,256]{2,1,0:T(8,128)S(1)} custom-call(f32[6,128,128]{2,1,0:T(8,128)S(1)} %get-tuple-element.29.field_ref, f32[128,128]{1,0:T(8,128)S(1)} %get-tuple-element.34.after_ref.row_ref, f32[128,128]{1,0:T(8,128)S(1)} %get-tuple-element.44.lam_ref, f32[8,32,256]{2,1,0:T(8,128)S(1)} %shard_map.92.after_ref.grid_ref), custom_call_target="tpu_custom_call" | custom-call | tf_op jit(solution)/shard_map/pallas_call | solution.py:655
  23.5 0.0 copy-start.1
  23.5 0.0 collective-permute-done.3.froma_ref
  23.5 0.0 collective-permute-done.4.fromb_ref
  23.5 0.1 shard_map.95
  23.7 0.9 %collective-permute-start.5 = (f32[16,256]{1,0:T(8,128)S(1)}, f32[16,256]{1,0:T(8,128)S(1)}, u32[]{:S(2)}, u32[]{:S(2)}) collective-permute-start(f32[16,256]{1,0:T(8,128)S(1)} %shard_map.95), channel_id=1, source_target_pairs={{0,1},{1,0},{2,3},{3,2},{4,5},{5,4},{6,7},{7,6},{8,9},{9,8},{10,11... | collective-permute-start | bytes 49160 | tf_op jit(solution)/shard_map/ppermute | solution.py:43
  24.6 0.0 copy-done.1
  24.6 1.5 %shard_map.93 = (f32[8,48,384]{2,1,0:T(8,128)S(1)}, f32[8,48,384]{2,1,0:T(8,128)S(1)}, f32[8,48,384]{2,1,0:T(8,128)S(1)}, f32[8,48,384]{2,1,0:T(8,128)S(1)}, f32...) custom-call(f32[8,32,256]{2,1,0:T(8,128)S(1)} %copy-done, f32[112,256]{1,0:T(8,128)S(1)} %collective-permute-done.recva_ref.refs_0_, ...), custom_call_target="tpu_custom_call" | custom-call | tf_op jit(solution)/shard_map/pallas_call | solution.py:655
  26.0 1.4 %collective-permute-done.5.refs_0_ = f32[16,256]{1,0:T(8,128)S(1)} collective-permute-done((f32[16,256]{1,0:T(8,128)S(1)}, f32[16,256]{1,0:T(8,128)S(1)}, u32[]{:S(2)}, u32[]{:S(2)}) %collective-permute-start.5) | collective-permute-done | bytes 16416 | tf_op jit(solution)/shard_map/ppermute | solution.py:43
  27.5 3.0 %shard_map.96 = (f32[8,32,256]{2,1,0:T(8,128)S(1)}, bf16[1024,256]{1,0:T(8,128)(2,1)S(1)}) custom-call(f32[8,32,256]{2,1,0:T(8,128)S(1)} %shard_map.92.after_ref.grid_ref, f32[8,8,256]{2,1,0:T(8,128)S(1)} %collective-permute-done.3.froma_ref, f32[8,8,256]{2,1,0:T(8,128)S(1)} %collective-permute-done.4.fromb_ref, f32[8,48,384]{2,1,0:T(8,128)S(1)} %get-tuple-element.39.cn_ref, ...), custom_call_target="tpu_custom_call" | custom-call | tf_op jit(solution)/shard_map/pallas_call | solution.py:655
  30.4 1.7 %shard_map.100 = f32[48,256]{1,0:T(8,128)S(1)} custom-call(bf16[1024,256]{1,0:T(8,128)(2,1)S(1)} %get-tuple-element.45.slope_ref, s32[8,128]{1,0:T(8,128)S(1)} %get-tuple-element.50.unit_ref, f32[88,256]{1,0:T(8,128)S(1)} %collective-permute-done.2.refs_0_), custom_call_target="tpu_custom_call" | custom-call | tf_op jit(solution)/shard_map/pallas_call | solution.py:655
  32.1 0.9 %collective-permute-start.6 = (f32[48,256]{1,0:T(8,128)S(1)}, f32[48,256]{1,0:T(8,128)S(1)}, u32[]{:S(2)}, u32[]{:S(2)}) collective-permute-start(f32[48,256]{1,0:T(8,128)S(1)} %shard_map.100), channel_id=1, source_target_pairs={{0,1},{1,0},{2,3},{3,2},{4,5},{5,4},{6,7},{7,6},{8,9},{9,8},{10,11... | collective-permute-start | bytes 147464 | tf_op jit(solution)/shard_map/ppermute | solution.py:43
  33.0 1.2 %shard_map.99.after_ref.refs_1_ = f32[1,48,256]{2,1,0:T(8,128)S(1)} custom-call(bf16[1024,256]{1,0:T(8,128)(2,1)S(1)} %get-tuple-element.45.slope_ref, f32[2,64,256]{2,1,0:T(8,128)S(1)} %shard_map.94.after_ref.order_ref, s32[4,128]{1,0:T(4,128)S(1)} %get-tuple-element.46.unit_ref), custom_call_target="tpu_custom_call" | custom-call | tf_op jit(solution)/shard_map/pallas_call | solution.py:655
  34.2 1.4 %shard_map.98.near_ref = f32[32,256]{1,0:T(8,128)S(1)} custom-call(bf16[1024,256]{1,0:T(8,128)(2,1)S(1)} %get-tuple-element.45.slope_ref, s32[8,128]{1,0:T(8,128)S(1)} %get-tuple-element.49.unit_ref, f32[112,256]{1,0:T(8,128)S(1)} %collective-permute-done.recva_ref.refs_0_, f32[112,256]{1,0:T(8,128)S(1)} %collective-permute-done.1.recvb_ref.refs_1_), custom_call_target="tpu_custom_call" | custom-call | tf_op jit(solution)/shard_map/pallas_call | solution.py:655
  35.5 0.7 %collective-permute-done.6.refs_0_ = f32[48,256]{1,0:T(8,128)S(1)} collective-permute-done((f32[48,256]{1,0:T(8,128)S(1)}, f32[48,256]{1,0:T(8,128)S(1)}, u32[]{:S(2)}, u32[]{:S(2)}) %collective-permute-start.6) | collective-permute-done | bytes 49184 | tf_op jit(solution)/shard_map/ppermute | solution.py:43
  36.3 0.0 collective-permute-start.7
  36.3 0.9 %collective-permute-start.8 = (f32[32,256]{1,0:T(8,128)S(1)}, f32[32,256]{1,0:T(8,128)S(1)}, u32[]{:S(2)}, u32[]{:S(2)}) collective-permute-start(f32[32,256]{1,0:T(8,128)S(1)} %get-tuple-element.52), channel_id=1, source_target_pairs={{0,1},{1,0},{2,4},{3,5},{4,2},{5,3},{6,8},{7,9},{8,6},{9,7},{10,12... | collective-permute-start | bytes 98312 | tf_op jit(solution)/shard_map/ppermute | solution.py:43
  37.2 2.4 %shard_map.97 = (f32[3,48,256]{2,1,0:T(8,128)S(1)}, f32[8,32,256]{2,1,0:T(8,128)}) custom-call(bf16[1024,256]{1,0:T(8,128)(2,1)S(1)} %get-tuple-element.45.slope_ref, f32[2,64,256]{2,1,0:T(8,128)S(1)} %shard_map.94.after_ref.order_ref, s32[4,128]{1,0:T(4,128)S(1)} %get-tuple-element.46.unit_ref, f32[8,32,256]{2,1,0:T(8,128)S(1)} %get-tuple-element.47.value_ref), custom_call_target="tpu_custom_call" | custom-call | tf_op jit(solution)/shard_map/pallas_call | solution.py:655
  39.6 0.0 collective-permute-done.7.backa_ref
  39.6 0.7 %collective-permute-done.8.backb_ref = f32[32,256]{1,0:T(8,128)S(1)} collective-permute-done((f32[32,256]{1,0:T(8,128)S(1)}, f32[32,256]{1,0:T(8,128)S(1)}, u32[]{:S(2)}, u32[]{:S(2)}) %collective-permute-start.8) | collective-permute-done | bytes 32800 | tf_op jit(solution)/shard_map/ppermute | solution.py:43
  40.3 3.6 %shard_map.102 = f32[2,16384]{1,0:T(2,128)} custom-call(f32[32,256]{1,0:T(8,128)S(1)} %collective-permute-done.7.backa_ref, f32[32,256]{1,0:T(8,128)S(1)} %collective-permute-done.8.backb_ref, f32[48,256]{1,0:T(8,128)S(1)} %collective-permute-done.6.refs_0_, f32[1,48,256]{2,1,0:T(8,128)S(1)} %shard_map.99.after_ref.refs_1_, ...), custom_call_target="tpu_custom_call" | custom-call | tf_op jit(solution)/shard_map/pallas_call | solution.py:655
  (1 shorter events, 0.0 us)
Async XLA Ops:
  5.5 6.8 %collective-permute-start = (f32[112,256]{1,0:T(8,128)S(1)}, f32[112,256]{1,0:T(8,128)S(1)}, u32[]{:S(2)}, u32[]{:S(2)}) collective-permute-start(f32[112,256]{1,0:T(8,128)S(1)} %get-tuple-element.31), channel_id=1, source_target_pairs={{0,2},{1,3},{2,0},{3,1},{4,6},{5,7},{6,4},{7,5},{8,10},{9,11},{10,... | collective-permute-start | bytes 344072 | tf_op jit(solution)/shard_map/ppermute | solution.py:43
  6.0 6.3 %collective-permute-start.1 = (f32[112,256]{1,0:T(8,128)S(1)}, f32[112,256]{1,0:T(8,128)S(1)}, u32[]{:S(2)}, u32[]{:S(2)}) collective-permute-start(f32[112,256]{1,0:T(8,128)S(1)} %get-tuple-element.32), channel_id=1, source_target_pairs={{0,1},{1,0},{2,4},{3,5},{4,2},{5,3},{6,8},{7,9},{8,6},{9,7},{10,12... | collective-permute-start | bytes 344072 | tf_op jit(solution)/shard_map/ppermute | solution.py:43
  8.6 3.7 %copy-start = (f32[8,32,256]{2,1,0:T(8,128)S(1)}, f32[8,32,256]{2,1,0:T(8,128)}, u32[]{:S(2)}) copy-start(f32[8,32,256]{2,1,0:T(8,128)} %cond_ref.3) | copy-start | bytes 786436
  12.5 4.8 %collective-permute-start.2 = (f32[88,256]{1,0:T(8,128)S(1)}, f32[88,256]{1,0:T(8,128)S(1)}, u32[]{:S(2)}, u32[]{:S(2)}) collective-permute-start(f32[88,256]{1,0:T(8,128)S(1)} %shard_map.90), channel_id=1, source_target_pairs={{0,1},{1,0},{2,3},{3,2},{4,5},{5,4},{6,7},{7,6},{8,9},{9,8},{10,11... | collective-permute-start | bytes 270344 | tf_op jit(solution)/shard_map/ppermute | solution.py:43
  18.3 5.2 %collective-permute-start.3 = (f32[8,8,256]{2,1,0:T(8,128)S(1)}, f32[8,8,256]{2,1,0:T(8,128)S(1)}, u32[]{:S(2)}, u32[]{:S(2)}) collective-permute-start(f32[8,8,256]{2,1,0:T(8,128)S(1)} %get-tuple-element.37), channel_id=1, source_target_pairs={{0,2},{1,3},{2,0},{3,1},{4,6},{5,7},{6,4},{7,5},{8,10},{9,11},{10,... | collective-permute-start | bytes 196616 | tf_op jit(solution)/shard_map/ppermute | solution.py:43
  18.7 4.8 %collective-permute-start.4 = (f32[8,8,256]{2,1,0:T(8,128)S(1)}, f32[8,8,256]{2,1,0:T(8,128)S(1)}, u32[]{:S(2)}, u32[]{:S(2)}) collective-permute-start(f32[8,8,256]{2,1,0:T(8,128)S(1)} %get-tuple-element.38), channel_id=1, source_target_pairs={{0,1},{1,0},{2,4},{3,5},{4,2},{5,3},{6,8},{7,9},{8,6},{9,7},{10,12... | collective-permute-start | bytes 196616 | tf_op jit(solution)/shard_map/ppermute | solution.py:43
  23.5 1.1 %copy-start.1 = (f32[7]{0:T(128)S(1)}, f32[7]{0:T(128)}, u32[]{:S(2)}) copy-start(f32[7]{0:T(128)} %coupling_ref.1) | copy-start | bytes 88
  23.7 3.8 %collective-permute-start.5 = (f32[16,256]{1,0:T(8,128)S(1)}, f32[16,256]{1,0:T(8,128)S(1)}, u32[]{:S(2)}, u32[]{:S(2)}) collective-permute-start(f32[16,256]{1,0:T(8,128)S(1)} %shard_map.95), channel_id=1, source_target_pairs={{0,1},{1,0},{2,3},{3,2},{4,5},{5,4},{6,7},{7,6},{8,9},{9,8},{10,11... | collective-permute-start | bytes 49160 | tf_op jit(solution)/shard_map/ppermute | solution.py:43
  32.1 4.2 %collective-permute-start.6 = (f32[48,256]{1,0:T(8,128)S(1)}, f32[48,256]{1,0:T(8,128)S(1)}, u32[]{:S(2)}, u32[]{:S(2)}) collective-permute-start(f32[48,256]{1,0:T(8,128)S(1)} %shard_map.100), channel_id=1, source_target_pairs={{0,1},{1,0},{2,3},{3,2},{4,5},{5,4},{6,7},{7,6},{8,9},{9,8},{10,11... | collective-permute-start | bytes 147464 | tf_op jit(solution)/shard_map/ppermute | solution.py:43
  36.3 3.3 %collective-permute-start.7 = (f32[32,256]{1,0:T(8,128)S(1)}, f32[32,256]{1,0:T(8,128)S(1)}, u32[]{:S(2)}, u32[]{:S(2)}) collective-permute-start(f32[32,256]{1,0:T(8,128)S(1)} %get-tuple-element.51), channel_id=1, source_target_pairs={{0,2},{1,3},{2,0},{3,1},{4,6},{5,7},{6,4},{7,5},{8,10},{9,11},{10,... | collective-permute-start | bytes 98312 | tf_op jit(solution)/shard_map/ppermute | solution.py:43
  36.3 4.0 %collective-permute-start.8 = (f32[32,256]{1,0:T(8,128)S(1)}, f32[32,256]{1,0:T(8,128)S(1)}, u32[]{:S(2)}, u32[]{:S(2)}) collective-permute-start(f32[32,256]{1,0:T(8,128)S(1)} %get-tuple-element.52), channel_id=1, source_target_pairs={{0,1},{1,0},{2,4},{3,5},{4,2},{5,3},{6,8},{7,9},{8,6},{9,7},{10,12... | collective-permute-start | bytes 98312 | tf_op jit(solution)/shard_map/ppermute | solution.py:43

commit v11 on v9

--- a/solution.py
+++ b/solution.py
@@ -788,7 +788,7 @@
         slope, near_unit, recv_a, recv_b,
         spaces={1: pltpu.SMEM},
     )
-    blocks, early = square[0] // BLOCK, 1
+    blocks, early = square[0] // BLOCK, 2
     units = order.shape[1] // blocks + layers
     (early_value,) = call(
         partial(stay_gather_kernel, layers, 0),

time: 43.8 us -> 44.1 us (level)
  waiting for transfers between devices: 1.91 us -> 2.37 us
    ppermute x9, waiting for transfers between devices: 1.91 us -> 2.37 us  [exchange(): return lax.ppermute(value, ('gx', 'gy'), pairs)]
  transfers between devices with their start and end apart: 9 -> 9, of which waited for: 3 -> 2; matrix products, arithmetic and copies ran while one was open for 0% -> 0% of each run, Pallas kernels for 40% -> 39%
where the time goes in v11:
time: 44.1 us; the launch traced here: 44 us
  Pallas kernels  31.8 us (72%)
  starting transfers between devices  8.92 us (20%)
  waiting for transfers between devices  2.37 us (5%)
  between operations  0.82 us (2%)
    pallas_call x17, Pallas kernels, call(): pl.pallas_call(kernel, out_shape=shapes, in_specs=specs, out_specs=[pl.Bl...  31.8 us
    ppermute x9, starting transfers between devices, exchange(): return lax.ppermute(value, ('gx', 'gy'), pairs)  8.92 us
    ppermute x9, waiting for transfers between devices, exchange(): return lax.ppermute(value, ('gx', 'gy'), pairs)  2.37 us
  transfers between devices with their start and end apart: 9, of which 2 were waited for; matrix products, arithmetic and copies ran while one was open for 0% of the time, Pallas kernels for 39%

profile of v11, /device:TPU:0, one launch (start us, length us, event | category | flops | bytes accessed | tf_op | source)
XLA Modules:
  0.0 44.0 jit_solution(10810708893413348519)
XLA Ops:
  0.6 4.9 %shard_map.86 = (f32[112,256]{1,0:T(8,128)S(1)}, f32[112,256]{1,0:T(8,128)S(1)}, f32[24,256]{1,0:T(8,128)S(1)}, f32[128,128]{1,0:T(8,128)S(1)}, f32[6,128,128]{2,1,0:T(8,128)S(1)}, /*index=5*/f32[128,128]{1,0:T(8,128)S(1)}) custom-call(s32[128,128]{1,0:T(8,128)} %bitcast.5, s32[128,128]{1,0:T(8,128)} %bitcast.6, s32[128,128]{1,0:T(8,128)} %bitcast.7, ...), custom_call_target="tpu_custom_call" | custom-call | tf_op jit(solution)/shard_map/pallas_call | solution.py:655
  5.5 0.5 %collective-permute-start = (f32[112,256]{1,0:T(8,128)S(1)}, f32[112,256]{1,0:T(8,128)S(1)}, u32[]{:S(2)}, u32[]{:S(2)}) collective-permute-start(f32[112,256]{1,0:T(8,128)S(1)} %get-tuple-element.31), channel_id=1, source_target_pairs={{0,2},{1,3},{2,0},{3,1},{4,6},{5,7},{6,4},{7,5},{8,10},{9,11},{10,... | collective-permute-start | bytes 344072 | tf_op jit(solution)/shard_map/ppermute | solution.py:43
  6.0 2.6 %collective-permute-start.1 = (f32[112,256]{1,0:T(8,128)S(1)}, f32[112,256]{1,0:T(8,128)S(1)}, u32[]{:S(2)}, u32[]{:S(2)}) collective-permute-start(f32[112,256]{1,0:T(8,128)S(1)} %get-tuple-element.32), channel_id=1, source_target_pairs={{0,1},{1,0},{2,4},{3,5},{4,2},{5,3},{6,8},{7,9},{8,6},{9,7},{10,12... | collective-permute-start | bytes 344072 | tf_op jit(solution)/shard_map/ppermute | solution.py:43
  8.6 0.0 copy-start
  8.6 3.4 %shard_map.87.stay_ref.after_ref = f32[512,256]{1,0:T(8,128)S(1)} custom-call(f32[6,128,128]{2,1,0:T(8,128)S(1)} %get-tuple-element.29.field_ref, f32[128,128]{1,0:T(8,128)S(1)} %get-tuple-element.30.slot_ref), custom_call_target="tpu_custom_call" | custom-call | tf_op jit(solution)/shard_map/pallas_call | solution.py:655
  12.0 0.0 collective-permute-done.recva_ref.refs_0_
  12.1 0.0 collective-permute-done.1.recvb_ref.refs_1_
  12.1 0.0 copy-done
  12.1 0.1 shard_map.90
  12.2 1.4 %collective-permute-start.2 = (f32[88,256]{1,0:T(8,128)S(1)}, f32[88,256]{1,0:T(8,128)S(1)}, u32[]{:S(2)}, u32[]{:S(2)}) collective-permute-start(f32[88,256]{1,0:T(8,128)S(1)} %shard_map.90), channel_id=1, source_target_pairs={{0,1},{1,0},{2,3},{3,2},{4,5},{5,4},{6,7},{7,6},{8,9},{9,8},{10,11... | collective-permute-start | bytes 270344 | tf_op jit(solution)/shard_map/ppermute | solution.py:43
  13.6 2.4 %shard_map.88 = (f32[512,256]{1,0:T(8,128)S(1)}, s32[8,128]{1,0:T(8,128)S(1)}) custom-call(f32[512,256]{1,0:T(8,128)S(1)} %shard_map.87.stay_ref.after_ref, f32[112,256]{1,0:T(8,128)S(1)} %collective-permute-done.recva_ref.refs_0_, f32[112,256]{1,0:T(8,128)S(1)} %collective-permute-done.1.recvb_ref.refs_1_, f32[6,128,128]{2,1,0:T(8,128)S(1)} %get-tuple-element.29.field_ref, ...), custom_call_target="tpu_custom_call" | custom-call | tf_op jit(solution)/shard_map/pallas_call | solution.py:655
  16.0 1.5 %shard_map.89 = (f32[128,128]{1,0:T(8,128)S(1)}, s32[4,128]{1,0:T(4,128)S(1)}, f32[128,128]{1,0:T(8,128)S(1)}, f32[128,128]{1,0:T(8,128)S(1)}) custom-call(f32[6,128,128]{2,1,0:T(8,128)S(1)} %get-tuple-element.29.field_ref, f32[128,128]{1,0:T(8,128)S(1)} %get-tuple-element.30.slot_ref, f32[512,256]{1,0:T(8,128)S(1)} %get-tuple-element.33.after_ref.near_ref), custom_call_target="tpu_custom_call" | custom-call | tf_op jit(solution)/shard_map/pallas_call | solution.py:655
  17.5 0.0 collective-permute-done.2.refs_0_
  17.5 1.1 %shard_map.91 = (f32[8,16,256]{2,1,0:T(8,128)S(1)}, f32[8,8,256]{2,1,0:T(8,128)S(1)}, f32[8,8,256]{2,1,0:T(8,128)S(1)}) custom-call(f32[512,256]{1,0:T(8,128)S(1)} %get-tuple-element.33.after_ref.near_ref, f32[128,128]{1,0:T(8,128)S(1)} %get-tuple-element.34.after_ref.row_ref, f32[88,256]{1,0:T(8,128)S(1)} %collective-permute-done.2.refs_0_), custom_call_target="tpu_custom_call" | custom-call | tf_op jit(solution)/shard_map/pallas_call | solution.py:655
  18.6 0.1 collective-permute-start.3
  18.7 0.9 %collective-permute-start.4 = (f32[8,8,256]{2,1,0:T(8,128)S(1)}, f32[8,8,256]{2,1,0:T(8,128)S(1)}, u32[]{:S(2)}, u32[]{:S(2)}) collective-permute-start(f32[8,8,256]{2,1,0:T(8,128)S(1)} %get-tuple-element.38), channel_id=1, source_target_pairs={{0,1},{1,0},{2,4},{3,5},{4,2},{5,3},{6,8},{7,9},{8,6},{9,7},{10,12... | collective-permute-start | bytes 196616 | tf_op jit(solution)/shard_map/ppermute | solution.py:43
  19.6 1.1 %shard_map.92.after_ref.grid_ref = f32[8,32,256]{2,1,0:T(8,128)S(1)} custom-call(f32[512,256]{1,0:T(8,128)S(1)} %get-tuple-element.33.after_ref.near_ref, f32[8,16,256]{2,1,0:T(8,128)S(1)} %get-tuple-element.36.outer_ref, f32[88,256]{1,0:T(8,128)S(1)} %collective-permute-done.2.refs_0_), custom_call_target="tpu_custom_call" | custom-call | tf_op jit(solution)/shard_map/pallas_call | solution.py:655
  20.7 2.5 %shard_map.94.after_ref.order_ref = f32[2,64,256]{2,1,0:T(8,128)S(1)} custom-call(f32[6,128,128]{2,1,0:T(8,128)S(1)} %get-tuple-element.29.field_ref, f32[128,128]{1,0:T(8,128)S(1)} %get-tuple-element.34.after_ref.row_ref, f32[128,128]{1,0:T(8,128)S(1)} %get-tuple-element.44.lam_ref, f32[8,32,256]{2,1,0:T(8,128)S(1)} %shard_map.92.after_ref.grid_ref), custom_call_target="tpu_custom_call" | custom-call | tf_op jit(solution)/shard_map/pallas_call | solution.py:655
  23.2 0.0 copy-start.1
  23.2 0.0 collective-permute-done.3.froma_ref
  23.3 0.0 collective-permute-done.4.fromb_ref
  23.3 0.1 shard_map.95
  23.4 1.2 %collective-permute-start.5 = (f32[16,256]{1,0:T(8,128)S(1)}, f32[16,256]{1,0:T(8,128)S(1)}, u32[]{:S(2)}, u32[]{:S(2)}) collective-permute-start(f32[16,256]{1,0:T(8,128)S(1)} %shard_map.95), channel_id=1, source_target_pairs={{0,1},{1,0},{2,3},{3,2},{4,5},{5,4},{6,7},{7,6},{8,9},{9,8},{10,11... | collective-permute-start | bytes 49160 | tf_op jit(solution)/shard_map/ppermute | solution.py:43
  24.6 0.0 copy-done.1
  24.6 1.5 %shard_map.93 = (f32[8,48,384]{2,1,0:T(8,128)S(1)}, f32[8,48,384]{2,1,0:T(8,128)S(1)}, f32[8,48,384]{2,1,0:T(8,128)S(1)}, f32[8,48,384]{2,1,0:T(8,128)S(1)}, f32...) custom-call(f32[8,32,256]{2,1,0:T(8,128)S(1)} %copy-done, f32[112,256]{1,0:T(8,128)S(1)} %collective-permute-done.recva_ref.refs_0_, ...), custom_call_target="tpu_custom_call" | custom-call | tf_op jit(solution)/shard_map/pallas_call | solution.py:655
  26.1 1.1 %collective-permute-done.5.refs_0_ = f32[16,256]{1,0:T(8,128)S(1)} collective-permute-done((f32[16,256]{1,0:T(8,128)S(1)}, f32[16,256]{1,0:T(8,128)S(1)}, u32[]{:S(2)}, u32[]{:S(2)}) %collective-permute-start.5) | collective-permute-done | bytes 16416 | tf_op jit(solution)/shard_map/ppermute | solution.py:43
  27.2 3.0 %shard_map.96 = (f32[8,32,256]{2,1,0:T(8,128)S(1)}, bf16[1024,256]{1,0:T(8,128)(2,1)S(1)}) custom-call(f32[8,32,256]{2,1,0:T(8,128)S(1)} %shard_map.92.after_ref.grid_ref, f32[8,8,256]{2,1,0:T(8,128)S(1)} %collective-permute-done.3.froma_ref, f32[8,8,256]{2,1,0:T(8,128)S(1)} %collective-permute-done.4.fromb_ref, f32[8,48,384]{2,1,0:T(8,128)S(1)} %get-tuple-element.39.cn_ref, ...), custom_call_target="tpu_custom_call" | custom-call | tf_op jit(solution)/shard_map/pallas_call | solution.py:655
  30.2 1.7 %shard_map.100 = f32[48,256]{1,0:T(8,128)S(1)} custom-call(bf16[1024,256]{1,0:T(8,128)(2,1)S(1)} %get-tuple-element.45.slope_ref, s32[8,128]{1,0:T(8,128)S(1)} %get-tuple-element.50.unit_ref, f32[88,256]{1,0:T(8,128)S(1)} %collective-permute-done.2.refs_0_), custom_call_target="tpu_custom_call" | custom-call | tf_op jit(solution)/shard_map/pallas_call | solution.py:655
  31.9 1.2 %collective-permute-start.6 = (f32[48,256]{1,0:T(8,128)S(1)}, f32[48,256]{1,0:T(8,128)S(1)}, u32[]{:S(2)}, u32[]{:S(2)}) collective-permute-start(f32[48,256]{1,0:T(8,128)S(1)} %shard_map.100), channel_id=1, source_target_pairs={{0,1},{1,0},{2,3},{3,2},{4,5},{5,4},{6,7},{7,6},{8,9},{9,8},{10,11... | collective-permute-start | bytes 147464 | tf_op jit(solution)/shard_map/ppermute | solution.py:43
  33.1 1.8 %shard_map.99.after_ref.refs_1_ = f32[2,48,256]{2,1,0:T(8,128)S(1)} custom-call(bf16[1024,256]{1,0:T(8,128)(2,1)S(1)} %get-tuple-element.45.slope_ref, f32[2,64,256]{2,1,0:T(8,128)S(1)} %shard_map.94.after_ref.order_ref, s32[4,128]{1,0:T(4,128)S(1)} %get-tuple-element.46.unit_ref), custom_call_target="tpu_custom_call" | custom-call | tf_op jit(solution)/shard_map/pallas_call | solution.py:655
  34.9 1.4 %shard_map.98.near_ref = f32[32,256]{1,0:T(8,128)S(1)} custom-call(bf16[1024,256]{1,0:T(8,128)(2,1)S(1)} %get-tuple-element.45.slope_ref, s32[8,128]{1,0:T(8,128)S(1)} %get-tuple-element.49.unit_ref, f32[112,256]{1,0:T(8,128)S(1)} %collective-permute-done.recva_ref.refs_0_, f32[112,256]{1,0:T(8,128)S(1)} %collective-permute-done.1.recvb_ref.refs_1_), custom_call_target="tpu_custom_call" | custom-call | tf_op jit(solution)/shard_map/pallas_call | solution.py:655
  36.2 0.0 collective-permute-done.6.refs_0_
  36.2 0.1 collective-permute-start.7
  36.3 0.9 %collective-permute-start.8 = (f32[32,256]{1,0:T(8,128)S(1)}, f32[32,256]{1,0:T(8,128)S(1)}, u32[]{:S(2)}, u32[]{:S(2)}) collective-permute-start(f32[32,256]{1,0:T(8,128)S(1)} %get-tuple-element.52), channel_id=1, source_target_pairs={{0,1},{1,0},{2,4},{3,5},{4,2},{5,3},{6,8},{7,9},{8,6},{9,7},{10,12... | collective-permute-start | bytes 98312 | tf_op jit(solution)/shard_map/ppermute | solution.py:43
  37.3 1.8 %shard_map.97 = (f32[2,48,256]{2,1,0:T(8,128)S(1)}, f32[8,32,256]{2,1,0:T(8,128)}) custom-call(bf16[1024,256]{1,0:T(8,128)(2,1)S(1)} %get-tuple-element.45.slope_ref, f32[2,64,256]{2,1,0:T(8,128)S(1)} %shard_map.94.after_ref.order_ref, s32[4,128]{1,0:T(4,128)S(1)} %get-tuple-element.46.unit_ref, f32[8,32,256]{2,1,0:T(8,128)S(1)} %get-tuple-element.47.value_ref), custom_call_target="tpu_custom_call" | custom-call | tf_op jit(solution)/shard_map/pallas_call | solution.py:655
  39.1 0.0 collective-permute-done.7.backa_ref
  39.1 1.2 %collective-permute-done.8.backb_ref = f32[32,256]{1,0:T(8,128)S(1)} collective-permute-done((f32[32,256]{1,0:T(8,128)S(1)}, f32[32,256]{1,0:T(8,128)S(1)}, u32[]{:S(2)}, u32[]{:S(2)}) %collective-permute-start.8) | collective-permute-done | bytes 32800 | tf_op jit(solution)/shard_map/ppermute | solution.py:43
  40.3 3.7 %shard_map.102 = f32[2,16384]{1,0:T(2,128)} custom-call(f32[32,256]{1,0:T(8,128)S(1)} %collective-permute-done.7.backa_ref, f32[32,256]{1,0:T(8,128)S(1)} %collective-permute-done.8.backb_ref, f32[48,256]{1,0:T(8,128)S(1)} %collective-permute-done.6.refs_0_, f32[2,48,256]{2,1,0:T(8,128)S(1)} %shard_map.99.after_ref.refs_1_, ...), custom_call_target="tpu_custom_call" | custom-call | tf_op jit(solution)/shard_map/pallas_call | solution.py:655
  (1 shorter events, 0.0 us)
Async XLA Ops:
  5.5 6.5 %collective-permute-start = (f32[112,256]{1,0:T(8,128)S(1)}, f32[112,256]{1,0:T(8,128)S(1)}, u32[]{:S(2)}, u32[]{:S(2)}) collective-permute-start(f32[112,256]{1,0:T(8,128)S(1)} %get-tuple-element.31), channel_id=1, source_target_pairs={{0,2},{1,3},{2,0},{3,1},{4,6},{5,7},{6,4},{7,5},{8,10},{9,11},{10,... | collective-permute-start | bytes 344072 | tf_op jit(solution)/shard_map/ppermute | solution.py:43
  6.0 6.0 %collective-permute-start.1 = (f32[112,256]{1,0:T(8,128)S(1)}, f32[112,256]{1,0:T(8,128)S(1)}, u32[]{:S(2)}, u32[]{:S(2)}) collective-permute-start(f32[112,256]{1,0:T(8,128)S(1)} %get-tuple-element.32), channel_id=1, source_target_pairs={{0,1},{1,0},{2,4},{3,5},{4,2},{5,3},{6,8},{7,9},{8,6},{9,7},{10,12... | collective-permute-start | bytes 344072 | tf_op jit(solution)/shard_map/ppermute | solution.py:43
  8.6 3.5 %copy-start = (f32[8,32,256]{2,1,0:T(8,128)S(1)}, f32[8,32,256]{2,1,0:T(8,128)}, u32[]{:S(2)}) copy-start(f32[8,32,256]{2,1,0:T(8,128)} %cond_ref.3) | copy-start | bytes 786436
  12.2 5.3 %collective-permute-start.2 = (f32[88,256]{1,0:T(8,128)S(1)}, f32[88,256]{1,0:T(8,128)S(1)}, u32[]{:S(2)}, u32[]{:S(2)}) collective-permute-start(f32[88,256]{1,0:T(8,128)S(1)} %shard_map.90), channel_id=1, source_target_pairs={{0,1},{1,0},{2,3},{3,2},{4,5},{5,4},{6,7},{7,6},{8,9},{9,8},{10,11... | collective-permute-start | bytes 270344 | tf_op jit(solution)/shard_map/ppermute | solution.py:43
  18.6 4.6 %collective-permute-start.3 = (f32[8,8,256]{2,1,0:T(8,128)S(1)}, f32[8,8,256]{2,1,0:T(8,128)S(1)}, u32[]{:S(2)}, u32[]{:S(2)}) collective-permute-start(f32[8,8,256]{2,1,0:T(8,128)S(1)} %get-tuple-element.37), channel_id=1, source_target_pairs={{0,2},{1,3},{2,0},{3,1},{4,6},{5,7},{6,4},{7,5},{8,10},{9,11},{10,... | collective-permute-start | bytes 196616 | tf_op jit(solution)/shard_map/ppermute | solution.py:43
  18.7 4.6 %collective-permute-start.4 = (f32[8,8,256]{2,1,0:T(8,128)S(1)}, f32[8,8,256]{2,1,0:T(8,128)S(1)}, u32[]{:S(2)}, u32[]{:S(2)}) collective-permute-start(f32[8,8,256]{2,1,0:T(8,128)S(1)} %get-tuple-element.38), channel_id=1, source_target_pairs={{0,1},{1,0},{2,4},{3,5},{4,2},{5,3},{6,8},{7,9},{8,6},{9,7},{10,12... | collective-permute-start | bytes 196616 | tf_op jit(solution)/shard_map/ppermute | solution.py:43
  23.2 1.4 %copy-start.1 = (f32[7]{0:T(128)S(1)}, f32[7]{0:T(128)}, u32[]{:S(2)}) copy-start(f32[7]{0:T(128)} %coupling_ref.1) | copy-start | bytes 88
  23.4 3.8 %collective-permute-start.5 = (f32[16,256]{1,0:T(8,128)S(1)}, f32[16,256]{1,0:T(8,128)S(1)}, u32[]{:S(2)}, u32[]{:S(2)}) collective-permute-start(f32[16,256]{1,0:T(8,128)S(1)} %shard_map.95), channel_id=1, source_target_pairs={{0,1},{1,0},{2,3},{3,2},{4,5},{5,4},{6,7},{7,6},{8,9},{9,8},{10,11... | collective-permute-start | bytes 49160 | tf_op jit(solution)/shard_map/ppermute | solution.py:43
  31.9 4.4 %collective-permute-start.6 = (f32[48,256]{1,0:T(8,128)S(1)}, f32[48,256]{1,0:T(8,128)S(1)}, u32[]{:S(2)}, u32[]{:S(2)}) collective-permute-start(f32[48,256]{1,0:T(8,128)S(1)} %shard_map.100), channel_id=1, source_target_pairs={{0,1},{1,0},{2,3},{3,2},{4,5},{5,4},{6,7},{7,6},{8,9},{9,8},{10,11... | collective-permute-start | bytes 147464 | tf_op jit(solution)/shard_map/ppermute | solution.py:43
  36.2 2.8 %collective-permute-start.7 = (f32[32,256]{1,0:T(8,128)S(1)}, f32[32,256]{1,0:T(8,128)S(1)}, u32[]{:S(2)}, u32[]{:S(2)}) collective-permute-start(f32[32,256]{1,0:T(8,128)S(1)} %get-tuple-element.51), channel_id=1, source_target_pairs={{0,2},{1,3},{2,0},{3,1},{4,6},{5,7},{6,4},{7,5},{8,10},{9,11},{10,... | collective-permute-start | bytes 98312 | tf_op jit(solution)/shard_map/ppermute | solution.py:43
  36.3 4.0 %collective-permute-start.8 = (f32[32,256]{1,0:T(8,128)S(1)}, f32[32,256]{1,0:T(8,128)S(1)}, u32[]{:S(2)}, u32[]{:S(2)}) collective-permute-start(f32[32,256]{1,0:T(8,128)S(1)} %get-tuple-element.52), channel_id=1, source_target_pairs={{0,1},{1,0},{2,4},{3,5},{4,2},{5,3},{6,8},{7,9},{8,6},{9,7},{10,12... | collective-permute-start | bytes 98312 | tf_op jit(solution)/shard_map/ppermute | solution.py:43
